TPU v7x, 512 devices: a whole 4x4x16 slice. The times are simulated.
512 devices in a mesh: rep: 8 (over y, core), exp: 64 (over x, z).
Axes of the slice: x: 4, y: 4, z: 16, core: 2. Of those that a mesh axis runs over, the one named last changes fastest.
Arguments:
- tokens: bfloat16 [65536, 3584], P(('rep', 'exp')), may hold values from -6 to 6
- cotangent: bfloat16 [65536, 3584], P(('rep', 'exp')), may hold values from -0.29882812 to 0.29882812
- gates: float32 [65536, 1], P(('rep', 'exp')), may hold values from 0.2 to 1.5
- routes: int32 [65536, 1], P(('rep', 'exp')), may hold values from 0 to 15; in each aligned block of 128 rows (0 to 127, 128 to 255, ...) at most 9 rows name the same one
- w_up: bfloat16 [57344, 1024], P(('exp', 'rep')), may hold values from -0.09375 to 0.09375
- w_down_t: bfloat16 [57344, 1024], P(('exp', 'rep')), may hold values from -0.1875 to 0.1875
Outputs:
- grad_tokens: bfloat16 [65536, 3584], P(('rep', 'exp'))
- grad_gates: float32 [65536, 1], P(('rep', 'exp'))
- grad_up: float32 [57344, 1024], P(('exp', 'rep'))
- grad_down_t: float32 [57344, 1024], P(('exp', 'rep'))
Inputs may be any that keep to these rules, and one draw needn't show every extreme that they name: `routes`: each row names one expert (1 = 1). Among the rows of one device no expert is named more than 9 times, and in every draw some expert is named exactly 9 times by the rows of some device.
All inputs are finite; a program needn't handle non-finite values.
Results may differ from a plain program's by a relative error of at most 0.012.
Values may be sent and summed in bfloat16 or wider, within the bound.
No kernel may reach another device: no remote copies, remote signals or barrier semaphores. Data moves between devices by JAX's collectives and lax.ppermute only.
A program may use at most 64 MiB of HBM per device.

v0:
```python
import jax
import jax.numpy as jnp
from jax import lax
from jax.sharding import PartitionSpec as P

SLICES = 4


def swapped(x, axis, distance):
    return lax.ppermute(x, axis, [(i, i ^ 1 << distance) for i in range(lax.axis_size(axis))])


def contract_last(left_side, right_side):
    return lax.dot_general(
        left_side, right_side, (((1,), (1,)), ((), ())), preferred_element_type=jnp.float32
    )


def contract_first(left_side, right_side):
    return lax.dot_general(
        left_side, right_side, (((0,), (0,)), ((), ())), preferred_element_type=jnp.float32
    )


def shards(tokens, cotangent, gates, routes, w_up, w_down_t):
    tok_dev, top_count = routes.shape
    model_width = tokens.shape[1]
    piece_width = model_width // SLICES
    slice_bits = SLICES.bit_length() - 1
    n_devices = lax.axis_size("exp")
    experts = n_devices // SLICES
    capacity = min(tok_dev, max(2, 9 * tok_dev * top_count // (8 * experts)))
    slot_rows = capacity * n_devices
    up_rows, down_rows = (
        lax.all_gather(w_up, "rep", axis=0, tiled=True),
        lax.all_gather(w_down_t, "rep", axis=0, tiled=True),
    )
    flat_route = routes.reshape(-1)
    choice_count = flat_route.shape[0]
    onehot = (flat_route[:, None] == jnp.arange(experts, dtype=jnp.int32)[None, :]).astype(
        jnp.int32
    )
    earlier = jnp.cumsum(onehot, axis=0) - onehot
    slot_index = jnp.sum(earlier * onehot, axis=1)
    position = slot_index * experts + flat_route
    matches = position[None, :] == jnp.arange(capacity * experts, dtype=jnp.int32)[:, None]
    filled = jnp.any(matches, axis=1)
    chosen = jnp.sum(
        jnp.where(matches, jnp.arange(choice_count, dtype=jnp.int32)[None, :], 0), axis=1
    )
    source_row = chosen // top_count
    weight = gates.reshape(-1)[chosen]
    inputs_buf = jnp.where(filled[:, None], tokens[source_row], jnp.zeros((), tokens.dtype))
    inputs_buf = inputs_buf.reshape(capacity, n_devices, piece_width)
    grads_buf = jnp.where(
        filled[:, None], weight[:, None] * cotangent[source_row].astype(jnp.float32), 0.0
    )
    grads_buf = grads_buf.astype(jnp.bfloat16).reshape(capacity, n_devices, piece_width)
    inputs_in = lax.all_to_all(inputs_buf, "exp", split_axis=1, concat_axis=1, tiled=True)
    x_rows = inputs_in.reshape(slot_rows, piece_width)
    partial_value = jnp.dot(x_rows, up_rows, preferred_element_type=jnp.float32).astype(
        jnp.bfloat16
    )
    collected = partial_value[None]
    for bit_number in range(slice_bits):
        collected = jnp.concatenate([collected, swapped(collected, "exp", bit_number)], axis=0)
    activation = jnp.sum(collected.astype(jnp.float32), axis=0)
    gating = jax.nn.sigmoid(activation)
    hidden_act = (activation * gating).astype(jnp.bfloat16)
    out_rows = contract_last(hidden_act, down_rows).astype(jnp.bfloat16)
    out_buf = out_rows.reshape(capacity, n_devices, piece_width)
    out_back = lax.all_to_all(out_buf, "exp", split_axis=1, concat_axis=1, tiled=True)
    grads_in = lax.all_to_all(grads_buf, "exp", split_axis=1, concat_axis=1, tiled=True)
    d_rows = grads_in.reshape(slot_rows, piece_width)
    grad_partial = jnp.dot(d_rows, down_rows, preferred_element_type=jnp.float32).astype(
        jnp.bfloat16
    )
    grad_collected = grad_partial[None]
    for bit_number in range(slice_bits):
        grad_collected = jnp.concatenate(
            [grad_collected, swapped(grad_collected, "exp", bit_number)], axis=0
        )
    grad_summed = jnp.sum(grad_collected.astype(jnp.float32), axis=0)
    act_grad = (grad_summed * gating * (1.0 + activation * (1.0 - gating))).astype(jnp.bfloat16)
    dx_rows = contract_last(act_grad, up_rows).astype(jnp.bfloat16)
    dx_buf = dx_rows.reshape(capacity, n_devices, piece_width)
    up_term = contract_first(x_rows, act_grad)
    down_term = contract_first(d_rows, hidden_act)
    weight_sums = lax.psum_scatter(
        jnp.concatenate([up_term, down_term], axis=1).astype(jnp.bfloat16),
        "rep",
        scatter_dimension=0,
        tiled=True,
    ).astype(jnp.float32)
    hidden = up_rows.shape[1]
    grad_up = weight_sums[:, :hidden]
    grad_down_t = weight_sums[:, hidden:]
    dx_back = lax.all_to_all(dx_buf, "exp", split_axis=1, concat_axis=1, tiled=True)
    out_table = out_back.reshape(capacity * experts, model_width)
    dx_table = dx_back.reshape(capacity * experts, model_width)
    picked = out_table[position].astype(jnp.float32)
    repeated = jnp.repeat(cotangent, top_count, axis=0).astype(jnp.float32)
    grad_gates = jnp.sum(repeated * picked, axis=1).reshape(tok_dev, top_count)
    grad_tokens = jnp.sum(
        dx_table[position].astype(jnp.float32).reshape(tok_dev, top_count, model_width), axis=1
    )
    return (grad_tokens.astype(jnp.bfloat16), grad_gates, grad_up, grad_down_t)


def solution(mesh):
    placed = (
        P(("rep", "exp"), None),
        P(("rep", "exp"), None),
        P(("rep", "exp"), None),
        P(("rep", "exp"), None),
        P(("exp", "rep"), None),
        P(("exp", "rep"), None),
    )
    return jax.shard_map(
        shards,
        mesh=mesh,
        in_specs=placed,
        out_specs=(
            P(("rep", "exp"), None),
            P(("rep", "exp"), None),
            P(("exp", "rep"), None),
            P(("exp", "rep"), None),
        ),
        check_vma=False,
    )
```

profile of v0, /device:TPU:1, one launch (start us, length us, event | category | flops | bytes accessed | tf_op | source)
XLA Modules:
  0.0 662.3 jit_solution(17063361368460367469)
XLA Ops:
  7.2 0.8 fusion.5
  8.2 0.8 select_reduce_fusion.1
  9.9 4.5 gather_fusion.1
  14.4 1.7 reshape.95
  16.1 1.6 gather_fusion
  18.1 3.1 fusion.1
  21.2 19.1 %all-to-all-start = ((bf16[9,64,896]{2,0,1:T(8,128)(2,1)}), bf16[9,64,896]{2,0,1:T(8,128)(2,1)S(1)}, u32[]{:S(2)}, u32[]{:S(2)}) async-start(bf16[9,64,896]{2,0,1:T(8,128)(2,1)} %fusion.1), calls=%async_computation | async-start | bytes 3670016 | tf_op jit(solution)/shard_map/all_to_all | solution.py:73
  40.3 0.7 all-gather.3.cloned.1.call-update
  41.0 2.2 gather_fusion.2
  43.2 2.5 gather.20
  45.7 3.2 copy_select_fusion
  48.9 73.1 %all-to-all-done = bf16[9,64,896]{2,0,1:T(8,128)(2,1)S(1)} async-done(((bf16[9,64,896]{2,0,1:T(8,128)(2,1)}), bf16[9,64,896]{2,0,1:T(8,128)(2,1)S(1)}, u32[]{:S(2)}, u32[]{:S(2)}) %all-to-all-start) | async-done | bytes 1032224 | tf_op jit(solution)/shard_map/all_to_all | solution.py:73
  122.0 13.0 %all-to-all-start.1 = ((bf16[9,64,896]{2,0,1:T(8,128)(2,1)}), bf16[9,64,896]{2,0,1:T(8,128)(2,1)}, u32[]{:S(2)}, u32[]{:S(2)}) async-start(bf16[9,64,896]{2,0,1:T(8,128)(2,1)} %copy_select_fusion), calls=%async_computation.1 | async-start | bytes 3670016 | tf_op jit(solution)/shard_map/all_to_all | solution.py:59
  135.0 0.7 all-gather.5.cloned.1.call-update
  135.7 1.2 copy.37
  136.9 3.2 fusion.2
  140.1 2.9 collective-permute-start
  143.0 73.6 %all-to-all-done.1 = bf16[9,64,896]{2,0,1:T(8,128)(2,1)} async-done(((bf16[9,64,896]{2,0,1:T(8,128)(2,1)}), bf16[9,64,896]{2,0,1:T(8,128)(2,1)}, u32[]{:S(2)}, u32[]{:S(2)}) %all-to-all-start.1) | async-done | bytes 1032224 | tf_op jit(solution)/shard_map/all_to_all | solution.py:59
  216.5 2.7 copy.39
  219.3 3.2 fusion.3
  222.5 6.9 %collective-permute-start.2 = (bf16[1,576,1024]{2,1,0:T(8,128)(2,1)S(1)}, bf16[1,576,1024]{2,1,0:T(8,128)(2,1)S(1)}, u32[]{:S(2)}, u32[]{:S(2)}) collective-permute-start(bf16[1,576,1024]{2,1,0:T(8,128)(2,1)S(1)} %fusion.3), channel_id=1, source_target_pairs={{0,1},{1,0},{2,3},{3,2},{4,5},{5,4},{6,7},{7,6},{8,9},{9,8},{10,11... | collective-permute-start | bytes 3538952 | tf_op jit(solution)/shard_map/ppermute | solution.py:10
  229.4 10.4 %collective-permute-done = bf16[1,576,1024]{2,1,0:T(8,128)(2,1)S(1)} collective-permute-done((bf16[1,576,1024]{2,1,0:T(8,128)(2,1)S(1)}, bf16[1,576,1024]{2,1,0:T(8,128)(2,1)S(1)}, u32[]{:S(2)}, u32[]{:S(2)}) %collective-permute-start) | collective-permute-done | bytes 1179680 | tf_op jit(solution)/shard_map/ppermute | solution.py:10
  240.0 4.1 collective-permute-start.1
  244.1 43.5 %collective-permute-done.2 = bf16[1,576,1024]{2,1,0:T(8,128)(2,1)S(1)} collective-permute-done((bf16[1,576,1024]{2,1,0:T(8,128)(2,1)S(1)}, bf16[1,576,1024]{2,1,0:T(8,128)(2,1)S(1)}, u32[]{:S(2)}, u32[]{:S(2)}) %collective-permute-start.2) | collective-permute-done | bytes 1179680 | tf_op jit(solution)/shard_map/ppermute | solution.py:10
  287.8 1.9 collective-permute-start.3
  289.7 104.7 %collective-permute-done.1 = bf16[2,576,1024]{2,1,0:T(8,128)(2,1)S(1)} collective-permute-done((bf16[2,576,1024]{2,1,0:T(8,128)(2,1)S(1)}, bf16[2,576,1024]{2,1,0:T(8,128)(2,1)S(1)}, u32[]{:S(2)}, u32[]{:S(2)}) %collective-permute-start.1) | collective-permute-done | bytes 2359328 | tf_op jit(solution)/shard_map/ppermute | solution.py:10
  394.4 1.2 convert_reduce_fusion.1
  395.7 49.3 %collective-permute-done.3 = bf16[2,576,1024]{2,1,0:T(8,128)(2,1)S(1)} collective-permute-done((bf16[2,576,1024]{2,1,0:T(8,128)(2,1)S(1)}, bf16[2,576,1024]{2,1,0:T(8,128)(2,1)S(1)}, u32[]{:S(2)}, u32[]{:S(2)}) %collective-permute-start.3) | collective-permute-done | bytes 2359328 | tf_op jit(solution)/shard_map/ppermute | solution.py:10
  445.0 1.1 convert_reduce_fusion
  446.1 0.9 multiply_convert_fusion.1
  447.6 1.4 convolution_convert_fusion.5
  449.1 1.9 copy.40
  451.0 16.7 %all-to-all-start.2 = ((bf16[9,64,896]{2,0,1:T(8,128)(2,1)}), bf16[9,64,896]{2,0,1:T(8,128)(2,1)}, u32[]{:S(2)}, u32[]{:S(2)}) async-start(bf16[9,64,896]{2,0,1:T(8,128)(2,1)} %copy.40), calls=%async_computation.2 | async-start | bytes 3670016 | tf_op jit(solution)/shard_map/all_to_all | solution.py:98
  467.8 3.3 convolution_convert_fusion.1
  471.1 1.7 convolution_convert_fusion
  472.8 2.1 pad_maximum_fusion
  475.0 2.9 convolution_convert_fusion.4
  477.9 1.9 copy.42
  479.8 68.3 %all-to-all-done.2 = bf16[9,64,896]{2,0,1:T(8,128)(2,1)} async-done(((bf16[9,64,896]{2,0,1:T(8,128)(2,1)}), bf16[9,64,896]{2,0,1:T(8,128)(2,1)}, u32[]{:S(2)}, u32[]{:S(2)}) %all-to-all-start.2) | async-done | bytes 1032224 | tf_op jit(solution)/shard_map/all_to_all | solution.py:98
  548.0 13.9 %all-to-all-start.3 = ((bf16[9,64,896]{2,0,1:T(8,128)(2,1)}), bf16[9,64,896]{2,0,1:T(8,128)(2,1)}, u32[]{:S(2)}, u32[]{:S(2)}) async-start(bf16[9,64,896]{2,0,1:T(8,128)(2,1)} %copy.42), calls=%async_computation.3 | async-start | bytes 3670016 | tf_op jit(solution)/shard_map/all_to_all | solution.py:72
  562.0 1.7 copy.41
  564.4 78.7 %all-to-all-done.3 = bf16[9,64,896]{2,0,1:T(8,128)(2,1)} async-done(((bf16[9,64,896]{2,0,1:T(8,128)(2,1)}), bf16[9,64,896]{2,0,1:T(8,128)(2,1)}, u32[]{:S(2)}, u32[]{:S(2)}) %all-to-all-start.3) | async-done | bytes 1032224 | tf_op jit(solution)/shard_map/all_to_all | solution.py:72
  643.1 2.7 copy.43
  645.8 1.7 reshape.93
  647.6 2.0 gather_fusion.3
  649.6 2.0 gather_fusion.4
  651.7 2.0 multiply_reduce_fusion
  653.7 2.1 fusion.7
  (38 shorter events, 3.3 us)
Async XLA Ops:
  7.2 33.8 %copy-start = (bf16[128,3584]{1,0:T(8,128)(2,1)S(1)}, bf16[128,3584]{1,0:T(8,128)(2,1)}, u32[]{:S(2)}) copy-start(bf16[128,3584]{1,0:T(8,128)(2,1)} %param.6) | copy-start | bytes 2752516
  14.4 1.7 copy-start.1
  21.2 100.8 %all-to-all-start = ((bf16[9,64,896]{2,0,1:T(8,128)(2,1)}), bf16[9,64,896]{2,0,1:T(8,128)(2,1)S(1)}, u32[]{:S(2)}, u32[]{:S(2)}) async-start(bf16[9,64,896]{2,0,1:T(8,128)(2,1)} %fusion.1), calls=%async_computation | async-start | bytes 3670016 | tf_op jit(solution)/shard_map/all_to_all | solution.py:73
  40.3 96.6 %all-gather.3.cloned.1.call-start = ((), (), s32[]{:S(2)}) async-start(), calls=%async_computation.5 | async-start | bytes 2064384 | tf_op jit(solution)/shard_map/all_gather | solution.py:36
  122.0 94.6 %all-to-all-start.1 = ((bf16[9,64,896]{2,0,1:T(8,128)(2,1)}), bf16[9,64,896]{2,0,1:T(8,128)(2,1)}, u32[]{:S(2)}, u32[]{:S(2)}) async-start(bf16[9,64,896]{2,0,1:T(8,128)(2,1)} %copy_select_fusion), calls=%async_computation.1 | async-start | bytes 3670016 | tf_op jit(solution)/shard_map/all_to_all | solution.py:59
  134.9 84.3 %all-gather.5.cloned.1.call-start = ((), (), s32[]{:S(2)}) async-start(), calls=%async_computation.6 | async-start | bytes 2064384 | tf_op jit(solution)/shard_map/all_gather | solution.py:35
  140.1 99.7 %collective-permute-start = (bf16[1,576,1024]{2,1,0:T(8,128)(2,1)S(1)}, bf16[1,576,1024]{2,1,0:T(8,128)(2,1)S(1)}, u32[]{:S(2)}, u32[]{:S(2)}) collective-permute-start(bf16[1,576,1024]{2,1,0:T(8,128)(2,1)S(1)} %fusion.2), channel_id=1, source_target_pairs={{0,1},{1,0},{2,3},{3,2},{4,5},{5,4},{6,7},{7,6},{8,9},{9,8},{10,11... | collective-permute-start | bytes 3538952 | tf_op jit(solution)/shard_map/ppermute | solution.py:10
  222.5 65.1 %collective-permute-start.2 = (bf16[1,576,1024]{2,1,0:T(8,128)(2,1)S(1)}, bf16[1,576,1024]{2,1,0:T(8,128)(2,1)S(1)}, u32[]{:S(2)}, u32[]{:S(2)}) collective-permute-start(bf16[1,576,1024]{2,1,0:T(8,128)(2,1)S(1)} %fusion.3), channel_id=1, source_target_pairs={{0,1},{1,0},{2,3},{3,2},{4,5},{5,4},{6,7},{7,6},{8,9},{9,8},{10,11... | collective-permute-start | bytes 3538952 | tf_op jit(solution)/shard_map/ppermute | solution.py:10
  240.0 154.4 %collective-permute-start.1 = (bf16[2,576,1024]{2,1,0:T(8,128)(2,1)S(1)}, bf16[2,576,1024]{2,1,0:T(8,128)(2,1)S(1)}, u32[]{:S(2)}, u32[]{:S(2)}) collective-permute-start(bf16[2,576,1024]{2,1,0:T(8,128)(2,1)S(1)} %pad_maximum_fusion.1), channel_id=1, source_target_pairs={{0,2},{1,3},{2,0},{3,1},{4,6},{5,7},{6,4},{7,5},{8,10},{9,11},{10,... | collective-permute-start | bytes 7077896 | tf_op jit(solution)/shard_map/ppermute | solution.py:10
  287.8 157.2 %collective-permute-start.3 = (bf16[2,576,1024]{2,1,0:T(8,128)(2,1)S(1)}, bf16[2,576,1024]{2,1,0:T(8,128)(2,1)S(1)}, u32[]{:S(2)}, u32[]{:S(2)}) collective-permute-start(bf16[2,576,1024]{2,1,0:T(8,128)(2,1)S(1)} %pad_maximum_fusion.2), channel_id=1, source_target_pairs={{0,2},{1,3},{2,0},{3,1},{4,6},{5,7},{6,4},{7,5},{8,10},{9,11},{10,... | collective-permute-start | bytes 7077896 | tf_op jit(solution)/shard_map/ppermute | solution.py:10
  446.1 1.5 copy-start.6
  447.6 1.4 copy-start.3
  451.0 97.0 %all-to-all-start.2 = ((bf16[9,64,896]{2,0,1:T(8,128)(2,1)}), bf16[9,64,896]{2,0,1:T(8,128)(2,1)}, u32[]{:S(2)}, u32[]{:S(2)}) async-start(bf16[9,64,896]{2,0,1:T(8,128)(2,1)} %copy.40), calls=%async_computation.2 | async-start | bytes 3670016 | tf_op jit(solution)/shard_map/all_to_all | solution.py:98
  467.7 186.0 %reduce-scatter.2.cloned.1.call-start = ((), (), s32[]{:S(2)}) async-start(), calls=%async_computation.7 | async-start | bytes 4128768 | tf_op jit(solution)/shard_map/reduce_scatter | solution.py:89
  467.8 3.3 copy-start.4
  479.8 82.2 %copy-start.5 = (s32[128,1]{0,1:T(1,128)S(1)}, s32[128,1]{0,1:T(1,128)}, u32[]{:S(2)}) copy-start(s32[128,1]{0,1:T(1,128)} %param.9) | copy-start | bytes 1540
  548.0 95.1 %all-to-all-start.3 = ((bf16[9,64,896]{2,0,1:T(8,128)(2,1)}), bf16[9,64,896]{2,0,1:T(8,128)(2,1)}, u32[]{:S(2)}, u32[]{:S(2)}) async-start(bf16[9,64,896]{2,0,1:T(8,128)(2,1)} %copy.42), calls=%async_computation.3 | async-start | bytes 3670016 | tf_op jit(solution)/shard_map/all_to_all | solution.py:72
  649.6 2.0 copy-start.2
Sparse Core Ops, SparseCore 0:
  43.2 34.2 all-gather.2
  137.9 34.1 all-gather.4
  475.1 45.5 reduce-scatter.1
where the time goes:
time: 669 us; the launch traced here: 662 us
  waiting for transfers between devices  503 us (75%)
  starting transfers between devices  78.6 us (12%)
  local copies, waits for them, and re-layouts  34 us (5%)
  other arithmetic  16.9 us (3%)
  matrix products  15.8 us (2%)
  between operations  14.1 us (2%)
    ppermute x4, waiting for transfers between devices, swapped(): lax.ppermute(x, axis, [(i, i ^ 1 << distance) for i in range(lax.axis_siz...  208 us
    all_to_all x1, waiting for transfers between devices, shards(): lax.all_to_all(out_buf, 'exp', split_axis=1, concat_axis=1, tiled=True)  78.7 us
    all_to_all x1, waiting for transfers between devices, shards(): lax.all_to_all(inputs_buf, 'exp', split_axis=1, concat_axis=1, tiled=True)  73.6 us
    all_to_all x1, waiting for transfers between devices, shards(): lax.all_to_all(grads_buf, 'exp', split_axis=1, concat_axis=1, tiled=True)  73.1 us
    all_to_all x1, waiting for transfers between devices, shards(): lax.all_to_all(dx_buf, 'exp', split_axis=1, concat_axis=1, tiled=True)  68.3 us
    all_to_all x1, starting transfers between devices, shards(): lax.all_to_all(grads_buf, 'exp', split_axis=1, concat_axis=1, tiled=True)  19.1 us
    all_to_all x1, starting transfers between devices, shards(): lax.all_to_all(dx_buf, 'exp', split_axis=1, concat_axis=1, tiled=True)  16.7 us
    ppermute x4, starting transfers between devices, swapped(): lax.ppermute(x, axis, [(i, i ^ 1 << distance) for i in range(lax.axis_siz...  15.8 us
  transfers between devices with their start and end apart: 11, of which 8 were waited for; matrix products, arithmetic and copies ran while one was open for 7% of the time, Pallas kernels for 0%

commit v1 on v0

v1 whole, which is shorter than its diff:
```python
import jax
import jax.numpy as jnp
from jax import lax
from jax.sharding import PartitionSpec as P

SLICES = 4
LANES = 128


def contract(left, right, dims):
    return lax.dot_general(
        left, right, ((dims[0], dims[1]), ((), ())), preferred_element_type=jnp.float32
    )


def xor_permute(x, bits):
    return lax.ppermute(x, "exp", [(i, i ^ bits) for i in range(lax.axis_size("exp"))])


def split3(x):
    first = x.astype(jnp.bfloat16)
    rest = x - first.astype(jnp.float32)
    second = rest.astype(jnp.bfloat16)
    third = (rest - second.astype(jnp.float32)).astype(jnp.bfloat16)
    return first, second, third


def shards(tokens, cotangent, gates, routes, w_up, w_down_t):
    tok_dev, model_width = tokens.shape
    piece = model_width // SLICES
    tiles = piece // LANES
    n_dev = lax.axis_size("exp")
    experts = n_dev // SLICES
    slots = 8
    quarter = n_dev // SLICES
    hidden = w_up.shape[1]
    bf16, f32 = jnp.bfloat16, jnp.float32
    me = lax.axis_index("exp") % SLICES

    up = lax.all_gather(w_up, "rep", axis=0, tiled=True)
    down = lax.all_gather(w_down_t, "rep", axis=0, tiled=True)

    route = routes.reshape(-1)
    order = jnp.arange(tok_dev, dtype=jnp.int32)
    same = (route[:, None] == route[None, :]) & (order[None, :] < order[:, None])
    slot = jnp.sum(same.astype(jnp.int32), axis=1)
    main_pos = jnp.where(slot < slots, route * slots + slot, experts * slots + route)
    rows = experts * (slots + 1)
    pick = (main_pos[None, :] == jnp.arange(rows, dtype=jnp.int32)[:, None]).astype(bf16)

    def dispatch(values):
        table = contract(pick, values, ((1,), (0,))).astype(bf16)
        main = table[: experts * slots].reshape(experts, slots, SLICES, tiles, LANES)
        main = main.transpose(0, 2, 3, 1, 4).reshape(n_dev, tiles, slots, LANES)
        extra = table[experts * slots :].reshape(n_dev, 1, tiles, LANES)
        extra = jnp.pad(extra, ((0, 0), (0, 0), (0, slots - tiles), (0, 0)))
        return lax.all_to_all(
            jnp.concatenate([main, extra], axis=1), "exp", split_axis=0, concat_axis=0, tiled=True
        )

    def unpack(got):
        main = got[:, :tiles].transpose(0, 2, 1, 3).reshape(SLICES, quarter * slots, piece)
        extra = got[:, tiles, :tiles].reshape(SLICES, quarter, piece)
        both = jnp.concatenate([main, extra], axis=1)
        return [
            lax.dynamic_index_in_dim(both, me ^ d, axis=0, keepdims=False) for d in range(SLICES)
        ]

    def reduced(blocks, weights):
        parts = [
            contract(blocks[d], weights, ((1,), (0,))).astype(bf16) for d in range(1, SLICES)
        ]
        got = [xor_permute(parts[d - 1], d) for d in range(1, SLICES)]
        own = contract(blocks[0], weights, ((1,), (0,))).astype(bf16)
        total = own.astype(f32)
        for part in got:
            total = total + part.astype(f32)
        return total

    def gathered(block):
        return [block] + [xor_permute(block, d) for d in range(1, SLICES)]

    x_blocks = unpack(dispatch(tokens))
    out_grad = (gates * cotangent.astype(f32)).astype(bf16)
    d_blocks = unpack(dispatch(out_grad))

    activation = reduced(x_blocks, up)
    gating = jax.nn.sigmoid(activation)
    hidden_act = (activation * gating).astype(bf16)
    h_all = jnp.concatenate(gathered(hidden_act), axis=0)
    hidden_grad = reduced(d_blocks, down)
    act_grad = (hidden_grad * gating * (1.0 + activation * (1.0 - gating))).astype(bf16)
    dots = jnp.sum(hidden_act.astype(f32) * hidden_grad, axis=1)
    g_blocks = gathered(act_grad)
    g_all = jnp.concatenate(g_blocks, axis=0)

    down_term = contract(jnp.concatenate(d_blocks, axis=0), h_all, ((0,), (0,))).astype(bf16)
    grad_down_t = lax.psum_scatter(down_term, "rep", scatter_dimension=0, tiled=True).astype(f32)
    up_term = contract(jnp.concatenate(x_blocks, axis=0), g_all, ((0,), (0,))).astype(bf16)
    grad_up = lax.psum_scatter(up_term, "rep", scatter_dimension=0, tiled=True).astype(f32)

    dx = contract(g_all, up, ((1,), (1,))).astype(bf16)
    dx = dx.reshape(SLICES, quarter * (slots + 1), piece)
    dx = jnp.stack(
        [lax.dynamic_index_in_dim(dx, me ^ d, axis=0, keepdims=False) for d in range(SLICES)]
    )
    main = dx[:, : quarter * slots].reshape(n_dev, slots, tiles, LANES).transpose(0, 2, 1, 3)
    extra = dx[:, quarter * slots :].reshape(n_dev, 1, tiles, LANES)
    per_source = jnp.concatenate(
        [dots[: quarter * slots].reshape(quarter, slots), dots[quarter * slots :][:, None]], axis=1
    )
    packed = jnp.concatenate(split3(per_source), axis=1)
    packed = jnp.pad(packed, ((0, 0), (0, LANES - packed.shape[1])))
    own = (jnp.arange(SLICES, dtype=jnp.int32) == me)[:, None, None]
    spare = jnp.where(own, packed[None], jnp.zeros((), bf16)).reshape(n_dev, 1, 1, LANES)
    extra = jnp.concatenate([extra, spare], axis=2)
    back = lax.all_to_all(
        jnp.concatenate([main, extra], axis=1), "exp", split_axis=0, concat_axis=0, tiled=True
    )

    main = back[:, :tiles].reshape(experts, SLICES, tiles, slots, LANES)
    main = main.transpose(0, 3, 1, 2, 4).reshape(experts * slots, model_width)
    extra = back[:, tiles, :tiles].reshape(experts, model_width)
    table = jnp.concatenate([main, extra], axis=0)
    grad_tokens = contract(pick, table, ((0,), (0,))).astype(bf16)
    spare = back[:, tiles, tiles].astype(f32).reshape(experts, SLICES, LANES).sum(axis=1)
    spare = spare[:, : 3 * (slots + 1)].reshape(experts, 3, slots + 1).sum(axis=1)
    flat = jnp.concatenate([spare[:, :slots].reshape(-1), spare[:, slots]])
    hit = main_pos[:, None] == jnp.arange(rows, dtype=jnp.int32)[None, :]
    grad_gates = jnp.sum(jnp.where(hit, flat[None, :], 0.0), axis=1, keepdims=True) / gates
    return grad_tokens, grad_gates, grad_up, grad_down_t


def solution(mesh):
    token_spec, weight_spec = P(("rep", "exp"), None), P(("exp", "rep"), None)
    return jax.shard_map(
        shards,
        mesh=mesh,
        in_specs=(token_spec,) * 4 + (weight_spec,) * 2,
        out_specs=(token_spec, token_spec, weight_spec, weight_spec),
        check_vma=False,
    )
```

time: 669 us -> 330 us (0.49)
  waiting for transfers between devices: 503 us -> 184 us
  local copies, waits for them, and re-layouts: 34 us -> 9.46 us
  matrix products: 15.8 us -> 23.6 us
    all_to_all x4 -> x3, waiting for transfers between devices: 294 us -> 82.7 us  [the longest x2 82.7 us: dispatch(): lax.all_to_all(jnp.concatenate([main, extra], axis=1), 'exp', split_axis=...]
    ppermute x4 -> x12, waiting for transfers between devices: 208 us -> 59.4 us  [xor_permute(): lax.ppermute(x, 'exp', [(i, i ^ bits) for i in range(lax.axis_size('exp'))])]
    reduce_scatter x1 -> x2, waiting for transfers between devices: 0.01 us -> 40.8 us  [the longest x1 40.8 us: shards(): lax.psum_scatter(up_term, 'rep', scatter_dimension=0, tiled=True)]
    ppermute x4 -> x12, starting transfers between devices: 15.8 us -> 37.4 us  [xor_permute(): lax.ppermute(x, 'exp', [(i, i ^ bits) for i in range(lax.axis_size('exp'))])]
    all_to_all x4 -> x3, starting transfers between devices: 62.7 us -> 43.4 us  [the longest x2 29.4 us: dispatch(): lax.all_to_all(jnp.concatenate([main, extra], axis=1), 'exp', split_axis=...]
    gather x6 -> x0, local copies, waits for them, and re-layouts: 14.8 us -> none  [the longest x2 4.68 us: shards(): tokens[source_row]]
    all_to_all x4 -> x0, local copies, waits for them, and re-layouts: 8.34 us -> none  [the longest x1 2.72 us: shards(): lax.all_to_all(out_buf, 'exp', split_axis=1, concat_axis=1, tiled=True)]
    dot_general x6 -> x14, matrix products: 15.8 us -> 23.6 us  [contract(): lax.dot_general(left, right, ((dims[0], dims[1]), ((), ())), preferred_el...]
  transfers between devices with their start and end apart: 11 -> 19, of which waited for: 8 -> 8; matrix products, arithmetic and copies ran while one was open for 7% -> 10% of each run, Pallas kernels for 0% -> 0%
where the time goes in v1:
time: 330 us; the launch traced here: 325 us
  waiting for transfers between devices  184 us (56%)
  starting transfers between devices  80.9 us (25%)
  matrix products  23.6 us (7%)
  between operations  14.3 us (4%)
  other arithmetic  12.1 us (4%)
  local copies, waits for them, and re-layouts  9.46 us (3%)
    all_to_all x2, waiting for transfers between devices, dispatch(): lax.all_to_all(jnp.concatenate([main, extra], axis=1), 'exp', split_axis=...  82.7 us
    ppermute x12, waiting for transfers between devices, xor_permute(): lax.ppermute(x, 'exp', [(i, i ^ bits) for i in range(lax.axis_size('exp'))])  59.4 us
    reduce_scatter x1, waiting for transfers between devices, shards(): lax.psum_scatter(up_term, 'rep', scatter_dimension=0, tiled=True)  40.8 us
    ppermute x12, starting transfers between devices, xor_permute(): lax.ppermute(x, 'exp', [(i, i ^ bits) for i in range(lax.axis_size('exp'))])  37.4 us
    all_to_all x2, starting transfers between devices, dispatch(): lax.all_to_all(jnp.concatenate([main, extra], axis=1), 'exp', split_axis=...  29.4 us
    dot_general x14, matrix products, contract(): lax.dot_general(left, right, ((dims[0], dims[1]), ((), ())), preferred_el...  23.6 us
    all_to_all x1, starting transfers between devices, shards(): lax.all_to_all(jnp.concatenate([main, extra], axis=1), 'exp', split_axis=...  14 us
  transfers between devices with their start and end apart: 19, of which 8 were waited for; matrix products, arithmetic and copies ran while one was open for 10% of the time, Pallas kernels for 0%

profile of v1, /device:TPU:1, one launch (start us, length us, event | category | flops | bytes accessed | tf_op | source)
XLA Modules:
  0.0 324.7 jit_solution(10073219279668408964)
XLA Ops:
  7.2 0.9 convert_reduce_fusion
  8.7 0.7 compare_select_fusion.1
  10.1 1.1 pad_maximum_fusion.2
  11.1 19.1 %all-to-all-start.1 = ((bf16[64,8,8,128]{3,2,1,0:T(8,128)(2,1)}), bf16[64,8,8,128]{3,2,1,0:T(8,128)(2,1)S(1)}, u32[]{:S(2)}, u32[]{:S(2)}) async-start(bf16[64,8,8,128]{3,2,1,0:T(8,128)(2,1)} %pad_maximum_fusion.2), calls=%async_computation.1 | async-start | bytes 2097152 | tf_op jit(solution)/shard_map/all_to_all | solution.py:57
  30.3 0.7 all-gather.5.cloned.1.call-update
  31.8 1.1 pad_maximum_fusion.1
  32.9 47.8 %all-to-all-done.1 = bf16[64,8,8,128]{3,2,1,0:T(8,128)(2,1)S(1)} async-done(((bf16[64,8,8,128]{3,2,1,0:T(8,128)(2,1)}), bf16[64,8,8,128]{3,2,1,0:T(8,128)(2,1)S(1)}, u32[]{:S(2)}, u32[]{:S(2)}) %all-to-all-start.1) | async-done | bytes 1048608 | tf_op jit(solution)/shard_map/all_to_all | solution.py:57
  80.7 10.3 %all-to-all-start = ((bf16[64,8,8,128]{3,2,1,0:T(8,128)(2,1)}), bf16[64,8,8,128]{3,2,1,0:T(8,128)(2,1)}, u32[]{:S(2)}, u32[]{:S(2)}) async-start(bf16[64,8,8,128]{3,2,1,0:T(8,128)(2,1)} %pad_maximum_fusion.1), calls=%async_computation | async-start | bytes 2097152 | tf_op jit(solution)/shard_map/all_to_all | solution.py:57
  91.0 0.7 all-gather.3.cloned.1.call-update
  92.1 0.8 fusion.32
  92.9 2.8 convolution_convert_fusion.6
  95.7 4.6 %collective-permute-start.5 = (bf16[144,1024]{1,0:T(8,128)(2,1)}, bf16[144,1024]{1,0:T(8,128)(2,1)}, u32[]{:S(2)}, u32[]{:S(2)}) collective-permute-start(bf16[144,1024]{1,0:T(8,128)(2,1)} %convolution_convert_fusion.6), channel_id=1, source_target_pairs={{0,3},{1,2},{2,1},{3,0},{4,7},{5,6},{6,5},{7,4},{8,11},{9,10},{10,... | collective-permute-start | bytes 884744 | tf_op jit(solution)/shard_map/ppermute | solution.py:17
  100.4 1.2 convolution_convert_fusion.7
  101.6 1.9 collective-permute-start.4
  103.5 1.2 convolution_convert_fusion.8
  104.7 2.7 collective-permute-start.3
  107.4 34.9 %all-to-all-done = bf16[64,8,8,128]{3,2,1,0:T(8,128)(2,1)} async-done(((bf16[64,8,8,128]{3,2,1,0:T(8,128)(2,1)}), bf16[64,8,8,128]{3,2,1,0:T(8,128)(2,1)}, u32[]{:S(2)}, u32[]{:S(2)}) %all-to-all-start) | async-done | bytes 1048608 | tf_op jit(solution)/shard_map/all_to_all | solution.py:57
  142.4 1.6 slice.83
  143.9 1.7 reshape_squeeze.9
  145.6 1.3 slice.82
  146.9 1.0 fusion.40
  147.9 2.3 convolution_convert_fusion.10
  150.2 4.5 %collective-permute-start.2 = (bf16[144,1024]{1,0:T(8,128)(2,1)S(1)}, bf16[144,1024]{1,0:T(8,128)(2,1)S(1)}, u32[]{:S(2)}, u32[]{:S(2)}) collective-permute-start(bf16[144,1024]{1,0:T(8,128)(2,1)S(1)} %convolution_convert_fusion.10), channel_id=1, source_target_pairs={{0,3},{1,2},{2,1},{3,0},{4,7},{5,6},{6,5},{7,4},{8,11},{9,10},{10,... | collective-permute-start | bytes 884744 | tf_op jit(solution)/shard_map/ppermute | solution.py:17
  155.3 2.5 collective-permute-start.1
  158.3 2.4 collective-permute-start
  161.2 8.2 %collective-permute-done.4 = bf16[144,1024]{1,0:T(8,128)(2,1)} collective-permute-done((bf16[144,1024]{1,0:T(8,128)(2,1)}, bf16[144,1024]{1,0:T(8,128)(2,1)}, u32[]{:S(2)}, u32[]{:S(2)}) %collective-permute-start.4) | collective-permute-done | bytes 294944 | tf_op jit(solution)/shard_map/ppermute | solution.py:17
  169.4 18.8 %collective-permute-done.1 = bf16[144,1024]{1,0:T(8,128)(2,1)S(1)} collective-permute-done((bf16[144,1024]{1,0:T(8,128)(2,1)S(1)}, bf16[144,1024]{1,0:T(8,128)(2,1)S(1)}, u32[]{:S(2)}, u32[]{:S(2)}) %collective-permute-start.1) | collective-permute-done | bytes 294944 | tf_op jit(solution)/shard_map/ppermute | solution.py:17
  188.3 2.8 multiply_reduce_fusion
  191.0 3.9 %collective-permute-start.11 = (bf16[144,1024]{1,0:T(8,128)(2,1)S(1)}, bf16[144,1024]{1,0:T(8,128)(2,1)S(1)}, u32[]{:S(2)}, u32[]{:S(2)}) collective-permute-start(bf16[144,1024]{1,0:T(8,128)(2,1)S(1)} %get-tuple-element.5), channel_id=1, source_target_pairs={{0,3},{1,2},{2,1},{3,0},{4,7},{5,6},{6,5},{7,4},{8,11},{9,10},{10,... | collective-permute-start | bytes 884744 | tf_op jit(solution)/shard_map/ppermute | solution.py:17
  194.9 1.9 collective-permute-start.10
  196.8 3.5 %collective-permute-start.9 = (bf16[144,1024]{1,0:T(8,128)(2,1)S(1)}, bf16[144,1024]{1,0:T(8,128)(2,1)S(1)}, u32[]{:S(2)}, u32[]{:S(2)}) collective-permute-start(bf16[144,1024]{1,0:T(8,128)(2,1)S(1)} %get-tuple-element.5), channel_id=1, source_target_pairs={{0,1},{1,0},{2,3},{3,2},{4,5},{5,4},{6,7},{7,6},{8,9},{9,8},{10,11... | collective-permute-start | bytes 884744 | tf_op jit(solution)/shard_map/ppermute | solution.py:17
  200.3 1.7 collective-permute-done.11
  202.0 16.7 %collective-permute-done.10 = bf16[144,1024]{1,0:T(8,128)(2,1)S(1)} collective-permute-done((bf16[144,1024]{1,0:T(8,128)(2,1)S(1)}, bf16[144,1024]{1,0:T(8,128)(2,1)S(1)}, u32[]{:S(2)}, u32[]{:S(2)}) %collective-permute-start.10) | collective-permute-done | bytes 294944 | tf_op jit(solution)/shard_map/ppermute | solution.py:17
  218.7 2.9 convolution_convert_fusion.3
  221.7 2.4 collective-permute-start.8
  224.2 1.9 collective-permute-start.7
  226.1 5.1 %collective-permute-start.6 = (bf16[144,1024]{1,0:T(8,128)(2,1)}, bf16[144,1024]{1,0:T(8,128)(2,1)}, u32[]{:S(2)}, u32[]{:S(2)}) collective-permute-start(bf16[144,1024]{1,0:T(8,128)(2,1)} %get-tuple-element.6), channel_id=1, source_target_pairs={{0,1},{1,0},{2,3},{3,2},{4,5},{5,4},{6,7},{7,6},{8,9},{9,8},{10,11... | collective-permute-start | bytes 884744 | tf_op jit(solution)/shard_map/ppermute | solution.py:17
  231.8 0.7 copy.35
  232.8 0.8 broadcast_select_fusion
  233.6 13.9 %collective-permute-done.7 = bf16[144,1024]{1,0:T(8,128)(2,1)} collective-permute-done((bf16[144,1024]{1,0:T(8,128)(2,1)}, bf16[144,1024]{1,0:T(8,128)(2,1)}, u32[]{:S(2)}, u32[]{:S(2)}) %collective-permute-start.7) | collective-permute-done | bytes 294944 | tf_op jit(solution)/shard_map/ppermute | solution.py:17
  247.5 2.7 convolution_convert_fusion.5
  251.2 1.2 maximum_maximum_fusion
  252.4 14.0 %all-to-all-start.2 = ((bf16[64,8,8,128]{3,2,1,0:T(8,128)(2,1)}), bf16[64,8,8,128]{3,2,1,0:T(8,128)(2,1)S(1)}, u32[]{:S(2)}, u32[]{:S(2)}) async-start(bf16[64,8,8,128]{3,2,1,0:T(8,128)(2,1)} %maximum_maximum_fusion), calls=%async_computation.2 | async-start | bytes 2097152 | tf_op jit(solution)/shard_map/all_to_all | solution.py:117
  266.5 4.0 %convolution_convert_fusion.4 = bf16[896,1024]{1,0:T(8,128)(2,1)} fusion(bf16[144,896]{1,0:T(8,128)(2,1)S(1)} %get-tuple-element.14, bf16[144,896]{1,0:T(8,128)(2,1)S(1)} %get-tuple-element.13, bf16[144,896]{1,0:T(8,128)(2,1)S(1)} %get-tuple-element.11, bf16[144,896]{1,0:T(8,128)(2,1)S(1)} %copy-done.7, bf16[144,1024]{1,0:T(8,128)(2,1)} %collective-permute-done.8, ...), kind=kOutput, calls=%fused_computation.13 | convolution fusion | flops 1066729472 | bytes 4046848 | tf_op jit(solution)/shard_map/dot_general | solution.py:11
  271.2 1.7 convert_element_type.158
  272.9 40.8 %reduce-scatter.3.cloned.1.call-done = bf16[112,1024]{1,0:T(8,128)(2,1)} async-done(((bf16[896,1024]{1,0:T(8,128)(2,1)}), bf16[112,1024]{1,0:T(8,128)(2,1)}) %reduce-scatter.3.cloned.1.call-update) | async-done | bytes 229392 | tf_op jit(solution)/shard_map/reduce_scatter | solution.py:100
  313.7 1.7 convert_element_type.156
  316.7 1.4 convolution_convert_fusion.2
  (98 shorter events, 7.9 us)
Async XLA Ops:
  7.2 2.2 copy-start
  8.1 0.6 copy-start.15
  10.1 20.9 %copy-start.8 = (bf16[128,3584]{1,0:T(8,128)(2,1)S(1)}, bf16[128,3584]{1,0:T(8,128)(2,1)}, u32[]{:S(2)}) copy-start(bf16[128,3584]{1,0:T(8,128)(2,1)} %param.7) | copy-start | bytes 2752516
  10.1 20.9 %copy-start.12 = (f32[128,1]{0,1:T(1,128)S(1)}, f32[128,1]{0,1:T(1,128)}, u32[]{:S(2)}) copy-start(f32[128,1]{0,1:T(1,128)} %param.8) | copy-start | bytes 1540
  11.1 69.5 %all-to-all-start.1 = ((bf16[64,8,8,128]{3,2,1,0:T(8,128)(2,1)}), bf16[64,8,8,128]{3,2,1,0:T(8,128)(2,1)S(1)}, u32[]{:S(2)}, u32[]{:S(2)}) async-start(bf16[64,8,8,128]{3,2,1,0:T(8,128)(2,1)} %pad_maximum_fusion.2), calls=%async_computation.1 | async-start | bytes 2097152 | tf_op jit(solution)/shard_map/all_to_all | solution.py:57
  30.3 62.6 %all-gather.5.cloned.1.call-start = ((), (), s32[]{:S(2)}) async-start(), calls=%async_computation.6 | async-start | bytes 2064384 | tf_op jit(solution)/shard_map/all_gather | solution.py:40
  80.7 61.7 %all-to-all-start = ((bf16[64,8,8,128]{3,2,1,0:T(8,128)(2,1)}), bf16[64,8,8,128]{3,2,1,0:T(8,128)(2,1)}, u32[]{:S(2)}, u32[]{:S(2)}) async-start(bf16[64,8,8,128]{3,2,1,0:T(8,128)(2,1)} %pad_maximum_fusion.1), calls=%async_computation | async-start | bytes 2097152 | tf_op jit(solution)/shard_map/all_to_all | solution.py:57
  91.0 57.0 %all-gather.3.cloned.1.call-start = ((), (), s32[]{:S(2)}) async-start(), calls=%async_computation.5 | async-start | bytes 2064384 | tf_op jit(solution)/shard_map/all_gather | solution.py:41
  91.7 179.5 %reduce-scatter.5.cloned.1.call-start = ((), (), s32[]{:S(2)}) async-start(), calls=%async_computation.8 | async-start | bytes 2064384 | tf_op jit(solution)/shard_map/reduce_scatter | solution.py:98
  92.9 7.5 %copy-start.1 = (bf16[896,1024]{1,0:T(8,128)(2,1)S(1)}, bf16[896,1024]{1,0:T(8,128)(2,1)}, u32[]{:S(2)}) copy-start(bf16[896,1024]{1,0:T(8,128)(2,1)} %all-gather.5.cloned.1.call-done) | copy-start | bytes 5505028
  95.7 62.6 %collective-permute-start.5 = (bf16[144,1024]{1,0:T(8,128)(2,1)}, bf16[144,1024]{1,0:T(8,128)(2,1)}, u32[]{:S(2)}, u32[]{:S(2)}) collective-permute-start(bf16[144,1024]{1,0:T(8,128)(2,1)} %convolution_convert_fusion.6), channel_id=1, source_target_pairs={{0,3},{1,2},{2,1},{3,0},{4,7},{5,6},{6,5},{7,4},{8,11},{9,10},{10,... | collective-permute-start | bytes 884744 | tf_op jit(solution)/shard_map/ppermute | solution.py:17
  101.6 67.8 %collective-permute-start.4 = (bf16[144,1024]{1,0:T(8,128)(2,1)}, bf16[144,1024]{1,0:T(8,128)(2,1)}, u32[]{:S(2)}, u32[]{:S(2)}) collective-permute-start(bf16[144,1024]{1,0:T(8,128)(2,1)} %convolution_convert_fusion.7), channel_id=1, source_target_pairs={{0,2},{1,3},{2,0},{3,1},{4,6},{5,7},{6,4},{7,5},{8,10},{9,11},{10,... | collective-permute-start | bytes 884744 | tf_op jit(solution)/shard_map/ppermute | solution.py:17
  104.7 64.7 %collective-permute-start.3 = (bf16[144,1024]{1,0:T(8,128)(2,1)}, bf16[144,1024]{1,0:T(8,128)(2,1)}, u32[]{:S(2)}, u32[]{:S(2)}) collective-permute-start(bf16[144,1024]{1,0:T(8,128)(2,1)} %convolution_convert_fusion.8), channel_id=1, source_target_pairs={{0,1},{1,0},{2,3},{3,2},{4,5},{5,4},{6,7},{7,6},{8,9},{9,8},{10,11... | collective-permute-start | bytes 884744 | tf_op jit(solution)/shard_map/ppermute | solution.py:17
  145.6 1.3 copy-start.9
  147.9 6.8 %copy-start.2 = (bf16[896,1024]{1,0:T(8,128)(2,1)S(1)}, bf16[896,1024]{1,0:T(8,128)(2,1)}, u32[]{:S(2)}) copy-start(bf16[896,1024]{1,0:T(8,128)(2,1)} %all-gather.3.cloned.1.call-done) | copy-start | bytes 5505028
  147.9 6.8 %copy-start.4 = (bf16[144,896]{1,0:T(8,128)(2,1)S(1)}, bf16[144,896]{1,0:T(8,128)(2,1)}, u32[]{:S(2)}) copy-start(bf16[144,896]{1,0:T(8,128)(2,1)} %get-tuple-element.17) | copy-start | bytes 774148
  147.9 9.8 %copy-start.3 = (bf16[144,896]{1,0:T(8,128)(2,1)S(1)}, bf16[144,896]{1,0:T(8,128)(2,1)}, u32[]{:S(2)}) copy-start(bf16[144,896]{1,0:T(8,128)(2,1)} %get-tuple-element.15) | copy-start | bytes 774148
  150.2 19.2 %collective-permute-start.2 = (bf16[144,1024]{1,0:T(8,128)(2,1)S(1)}, bf16[144,1024]{1,0:T(8,128)(2,1)S(1)}, u32[]{:S(2)}, u32[]{:S(2)}) collective-permute-start(bf16[144,1024]{1,0:T(8,128)(2,1)S(1)} %convolution_convert_fusion.10), channel_id=1, source_target_pairs={{0,3},{1,2},{2,1},{3,0},{4,7},{5,6},{6,5},{7,4},{8,11},{9,10},{10,... | collective-permute-start | bytes 884744 | tf_op jit(solution)/shard_map/ppermute | solution.py:17
  154.8 5.9 %copy-start.6 = (bf16[144,896]{1,0:T(8,128)(2,1)S(1)}, bf16[144,896]{1,0:T(8,128)(2,1)}, u32[]{:S(2)}) copy-start(bf16[144,896]{1,0:T(8,128)(2,1)} %get-tuple-element.12) | copy-start | bytes 774148
  155.3 33.0 %collective-permute-start.1 = (bf16[144,1024]{1,0:T(8,128)(2,1)S(1)}, bf16[144,1024]{1,0:T(8,128)(2,1)S(1)}, u32[]{:S(2)}, u32[]{:S(2)}) collective-permute-start(bf16[144,1024]{1,0:T(8,128)(2,1)S(1)} %convolution_convert_fusion.11), channel_id=1, source_target_pairs={{0,2},{1,3},{2,0},{3,1},{4,6},{5,7},{6,4},{7,5},{8,10},{9,11},{10,... | collective-permute-start | bytes 884744 | tf_op jit(solution)/shard_map/ppermute | solution.py:17
  158.3 30.0 %copy-start.10 = (bf16[144,896]{1,0:T(8,128)(2,1)S(1)}, bf16[144,896]{1,0:T(8,128)(2,1)}, u32[]{:S(2)}) copy-start(bf16[144,896]{1,0:T(8,128)(2,1)} %get-tuple-element.16) | copy-start | bytes 774148
  158.3 30.0 %collective-permute-start = (bf16[144,1024]{1,0:T(8,128)(2,1)S(1)}, bf16[144,1024]{1,0:T(8,128)(2,1)S(1)}, u32[]{:S(2)}, u32[]{:S(2)}) collective-permute-start(bf16[144,1024]{1,0:T(8,128)(2,1)S(1)} %convolution_convert_fusion.12), channel_id=1, source_target_pairs={{0,1},{1,0},{2,3},{3,2},{4,5},{5,4},{6,7},{7,6},{8,9},{9,8},{10,11... | collective-permute-start | bytes 884744 | tf_op jit(solution)/shard_map/ppermute | solution.py:17
  188.2 30.4 %copy-start.5 = (bf16[144,896]{1,0:T(8,128)(2,1)S(1)}, bf16[144,896]{1,0:T(8,128)(2,1)}, u32[]{:S(2)}) copy-start(bf16[144,896]{1,0:T(8,128)(2,1)} %get-tuple-element.18) | copy-start | bytes 774148
  191.0 10.9 %collective-permute-start.11 = (bf16[144,1024]{1,0:T(8,128)(2,1)S(1)}, bf16[144,1024]{1,0:T(8,128)(2,1)S(1)}, u32[]{:S(2)}, u32[]{:S(2)}) collective-permute-start(bf16[144,1024]{1,0:T(8,128)(2,1)S(1)} %get-tuple-element.5), channel_id=1, source_target_pairs={{0,3},{1,2},{2,1},{3,0},{4,7},{5,6},{6,5},{7,4},{8,11},{9,10},{10,... | collective-permute-start | bytes 884744 | tf_op jit(solution)/shard_map/ppermute | solution.py:17
  194.9 23.8 %collective-permute-start.10 = (bf16[144,1024]{1,0:T(8,128)(2,1)S(1)}, bf16[144,1024]{1,0:T(8,128)(2,1)S(1)}, u32[]{:S(2)}, u32[]{:S(2)}) collective-permute-start(bf16[144,1024]{1,0:T(8,128)(2,1)S(1)} %get-tuple-element.5), channel_id=1, source_target_pairs={{0,2},{1,3},{2,0},{3,1},{4,6},{5,7},{6,4},{7,5},{8,10},{9,11},{10,... | collective-permute-start | bytes 884744 | tf_op jit(solution)/shard_map/ppermute | solution.py:17
  196.8 21.9 %collective-permute-start.9 = (bf16[144,1024]{1,0:T(8,128)(2,1)S(1)}, bf16[144,1024]{1,0:T(8,128)(2,1)S(1)}, u32[]{:S(2)}, u32[]{:S(2)}) collective-permute-start(bf16[144,1024]{1,0:T(8,128)(2,1)S(1)} %get-tuple-element.5), channel_id=1, source_target_pairs={{0,1},{1,0},{2,3},{3,2},{4,5},{5,4},{6,7},{7,6},{8,9},{9,8},{10,11... | collective-permute-start | bytes 884744 | tf_op jit(solution)/shard_map/ppermute | solution.py:17
  221.7 11.8 %collective-permute-start.8 = (bf16[144,1024]{1,0:T(8,128)(2,1)}, bf16[144,1024]{1,0:T(8,128)(2,1)}, u32[]{:S(2)}, u32[]{:S(2)}) collective-permute-start(bf16[144,1024]{1,0:T(8,128)(2,1)} %get-tuple-element.6), channel_id=1, source_target_pairs={{0,3},{1,2},{2,1},{3,0},{4,7},{5,6},{6,5},{7,4},{8,11},{9,10},{10,... | collective-permute-start | bytes 884744 | tf_op jit(solution)/shard_map/ppermute | solution.py:17
  224.2 23.3 %collective-permute-start.7 = (bf16[144,1024]{1,0:T(8,128)(2,1)}, bf16[144,1024]{1,0:T(8,128)(2,1)}, u32[]{:S(2)}, u32[]{:S(2)}) collective-permute-start(bf16[144,1024]{1,0:T(8,128)(2,1)} %get-tuple-element.6), channel_id=1, source_target_pairs={{0,2},{1,3},{2,0},{3,1},{4,6},{5,7},{6,4},{7,5},{8,10},{9,11},{10,... | collective-permute-start | bytes 884744 | tf_op jit(solution)/shard_map/ppermute | solution.py:17
  226.1 21.4 %collective-permute-start.6 = (bf16[144,1024]{1,0:T(8,128)(2,1)}, bf16[144,1024]{1,0:T(8,128)(2,1)}, u32[]{:S(2)}, u32[]{:S(2)}) collective-permute-start(bf16[144,1024]{1,0:T(8,128)(2,1)} %get-tuple-element.6), channel_id=1, source_target_pairs={{0,1},{1,0},{2,3},{3,2},{4,5},{5,4},{6,7},{7,6},{8,9},{9,8},{10,11... | collective-permute-start | bytes 884744 | tf_op jit(solution)/shard_map/ppermute | solution.py:17
  250.5 0.8 copy-start.11
  251.2 15.3 %copy-start.7 = (bf16[144,896]{1,0:T(8,128)(2,1)S(1)}, bf16[144,896]{1,0:T(8,128)(2,1)}, u32[]{:S(2)}) copy-start(bf16[144,896]{1,0:T(8,128)(2,1)} %get-tuple-element.12) | copy-start | bytes 774148
  251.2 15.3 %copy-start.13 = (bf16[144,1024]{1,0:T(8,128)(2,1)S(1)}, bf16[144,1024]{1,0:T(8,128)(2,1)}, u32[]{:S(2)}) copy-start(bf16[144,1024]{1,0:T(8,128)(2,1)} %get-tuple-element.6) | copy-start | bytes 884740
  252.4 63.1 %all-to-all-start.2 = ((bf16[64,8,8,128]{3,2,1,0:T(8,128)(2,1)}), bf16[64,8,8,128]{3,2,1,0:T(8,128)(2,1)S(1)}, u32[]{:S(2)}, u32[]{:S(2)}) async-start(bf16[64,8,8,128]{3,2,1,0:T(8,128)(2,1)} %maximum_maximum_fusion), calls=%async_computation.2 | async-start | bytes 2097152 | tf_op jit(solution)/shard_map/all_to_all | solution.py:117
  266.5 47.3 %reduce-scatter.3.cloned.1.call-start = ((), (), s32[]{:S(2)}) async-start(), calls=%async_computation.7 | async-start | bytes 2064384 | tf_op jit(solution)/shard_map/reduce_scatter | solution.py:100
  270.5 0.7 copy-start.14
  270.5 0.7 copy-start.16
Sparse Core Ops, SparseCore 0:
  33.2 34.2 all-gather.4
  93.9 34.4 all-gather.2
  221.7 39.5 reduce-scatter.4
  270.7 43.0 reduce-scatter.2

commit v2 on v1

v2 whole, which is shorter than its diff:
```python
import jax
import jax.numpy as jnp
from jax import lax
from jax.sharding import PartitionSpec as P

SLICES = 4
LANES = 128
BOTH = ("rep", "exp")


def contract(left, right, dims):
    return lax.dot_general(
        left, right, ((dims[0], dims[1]), ((), ())), preferred_element_type=jnp.float32
    )


def split3(x):
    first = x.astype(jnp.bfloat16)
    rest = x - first.astype(jnp.float32)
    second = rest.astype(jnp.bfloat16)
    third = (rest - second.astype(jnp.float32)).astype(jnp.bfloat16)
    return first, second, third


def moved(x, n_rep, n_exp, where):
    pairs = []
    for rep in range(n_rep):
        for exp in range(n_exp):
            y, core, base, far, near = rep // 2, rep % 2, exp // 4 * 4, exp // 2 % 2, exp % 2
            core, far, near = where(core, far, near)
            pairs.append((rep * n_exp + exp, (y * 2 + core) * n_exp + base + far * 2 + near))
    return lax.ppermute(x, BOTH, pairs)


def shards(tokens, cotangent, gates, routes, w_up, w_down_t):
    tok_dev, model_width = tokens.shape
    piece = model_width // SLICES
    tiles = piece // LANES
    n_rep, n_dev = lax.axis_size("rep"), lax.axis_size("exp")
    experts = n_dev // SLICES
    slots = 8
    quarter = n_dev // SLICES
    per_quarter = quarter * (slots + 1)
    hidden = w_up.shape[1]
    bf16, f32 = jnp.bfloat16, jnp.float32
    core, far, near = lax.axis_index("rep") % 2, lax.axis_index("exp") // 2 % 2, lax.axis_index("exp") % 2
    me = core * 2 + near
    y_groups = [list(range(first, n_rep, 2)) for first in range(2)]
    token_groups = [
        [
            (y * 2 + c) * n_dev + e * SLICES + h * 2 + b
            for e in range(experts)
            for c in range(2)
            for b in range(2)
        ]
        for y in range(n_rep // 2)
        for h in range(2)
    ]

    def routed(x):
        return lax.all_to_all(
            x, BOTH, split_axis=0, concat_axis=0, axis_index_groups=token_groups, tiled=True
        )

    def other_core(x):
        return moved(x, n_rep, n_dev, lambda c, h, b: (1 - c, h, b))

    def other_near(x):
        return moved(x, n_rep, n_dev, lambda c, h, b: (c, h, 1 - b))

    def weights(w):
        first = moved(w, n_rep, n_dev, lambda c, h, b: (h, c, b))
        second = moved(w, n_rep, n_dev, lambda c, h, b: (h, 1 - c, b))
        pair = jnp.where(
            far == 0,
            jnp.concatenate([first, second], axis=0),
            jnp.concatenate([second, first], axis=0),
        )
        return lax.all_gather(pair, "rep", axis=0, axis_index_groups=y_groups, tiled=True)

    up = weights(w_up)
    down = weights(w_down_t)

    route = routes.reshape(-1)
    order = jnp.arange(tok_dev, dtype=jnp.int32)
    same = (route[:, None] == route[None, :]) & (order[None, :] < order[:, None])
    slot = jnp.sum(same.astype(jnp.int32), axis=1)
    main_pos = jnp.where(slot < slots, route * slots + slot, experts * slots + route)
    rows = experts * (slots + 1)
    pick = (main_pos[None, :] == jnp.arange(rows, dtype=jnp.int32)[:, None]).astype(bf16)

    def packed_rows(values):
        table = contract(pick, values, ((1,), (0,))).astype(bf16)
        main = table[: experts * slots].reshape(experts, slots, SLICES, tiles, LANES)
        main = main.transpose(0, 2, 3, 1, 4).reshape(n_dev, tiles, slots, LANES)
        extra = table[experts * slots :].reshape(n_dev, 1, tiles, LANES)
        extra = jnp.pad(extra, ((0, 0), (0, 0), (0, slots - tiles), (0, 0)))
        return [main, extra]

    def unpack(got):
        main = got[:, :tiles].transpose(0, 2, 1, 3).reshape(SLICES, quarter * slots, piece)
        extra = got[:, tiles, :tiles].reshape(SLICES, quarter, piece)
        both = jnp.concatenate([main, extra], axis=1)
        blocks = [
            lax.dynamic_index_in_dim(both, me ^ d, axis=0, keepdims=False) for d in range(SLICES)
        ]
        return jnp.concatenate(blocks, axis=0)

    def reduced(rows_in, matrix):
        theirs = contract(rows_in[2 * per_quarter :], matrix, ((1,), (0,))).astype(bf16)
        theirs = other_core(theirs)
        mine = contract(rows_in[: 2 * per_quarter], matrix, ((1,), (0,)))
        mine = mine + theirs.astype(f32)
        passed = other_near(mine[per_quarter:].astype(bf16))
        return mine[:per_quarter] + passed.astype(f32)

    def gathered(block):
        pair = jnp.concatenate([block, other_near(block)], axis=0)
        return jnp.concatenate([pair, other_core(pair)], axis=0)

    out_grad = (gates * cotangent.astype(f32)).astype(bf16)
    got = routed(jnp.concatenate(packed_rows(tokens) + packed_rows(out_grad), axis=1))
    x_rows = unpack(got[:, : tiles + 1])
    d_rows = unpack(got[:, tiles + 1 :])

    activation = reduced(x_rows, up)
    hidden_grad = reduced(d_rows, down)
    gating = jax.nn.sigmoid(activation)
    hidden_act = (activation * gating).astype(bf16)
    h_all = gathered(hidden_act)
    act_grad = (hidden_grad * gating * (1.0 + activation * (1.0 - gating))).astype(bf16)
    dots = jnp.sum(hidden_act.astype(f32) * hidden_grad, axis=1)
    g_all = gathered(act_grad)

    dx = contract(g_all, up, ((1,), (1,))).astype(bf16).reshape(SLICES, per_quarter, piece)
    dx = jnp.stack(
        [lax.dynamic_index_in_dim(dx, me ^ d, axis=0, keepdims=False) for d in range(SLICES)]
    )
    main = dx[:, : quarter * slots].reshape(n_dev, slots, tiles, LANES).transpose(0, 2, 1, 3)
    extra = dx[:, quarter * slots :].reshape(n_dev, 1, tiles, LANES)
    per_source = jnp.concatenate(
        [dots[: quarter * slots].reshape(quarter, slots), dots[quarter * slots :][:, None]], axis=1
    )
    packed = jnp.concatenate(split3(per_source), axis=1)
    packed = jnp.pad(packed, ((0, 0), (0, LANES - packed.shape[1])))
    own = (jnp.arange(SLICES, dtype=jnp.int32) == me)[:, None, None]
    spare = jnp.where(own, packed[None], jnp.zeros((), bf16)).reshape(n_dev, 1, 1, LANES)
    spare = jnp.pad(spare, ((0, 0), (0, 0), (0, slots - tiles - 1), (0, 0)))
    extra = jnp.concatenate([extra, spare], axis=2)
    back = routed(jnp.concatenate([main, extra], axis=1))

    down_term = contract(d_rows, h_all, ((0,), (0,))).astype(bf16)
    up_term = contract(x_rows, g_all, ((0,), (0,))).astype(bf16)
    terms = lax.psum_scatter(
        jnp.concatenate([up_term, down_term], axis=1),
        "rep",
        scatter_dimension=0,
        axis_index_groups=y_groups,
        tiled=True,
    )
    part = terms.shape[0] // 2
    low, high = terms[:part], terms[part:]
    swap = far == 1
    sums = moved(jnp.where(swap, high, low), n_rep, n_dev, lambda c, h, b: (h, c, b)).astype(f32)
    sums = sums + moved(
        jnp.where(swap, low, high), n_rep, n_dev, lambda c, h, b: (1 - h, c, b)
    ).astype(f32)

    main = back[:, :tiles].reshape(experts, SLICES, tiles, slots, LANES)
    main = main.transpose(0, 3, 1, 2, 4).reshape(experts * slots, model_width)
    extra = back[:, tiles, :tiles].reshape(experts, model_width)
    table = jnp.concatenate([main, extra], axis=0)
    grad_tokens = contract(pick, table, ((0,), (0,))).astype(bf16)
    spare = back[:, tiles, tiles].astype(f32).reshape(experts, SLICES, LANES).sum(axis=1)
    spare = spare[:, : 3 * (slots + 1)].reshape(experts, 3, slots + 1).sum(axis=1)
    flat = jnp.concatenate([spare[:, :slots].reshape(-1), spare[:, slots]])
    hit = main_pos[:, None] == jnp.arange(rows, dtype=jnp.int32)[None, :]
    grad_gates = jnp.sum(jnp.where(hit, flat[None, :], 0.0), axis=1, keepdims=True) / gates
    return grad_tokens, grad_gates, sums[:, :hidden], sums[:, hidden:]


def solution(mesh):
    token_spec, weight_spec = P(("rep", "exp"), None), P(("exp", "rep"), None)
    return jax.shard_map(
        shards,
        mesh=mesh,
        in_specs=(token_spec,) * 4 + (weight_spec,) * 2,
        out_specs=(token_spec, token_spec, weight_spec, weight_spec),
        check_vma=False,
    )
```

time: 330 us -> 373 us (1.13); the launches traced: 325 us -> 372 us
  waiting for transfers between devices: 184 us -> 242 us
  matrix products: 23.6 us -> 18.3 us
  local copies, waits for them, and re-layouts: 9.46 us -> 5.41 us
    ppermute x12 -> x14, waiting for transfers between devices: 59.4 us -> 140 us  [moved(): return lax.ppermute(x, BOTH, pairs)]
    all_gather x2, waiting for transfers between devices: 0.01 us -> 51.1 us  [weights(): lax.all_gather(pair, 'rep', axis=0, axis_index_groups=y_groups, tiled=True)]
    reduce_scatter x2 -> x1, waiting for transfers between devices: 40.8 us -> 0.02 us  [shards(): lax.psum_scatter(jnp.concatenate([up_term, down_term], axis=1), 'rep', sc...]
    all_to_all x3 -> x2, waiting for transfers between devices: 82.7 us -> 50.8 us  [routed(): lax.all_to_all(x, BOTH, split_axis=0, concat_axis=0, axis_index_groups=to...]
    all_to_all x3 -> x2, starting transfers between devices: 43.4 us -> 34.9 us  [routed(): lax.all_to_all(x, BOTH, split_axis=0, concat_axis=0, axis_index_groups=to...]
    ppermute x12 -> x14, starting transfers between devices: 37.4 us -> 44.3 us  [moved(): return lax.ppermute(x, BOTH, pairs)]
    dot_general x14 -> x10, matrix products: 23.6 us -> 18.3 us  [contract(): lax.dot_general(left, right, ((dims[0], dims[1]), ((), ())), preferred_el...]
  transfers between devices with their start and end apart: 19 -> 19, of which waited for: 8 -> 12; matrix products, arithmetic and copies ran while one was open for 10% -> 6% of each run, Pallas kernels for 0% -> 0%
where the time goes in v2:
time: 373 us; the launch traced here: 372 us
  waiting for transfers between devices  242 us (65%)
  starting transfers between devices  79.4 us (21%)
  matrix products  18.3 us (5%)
  between operations  14.4 us (4%)
  other arithmetic  12.3 us (3%)
  local copies, waits for them, and re-layouts  5.41 us (1%)
    ppermute x14, waiting for transfers between devices, moved(): return lax.ppermute(x, BOTH, pairs)  140 us
    all_gather x2, waiting for transfers between devices, weights(): lax.all_gather(pair, 'rep', axis=0, axis_index_groups=y_groups, tiled=True)  51.1 us
    all_to_all x2, waiting for transfers between devices, routed(): lax.all_to_all(x, BOTH, split_axis=0, concat_axis=0, axis_index_groups=to...  50.8 us
    ppermute x14, starting transfers between devices, moved(): return lax.ppermute(x, BOTH, pairs)  44.3 us
    all_to_all x2, starting transfers between devices, routed(): lax.all_to_all(x, BOTH, split_axis=0, concat_axis=0, axis_index_groups=to...  34.9 us
    dot_general x10, matrix products, contract(): lax.dot_general(left, right, ((dims[0], dims[1]), ((), ())), preferred_el...  18.3 us
  transfers between devices with their start and end apart: 19, of which 12 were waited for; matrix products, arithmetic and copies ran while one was open for 6% of the time, Pallas kernels for 0%

profile of v2, /device:TPU:1, one launch (start us, length us, event | category | flops | bytes accessed | tf_op | source)
XLA Modules:
  0.0 371.7 jit_solution(853739597305829840)
XLA Ops:
  7.2 0.9 convert_reduce_fusion
  8.1 0.7 compare_select_fusion.1
  8.8 1.7 convolution_convert_fusion
  11.5 1.6 pad_maximum_fusion.1
  13.1 19.6 %all-to-all-start = ((bf16[64,16,8,128]{3,2,1,0:T(8,128)(2,1)}), bf16[64,16,8,128]{3,2,1,0:T(8,128)(2,1)S(1)}, u32[]{:S(2)}, u32[]{:S(2)}) async-start(bf16[64,16,8,128]{3,2,1,0:T(8,128)(2,1)} %pad_maximum_fusion.1), calls=%async_computation | async-start | bytes 4194304 | tf_op jit(solution)/shard_map/all_to_all | solution.py:61
  32.7 2.4 collective-permute-start.1
  35.1 3.0 collective-permute-start
  38.2 95.7 %collective-permute-done.1 = bf16[112,1024]{1,0:T(8,128)(2,1)S(1)} collective-permute-done((bf16[112,1024]{1,0:T(8,128)(2,1)}, bf16[112,1024]{1,0:T(8,128)(2,1)S(1)}, u32[]{:S(2)}, u32[]{:S(2)}) %collective-permute-start.1) | collective-permute-done | bytes 229408 | tf_op jit(solution)/shard_map/ppermute | solution.py:32
  134.4 0.9 maximum_select_fusion
  135.4 1.9 collective-permute-start.5
  137.3 1.9 collective-permute-start.4
  139.2 9.5 %collective-permute-done.5 = bf16[112,1024]{1,0:T(8,128)(2,1)S(1)} collective-permute-done((bf16[112,1024]{1,0:T(8,128)(2,1)}, bf16[112,1024]{1,0:T(8,128)(2,1)S(1)}, u32[]{:S(2)}, u32[]{:S(2)}) %collective-permute-start.5) | collective-permute-done | bytes 229408 | tf_op jit(solution)/shard_map/ppermute | solution.py:32
  148.8 1.0 collective-permute-done.4
  149.7 0.9 maximum_select_fusion.1
  151.0 1.1 fusion.72
  152.1 19.1 %all-gather.3.cloned.1.call-done = bf16[896,1024]{1,0:T(8,128)(2,1)} async-done(((bf16[224,1024]{1,0:T(8,128)(2,1)}), bf16[896,1024]{1,0:T(8,128)(2,1)}) %all-gather.3.cloned.1.call-update) | async-done | bytes 1835024 | tf_op jit(solution)/shard_map/all_gather | solution.py:79
  171.2 3.2 convolution_convert_fusion.7
  174.4 2.7 collective-permute-start.2
  177.3 0.9 fusion.38
  178.2 32.0 %all-gather.5.cloned.1.call-done = bf16[896,1024]{1,0:T(8,128)(2,1)} async-done(((bf16[224,1024]{1,0:T(8,128)(2,1)}), bf16[896,1024]{1,0:T(8,128)(2,1)}) %all-gather.5.cloned.1.call-update) | async-done | bytes 1835024 | tf_op jit(solution)/shard_map/all_gather | solution.py:79
  210.2 2.7 convolution_convert_fusion.6
  212.9 2.7 collective-permute-start.6
  215.7 2.0 convolution_add_fusion.1
  217.7 3.2 collective-permute-start.3
  220.9 0.8 convolution_add_fusion
  221.8 2.1 collective-permute-start.7
  223.9 4.3 %collective-permute-done.3 = bf16[144,1024]{1,0:T(8,128)(2,1)S(1)} collective-permute-done((bf16[144,1024]{1,0:T(8,128)(2,1)S(1)}, bf16[144,1024]{1,0:T(8,128)(2,1)S(1)}, u32[]{:S(2)}, u32[]{:S(2)}) %collective-permute-start.3) | collective-permute-done | bytes 294944 | tf_op jit(solution)/shard_map/ppermute | solution.py:32
  228.2 6.3 %collective-permute-done.7 = bf16[144,1024]{1,0:T(8,128)(2,1)S(1)} collective-permute-done((bf16[144,1024]{1,0:T(8,128)(2,1)S(1)}, bf16[144,1024]{1,0:T(8,128)(2,1)S(1)}, u32[]{:S(2)}, u32[]{:S(2)}) %collective-permute-start.7) | collective-permute-done | bytes 294944 | tf_op jit(solution)/shard_map/ppermute | solution.py:32
  234.9 3.2 collective-permute-start.10
  238.0 2.1 collective-permute-start.8
  240.1 4.3 %collective-permute-done.10 = bf16[144,1024]{1,0:T(8,128)(2,1)S(1)} collective-permute-done((bf16[144,1024]{1,0:T(8,128)(2,1)S(1)}, bf16[144,1024]{1,0:T(8,128)(2,1)S(1)}, u32[]{:S(2)}, u32[]{:S(2)}) %collective-permute-start.10) | collective-permute-done | bytes 294944 | tf_op jit(solution)/shard_map/ppermute | solution.py:32
  244.5 5.0 %collective-permute-start.11 = (bf16[288,1024]{1,0:T(8,128)(2,1)S(1)}, bf16[288,1024]{1,0:T(8,128)(2,1)S(1)}, u32[]{:S(2)}, u32[]{:S(2)}) collective-permute-start(bf16[288,1024]{1,0:T(8,128)(2,1)S(1)} %pad_maximum_fusion.5), channel_id=1, source_target_pairs={{0,64},{1,65},{2,66},{3,67},{4,68},{5,69},{6,70},{7,71},{8,72},{9,... | collective-permute-start | bytes 1769480 | tf_op jit(solution)/shard_map/ppermute | solution.py:32
  249.5 1.3 collective-permute-done.8
  250.8 4.0 %collective-permute-start.9 = (bf16[288,1024]{1,0:T(8,128)(2,1)S(1)}, bf16[288,1024]{1,0:T(8,128)(2,1)S(1)}, u32[]{:S(2)}, u32[]{:S(2)}) collective-permute-start(bf16[288,1024]{1,0:T(8,128)(2,1)S(1)} %pad_maximum_fusion.4), channel_id=1, source_target_pairs={{0,64},{1,65},{2,66},{3,67},{4,68},{5,69},{6,70},{7,71},{8,72},{9,... | collective-permute-start | bytes 1769480 | tf_op jit(solution)/shard_map/ppermute | solution.py:32
  254.8 1.6 convolution_convert_fusion.3
  256.4 0.8 copy-done.7
  257.3 1.6 convolution_convert_fusion.4
  258.9 2.2 pad_maximum_fusion
  262.2 2.9 convolution_convert_fusion.5
  265.6 1.2 maximum_maximum_fusion
  266.8 15.3 %all-to-all-start.1 = ((bf16[64,8,8,128]{3,2,1,0:T(8,128)(2,1)}), bf16[64,8,8,128]{3,2,1,0:T(8,128)(2,1)S(1)}, u32[]{:S(2)}, u32[]{:S(2)}) async-start(bf16[64,8,8,128]{3,2,1,0:T(8,128)(2,1)} %maximum_maximum_fusion), calls=%async_computation.1 | async-start | bytes 2097152 | tf_op jit(solution)/shard_map/all_to_all | solution.py:61
  282.2 50.8 %all-to-all-done.1 = bf16[64,8,8,128]{3,2,1,0:T(8,128)(2,1)S(1)} async-done(((bf16[64,8,8,128]{3,2,1,0:T(8,128)(2,1)}), bf16[64,8,8,128]{3,2,1,0:T(8,128)(2,1)S(1)}, u32[]{:S(2)}, u32[]{:S(2)}) %all-to-all-start.1) | async-done | bytes 1048608 | tf_op jit(solution)/shard_map/all_to_all | solution.py:61
  333.7 1.2 broadcast_select_fusion.1
  335.0 5.0 %collective-permute-start.13 = (bf16[112,2048]{1,0:T(8,128)(2,1)S(1)}, bf16[112,2048]{1,0:T(8,128)(2,1)S(1)}, u32[]{:S(2)}, u32[]{:S(2)}) collective-permute-start(bf16[112,2048]{1,0:T(8,128)(2,1)S(1)} %get-tuple-element.26), channel_id=1, source_target_pairs={{0,64},{1,65},{2,0},{3,1},{4,68},{5,69},{6,4},{7,5},{8,72},{9,73},... | collective-permute-start | bytes 1376264 | tf_op jit(solution)/shard_map/ppermute | solution.py:32
  340.0 5.1 %collective-permute-start.12 = (bf16[112,2048]{1,0:T(8,128)(2,1)S(1)}, bf16[112,2048]{1,0:T(8,128)(2,1)S(1)}, u32[]{:S(2)}, u32[]{:S(2)}) collective-permute-start(bf16[112,2048]{1,0:T(8,128)(2,1)S(1)} %get-tuple-element.25), channel_id=1, source_target_pairs={{0,0},{1,1},{2,64},{3,65},{4,4},{5,5},{6,68},{7,69},{8,8},{9,9},{1... | collective-permute-start | bytes 1376264 | tf_op jit(solution)/shard_map/ppermute | solution.py:32
  345.6 1.4 convolution_convert_fusion.2
  347.0 17.1 %collective-permute-done.12 = bf16[112,2048]{1,0:T(8,128)(2,1)S(1)} collective-permute-done((bf16[112,2048]{1,0:T(8,128)(2,1)S(1)}, bf16[112,2048]{1,0:T(8,128)(2,1)S(1)}, u32[]{:S(2)}, u32[]{:S(2)}) %collective-permute-start.12) | collective-permute-done | bytes 458784 | tf_op jit(solution)/shard_map/ppermute | solution.py:32
  364.1 1.0 fusion.73
  (84 shorter events, 5.5 us)
Async XLA Ops:
  7.2 3.4 copy-start
  13.1 137.6 %all-to-all-start = ((bf16[64,16,8,128]{3,2,1,0:T(8,128)(2,1)}), bf16[64,16,8,128]{3,2,1,0:T(8,128)(2,1)S(1)}, u32[]{:S(2)}, u32[]{:S(2)}) async-start(bf16[64,16,8,128]{3,2,1,0:T(8,128)(2,1)} %pad_maximum_fusion.1), calls=%async_computation | async-start | bytes 4194304 | tf_op jit(solution)/shard_map/all_to_all | solution.py:61
  32.7 138.5 %all-gather.3.cloned.1.call-start = ((), (), s32[]{:S(2)}) async-start(), calls=%async_computation.3 | async-start | bytes 2293760 | tf_op jit(solution)/shard_map/all_gather | solution.py:79
  32.7 101.2 %collective-permute-start.1 = (bf16[112,1024]{1,0:T(8,128)(2,1)}, bf16[112,1024]{1,0:T(8,128)(2,1)S(1)}, u32[]{:S(2)}, u32[]{:S(2)}) collective-permute-start(bf16[112,1024]{1,0:T(8,128)(2,1)} %param.11), channel_id=1, source_target_pairs={{0,2},{1,3},{2,66},{3,67},{4,6},{5,7},{6,70},{7,71},{8,10},{9,11},... | collective-permute-start | bytes 688136 | tf_op jit(solution)/shard_map/ppermute | solution.py:32
  35.1 99.3 %collective-permute-start = (bf16[112,1024]{1,0:T(8,128)(2,1)}, bf16[112,1024]{1,0:T(8,128)(2,1)S(1)}, u32[]{:S(2)}, u32[]{:S(2)}) collective-permute-start(bf16[112,1024]{1,0:T(8,128)(2,1)} %param.11), channel_id=1, source_target_pairs={{0,0},{1,1},{2,64},{3,65},{4,4},{5,5},{6,68},{7,69},{8,8},{9,9},{1... | collective-permute-start | bytes 688136 | tf_op jit(solution)/shard_map/ppermute | solution.py:32
  135.3 74.9 %all-gather.5.cloned.1.call-start = ((), (), s32[]{:S(2)}) async-start(), calls=%async_computation.4 | async-start | bytes 2293760 | tf_op jit(solution)/shard_map/all_gather | solution.py:79
  135.4 13.4 %collective-permute-start.5 = (bf16[112,1024]{1,0:T(8,128)(2,1)}, bf16[112,1024]{1,0:T(8,128)(2,1)S(1)}, u32[]{:S(2)}, u32[]{:S(2)}) collective-permute-start(bf16[112,1024]{1,0:T(8,128)(2,1)} %param.10), channel_id=1, source_target_pairs={{0,2},{1,3},{2,66},{3,67},{4,6},{5,7},{6,70},{7,71},{8,10},{9,11},... | collective-permute-start | bytes 688136 | tf_op jit(solution)/shard_map/ppermute | solution.py:32
  137.3 12.4 %collective-permute-start.4 = (bf16[112,1024]{1,0:T(8,128)(2,1)}, bf16[112,1024]{1,0:T(8,128)(2,1)S(1)}, u32[]{:S(2)}, u32[]{:S(2)}) collective-permute-start(bf16[112,1024]{1,0:T(8,128)(2,1)} %param.10), channel_id=1, source_target_pairs={{0,0},{1,1},{2,64},{3,65},{4,4},{5,5},{6,68},{7,69},{8,8},{9,9},{1... | collective-permute-start | bytes 688136 | tf_op jit(solution)/shard_map/ppermute | solution.py:32
  150.6 183.1 %reduce-scatter.2.cloned.1.call-start = ((), (), s32[]{:S(2)}) async-start(), calls=%async_computation.5 | async-start | bytes 4587520 | tf_op jit(solution)/shard_map/reduce_scatter | solution.py:154
  171.2 6.1 %copy-start.1 = (bf16[64,7,8,128]{3,2,1,0:T(8,128)(2,1)S(1)}, bf16[64,7,8,128]{3,2,1,0:T(8,128)(2,1)}, u32[]{:S(2)}) copy-start(bf16[64,7,8,128]{3,2,1,0:T(8,128)(2,1)} %get-tuple-element.9) | copy-start | bytes 2752516
  174.4 41.3 %collective-permute-start.2 = (bf16[288,1024]{1,0:T(8,128)(2,1)}, bf16[288,1024]{1,0:T(8,128)(2,1)}, u32[]{:S(2)}, u32[]{:S(2)}) collective-permute-start(bf16[288,1024]{1,0:T(8,128)(2,1)} %convolution_convert_fusion.7), channel_id=1, source_target_pairs={{0,64},{1,65},{2,66},{3,67},{4,68},{5,69},{6,70},{7,71},{8,72},{9,... | collective-permute-start | bytes 1769480 | tf_op jit(solution)/shard_map/ppermute | solution.py:32
  210.2 5.4 %copy-start.6 = (bf16[896,1024]{1,0:T(8,128)(2,1)S(1)}, bf16[896,1024]{1,0:T(8,128)(2,1)}, u32[]{:S(2)}) copy-start(bf16[896,1024]{1,0:T(8,128)(2,1)} %all-gather.3.cloned.1.call-done) | copy-start | bytes 5505028
  212.9 8.0 %collective-permute-start.6 = (bf16[288,1024]{1,0:T(8,128)(2,1)S(1)}, bf16[288,1024]{1,0:T(8,128)(2,1)S(1)}, u32[]{:S(2)}, u32[]{:S(2)}) collective-permute-start(bf16[288,1024]{1,0:T(8,128)(2,1)S(1)} %convolution_convert_fusion.6), channel_id=1, source_target_pairs={{0,64},{1,65},{2,66},{3,67},{4,68},{5,69},{6,70},{7,71},{8,72},{9,... | collective-permute-start | bytes 1769480 | tf_op jit(solution)/shard_map/ppermute | solution.py:32
  215.7 5.2 %copy-start.5 = (bf16[896,1024]{1,0:T(8,128)(2,1)S(1)}, bf16[896,1024]{1,0:T(8,128)(2,1)}, u32[]{:S(2)}) copy-start(bf16[896,1024]{1,0:T(8,128)(2,1)} %all-gather.5.cloned.1.call-done) | copy-start | bytes 5505028
  217.7 10.4 %collective-permute-start.3 = (bf16[144,1024]{1,0:T(8,128)(2,1)S(1)}, bf16[144,1024]{1,0:T(8,128)(2,1)S(1)}, u32[]{:S(2)}, u32[]{:S(2)}) collective-permute-start(bf16[144,1024]{1,0:T(8,128)(2,1)S(1)} %slice.171), channel_id=1, source_target_pairs={{0,1},{1,0},{2,3},{3,2},{4,5},{5,4},{6,7},{7,6},{8,9},{9,8},{10,11... | collective-permute-start | bytes 884744 | tf_op jit(solution)/shard_map/ppermute | solution.py:32
  221.8 12.7 %collective-permute-start.7 = (bf16[144,1024]{1,0:T(8,128)(2,1)S(1)}, bf16[144,1024]{1,0:T(8,128)(2,1)S(1)}, u32[]{:S(2)}, u32[]{:S(2)}) collective-permute-start(bf16[144,1024]{1,0:T(8,128)(2,1)S(1)} %slice.170), channel_id=1, source_target_pairs={{0,1},{1,0},{2,3},{3,2},{4,5},{5,4},{6,7},{7,6},{8,9},{9,8},{10,11... | collective-permute-start | bytes 884744 | tf_op jit(solution)/shard_map/ppermute | solution.py:32
  234.9 9.6 %collective-permute-start.10 = (bf16[144,1024]{1,0:T(8,128)(2,1)S(1)}, bf16[144,1024]{1,0:T(8,128)(2,1)S(1)}, u32[]{:S(2)}, u32[]{:S(2)}) collective-permute-start(bf16[144,1024]{1,0:T(8,128)(2,1)S(1)} %get-tuple-element.5), channel_id=1, source_target_pairs={{0,1},{1,0},{2,3},{3,2},{4,5},{5,4},{6,7},{7,6},{8,9},{9,8},{10,11... | collective-permute-start | bytes 884744 | tf_op jit(solution)/shard_map/ppermute | solution.py:32
  238.0 12.7 %collective-permute-start.8 = (bf16[144,1024]{1,0:T(8,128)(2,1)S(1)}, bf16[144,1024]{1,0:T(8,128)(2,1)S(1)}, u32[]{:S(2)}, u32[]{:S(2)}) collective-permute-start(bf16[144,1024]{1,0:T(8,128)(2,1)S(1)} %get-tuple-element.6), channel_id=1, source_target_pairs={{0,1},{1,0},{2,3},{3,2},{4,5},{5,4},{6,7},{7,6},{8,9},{9,8},{10,11... | collective-permute-start | bytes 884744 | tf_op jit(solution)/shard_map/ppermute | solution.py:32
  244.5 10.3 %collective-permute-start.11 = (bf16[288,1024]{1,0:T(8,128)(2,1)S(1)}, bf16[288,1024]{1,0:T(8,128)(2,1)S(1)}, u32[]{:S(2)}, u32[]{:S(2)}) collective-permute-start(bf16[288,1024]{1,0:T(8,128)(2,1)S(1)} %pad_maximum_fusion.5), channel_id=1, source_target_pairs={{0,64},{1,65},{2,66},{3,67},{4,68},{5,69},{6,70},{7,71},{8,72},{9,... | collective-permute-start | bytes 1769480 | tf_op jit(solution)/shard_map/ppermute | solution.py:32
  250.8 6.5 %copy-start.2 = (bf16[144,896]{1,0:T(8,128)(2,1)S(1)}, bf16[144,896]{1,0:T(8,128)(2,1)}, u32[]{:S(2)}) copy-start(bf16[144,896]{1,0:T(8,128)(2,1)} %get-tuple-element.17) | copy-start | bytes 774148
  250.8 6.5 %copy-start.3 = (bf16[144,896]{1,0:T(8,128)(2,1)S(1)}, bf16[144,896]{1,0:T(8,128)(2,1)}, u32[]{:S(2)}) copy-start(bf16[144,896]{1,0:T(8,128)(2,1)} %get-tuple-element.18) | copy-start | bytes 774148
  250.8 5.6 %collective-permute-start.9 = (bf16[288,1024]{1,0:T(8,128)(2,1)S(1)}, bf16[288,1024]{1,0:T(8,128)(2,1)S(1)}, u32[]{:S(2)}, u32[]{:S(2)}) collective-permute-start(bf16[288,1024]{1,0:T(8,128)(2,1)S(1)} %pad_maximum_fusion.4), channel_id=1, source_target_pairs={{0,64},{1,65},{2,66},{3,67},{4,68},{5,69},{6,70},{7,71},{8,72},{9,... | collective-permute-start | bytes 1769480 | tf_op jit(solution)/shard_map/ppermute | solution.py:32
  256.4 0.8 copy-start.7
  261.1 1.1 copy-start.8
  265.6 16.5 %copy-start.9 = (s32[128,1]{0,1:T(1,128)S(1)}, s32[128,1]{0,1:T(1,128)}, u32[]{:S(2)}) copy-start(s32[128,1]{0,1:T(1,128)} %param.9) | copy-start | bytes 1540
  266.8 66.1 %all-to-all-start.1 = ((bf16[64,8,8,128]{3,2,1,0:T(8,128)(2,1)}), bf16[64,8,8,128]{3,2,1,0:T(8,128)(2,1)S(1)}, u32[]{:S(2)}, u32[]{:S(2)}) async-start(bf16[64,8,8,128]{3,2,1,0:T(8,128)(2,1)} %maximum_maximum_fusion), calls=%async_computation.1 | async-start | bytes 2097152 | tf_op jit(solution)/shard_map/all_to_all | solution.py:61
  333.0 12.1 %copy-start.4 = (f32[128,1]{0,1:T(1,128)S(1)}, f32[128,1]{0,1:T(1,128)}, u32[]{:S(2)}) copy-start(f32[128,1]{0,1:T(1,128)} %param.8) | copy-start | bytes 1540
  335.0 12.0 %collective-permute-start.13 = (bf16[112,2048]{1,0:T(8,128)(2,1)S(1)}, bf16[112,2048]{1,0:T(8,128)(2,1)S(1)}, u32[]{:S(2)}, u32[]{:S(2)}) collective-permute-start(bf16[112,2048]{1,0:T(8,128)(2,1)S(1)} %get-tuple-element.26), channel_id=1, source_target_pairs={{0,64},{1,65},{2,0},{3,1},{4,68},{5,69},{6,4},{7,5},{8,72},{9,73},... | collective-permute-start | bytes 1376264 | tf_op jit(solution)/shard_map/ppermute | solution.py:32
  340.0 24.0 %collective-permute-start.12 = (bf16[112,2048]{1,0:T(8,128)(2,1)S(1)}, bf16[112,2048]{1,0:T(8,128)(2,1)S(1)}, u32[]{:S(2)}, u32[]{:S(2)}) collective-permute-start(bf16[112,2048]{1,0:T(8,128)(2,1)S(1)} %get-tuple-element.25), channel_id=1, source_target_pairs={{0,0},{1,1},{2,64},{3,65},{4,4},{5,5},{6,68},{7,69},{8,8},{9,9},{1... | collective-permute-start | bytes 1376264 | tf_op jit(solution)/shard_map/ppermute | solution.py:32
Sparse Core Ops, SparseCore 0:
  135.4 35.7 all-gather.2
  173.9 36.3 all-gather.4
  261.2 49.7 reduce-scatter.1

commit v3 on v2

--- a/solution.py
+++ b/solution.py
@@ -3,8 +3,10 @@
 from jax import lax
 from jax.sharding import PartitionSpec as P
 
+
 SLICES = 4
 LANES = 128
+Z_BLOCKS = 4
 BOTH = ("rep", "exp")
 
 
@@ -48,13 +50,13 @@
     y_groups = [list(range(first, n_rep, 2)) for first in range(2)]
     token_groups = [
         [
-            (y * 2 + c) * n_dev + e * SLICES + h * 2 + b
+            (y * 2 + c) * n_dev + e * SLICES + (k ^ e % Z_BLOCKS // 2) * 2 + b
             for e in range(experts)
             for c in range(2)
             for b in range(2)
         ]
         for y in range(n_rep // 2)
-        for h in range(2)
+        for k in range(2)
     ]
 
     def routed(x):
@@ -119,7 +121,8 @@
         return jnp.concatenate([pair, other_core(pair)], axis=0)
 
     out_grad = (gates * cotangent.astype(f32)).astype(bf16)
-    got = routed(jnp.concatenate(packed_rows(tokens) + packed_rows(out_grad), axis=1))
+    sent = jnp.concatenate(packed_rows(tokens) + packed_rows(out_grad), axis=1)
+    got = routed(sent)
     x_rows = unpack(got[:, : tiles + 1])
     d_rows = unpack(got[:, tiles + 1 :])
 
@@ -147,7 +150,8 @@
     spare = jnp.where(own, packed[None], jnp.zeros((), bf16)).reshape(n_dev, 1, 1, LANES)
     spare = jnp.pad(spare, ((0, 0), (0, 0), (0, slots - tiles - 1), (0, 0)))
     extra = jnp.concatenate([extra, spare], axis=2)
-    back = routed(jnp.concatenate([main, extra], axis=1))
+    sent = jnp.concatenate([main, extra], axis=1)
+    back = routed(sent)
 
     down_term = contract(d_rows, h_all, ((0,), (0,))).astype(bf16)
     up_term = contract(x_rows, g_all, ((0,), (0,))).astype(bf16)
@@ -161,10 +165,10 @@
     part = terms.shape[0] // 2
     low, high = terms[:part], terms[part:]
     swap = far == 1
-    sums = moved(jnp.where(swap, high, low), n_rep, n_dev, lambda c, h, b: (h, c, b)).astype(f32)
-    sums = sums + moved(
-        jnp.where(swap, low, high), n_rep, n_dev, lambda c, h, b: (1 - h, c, b)
-    ).astype(f32)
+    first, second = jnp.where(swap, high, low), jnp.where(swap, low, high)
+    first = moved(first, n_rep, n_dev, lambda c, h, b: (h, c, b))
+    second = moved(second, n_rep, n_dev, lambda c, h, b: (1 - h, c, b))
+    sums = first.astype(f32) + second.astype(f32)
 
     main = back[:, :tiles].reshape(experts, SLICES, tiles, slots, LANES)
     main = main.transpose(0, 3, 1, 2, 4).reshape(experts * slots, model_width)

time: 373 us -> 358 us (0.960)
  waiting for transfers between devices: 242 us -> 226 us
    ppermute x14, waiting for transfers between devices: 140 us -> 118 us  [moved(): return lax.ppermute(x, BOTH, pairs)]
    all_gather x2, waiting for transfers between devices: 51.1 us -> 55.6 us  [weights(): lax.all_gather(pair, 'rep', axis=0, axis_index_groups=y_groups, tiled=True)]
    ppermute x14, starting transfers between devices: 44.3 us -> 48.7 us  [moved(): return lax.ppermute(x, BOTH, pairs)]
where the time goes in v3:
time: 358 us; the launch traced here: 357 us
  waiting for transfers between devices  226 us (63%)
  starting transfers between devices  81.2 us (23%)
  matrix products  18.3 us (5%)
  between operations  14.4 us (4%)
  other arithmetic  12.3 us (3%)
  local copies, waits for them, and re-layouts  5.41 us (2%)
    ppermute x14, waiting for transfers between devices, moved(): return lax.ppermute(x, BOTH, pairs)  118 us
    all_gather x2, waiting for transfers between devices, weights(): lax.all_gather(pair, 'rep', axis=0, axis_index_groups=y_groups, tiled=True)  55.6 us
    all_to_all x2, waiting for transfers between devices, routed(): lax.all_to_all(x, BOTH, split_axis=0, concat_axis=0, axis_index_groups=to...  51.7 us
    ppermute x14, starting transfers between devices, moved(): return lax.ppermute(x, BOTH, pairs)  48.7 us
    all_to_all x2, starting transfers between devices, routed(): lax.all_to_all(x, BOTH, split_axis=0, concat_axis=0, axis_index_groups=to...  32.4 us
    dot_general x10, matrix products, contract(): lax.dot_general(left, right, ((dims[0], dims[1]), ((), ())), preferred_el...  18.3 us
  transfers between devices with their start and end apart: 19, of which 12 were waited for; matrix products, arithmetic and copies ran while one was open for 6% of the time, Pallas kernels for 0%

profile of v3, /device:TPU:1, one launch (start us, length us, event | category | flops | bytes accessed | tf_op | source)
XLA Modules:
  0.0 357.3 jit_solution(11820869911304529665)
XLA Ops:
  7.2 0.9 convert_reduce_fusion
  8.8 1.7 convolution_convert_fusion
  11.5 1.6 pad_maximum_fusion.1
  13.1 18.7 %all-to-all-start = ((bf16[64,16,8,128]{3,2,1,0:T(8,128)(2,1)}), bf16[64,16,8,128]{3,2,1,0:T(8,128)(2,1)S(1)}, u32[]{:S(2)}, u32[]{:S(2)}) async-start(bf16[64,16,8,128]{3,2,1,0:T(8,128)(2,1)} %pad_maximum_fusion.1), calls=%async_computation | async-start | bytes 4194304 | tf_op jit(solution)/shard_map/all_to_all | solution.py:63
  31.8 2.4 collective-permute-start.1
  34.2 3.5 collective-permute-start
  37.7 29.5 %collective-permute-done.1 = bf16[112,1024]{1,0:T(8,128)(2,1)S(1)} collective-permute-done((bf16[112,1024]{1,0:T(8,128)(2,1)}, bf16[112,1024]{1,0:T(8,128)(2,1)S(1)}, u32[]{:S(2)}, u32[]{:S(2)}) %collective-permute-start.1) | collective-permute-done | bytes 229408 | tf_op jit(solution)/shard_map/ppermute | solution.py:34
  67.2 46.2 %collective-permute-done = bf16[112,1024]{1,0:T(8,128)(2,1)S(1)} collective-permute-done((bf16[112,1024]{1,0:T(8,128)(2,1)}, bf16[112,1024]{1,0:T(8,128)(2,1)S(1)}, u32[]{:S(2)}, u32[]{:S(2)}) %collective-permute-start) | collective-permute-done | bytes 229408 | tf_op jit(solution)/shard_map/ppermute | solution.py:34
  113.4 0.9 maximum_select_fusion
  114.4 3.9 %collective-permute-start.5 = (bf16[112,1024]{1,0:T(8,128)(2,1)}, bf16[112,1024]{1,0:T(8,128)(2,1)S(1)}, u32[]{:S(2)}, u32[]{:S(2)}) collective-permute-start(bf16[112,1024]{1,0:T(8,128)(2,1)} %param.10), channel_id=1, source_target_pairs={{0,2},{1,3},{2,66},{3,67},{4,6},{5,7},{6,70},{7,71},{8,10},{9,11},... | collective-permute-start | bytes 688136 | tf_op jit(solution)/shard_map/ppermute | solution.py:34
  118.3 5.0 %collective-permute-start.4 = (bf16[112,1024]{1,0:T(8,128)(2,1)}, bf16[112,1024]{1,0:T(8,128)(2,1)S(1)}, u32[]{:S(2)}, u32[]{:S(2)}) collective-permute-start(bf16[112,1024]{1,0:T(8,128)(2,1)} %param.10), channel_id=1, source_target_pairs={{0,0},{1,1},{2,64},{3,65},{4,4},{5,5},{6,68},{7,69},{8,8},{9,9},{1... | collective-permute-start | bytes 688136 | tf_op jit(solution)/shard_map/ppermute | solution.py:34
  123.3 8.2 %collective-permute-done.5 = bf16[112,1024]{1,0:T(8,128)(2,1)S(1)} collective-permute-done((bf16[112,1024]{1,0:T(8,128)(2,1)}, bf16[112,1024]{1,0:T(8,128)(2,1)S(1)}, u32[]{:S(2)}, u32[]{:S(2)}) %collective-permute-start.5) | collective-permute-done | bytes 229408 | tf_op jit(solution)/shard_map/ppermute | solution.py:34
  131.5 1.5 collective-permute-done.4
  132.9 0.9 maximum_select_fusion.1
  134.2 1.1 fusion.72
  135.4 23.5 %all-gather.3.cloned.1.call-done = bf16[896,1024]{1,0:T(8,128)(2,1)} async-done(((bf16[224,1024]{1,0:T(8,128)(2,1)}), bf16[896,1024]{1,0:T(8,128)(2,1)}) %all-gather.3.cloned.1.call-update) | async-done | bytes 1835024 | tf_op jit(solution)/shard_map/all_gather | solution.py:81
  158.9 3.2 convolution_convert_fusion.7
  162.1 2.7 collective-permute-start.2
  165.0 0.9 fusion.38
  165.9 32.0 %all-gather.5.cloned.1.call-done = bf16[896,1024]{1,0:T(8,128)(2,1)} async-done(((bf16[224,1024]{1,0:T(8,128)(2,1)}), bf16[896,1024]{1,0:T(8,128)(2,1)}) %all-gather.5.cloned.1.call-update) | async-done | bytes 1835024 | tf_op jit(solution)/shard_map/all_gather | solution.py:81
  197.9 2.7 convolution_convert_fusion.6
  200.6 2.7 collective-permute-start.6
  203.4 2.0 convolution_add_fusion.1
  205.4 3.2 collective-permute-start.3
  208.6 0.8 convolution_add_fusion
  209.4 2.1 collective-permute-start.7
  211.6 4.3 %collective-permute-done.3 = bf16[144,1024]{1,0:T(8,128)(2,1)S(1)} collective-permute-done((bf16[144,1024]{1,0:T(8,128)(2,1)S(1)}, bf16[144,1024]{1,0:T(8,128)(2,1)S(1)}, u32[]{:S(2)}, u32[]{:S(2)}) %collective-permute-start.3) | collective-permute-done | bytes 294944 | tf_op jit(solution)/shard_map/ppermute | solution.py:34
  215.9 6.3 %collective-permute-done.7 = bf16[144,1024]{1,0:T(8,128)(2,1)S(1)} collective-permute-done((bf16[144,1024]{1,0:T(8,128)(2,1)S(1)}, bf16[144,1024]{1,0:T(8,128)(2,1)S(1)}, u32[]{:S(2)}, u32[]{:S(2)}) %collective-permute-start.7) | collective-permute-done | bytes 294944 | tf_op jit(solution)/shard_map/ppermute | solution.py:34
  222.6 3.1 collective-permute-start.10
  225.7 2.1 collective-permute-start.8
  227.8 4.3 %collective-permute-done.10 = bf16[144,1024]{1,0:T(8,128)(2,1)S(1)} collective-permute-done((bf16[144,1024]{1,0:T(8,128)(2,1)S(1)}, bf16[144,1024]{1,0:T(8,128)(2,1)S(1)}, u32[]{:S(2)}, u32[]{:S(2)}) %collective-permute-start.10) | collective-permute-done | bytes 294944 | tf_op jit(solution)/shard_map/ppermute | solution.py:34
  232.2 4.9 %collective-permute-start.11 = (bf16[288,1024]{1,0:T(8,128)(2,1)S(1)}, bf16[288,1024]{1,0:T(8,128)(2,1)S(1)}, u32[]{:S(2)}, u32[]{:S(2)}) collective-permute-start(bf16[288,1024]{1,0:T(8,128)(2,1)S(1)} %pad_maximum_fusion.5), channel_id=1, source_target_pairs={{0,64},{1,65},{2,66},{3,67},{4,68},{5,69},{6,70},{7,71},{8,72},{9,... | collective-permute-start | bytes 1769480 | tf_op jit(solution)/shard_map/ppermute | solution.py:34
  237.1 1.3 collective-permute-done.8
  238.5 3.9 %collective-permute-start.9 = (bf16[288,1024]{1,0:T(8,128)(2,1)S(1)}, bf16[288,1024]{1,0:T(8,128)(2,1)S(1)}, u32[]{:S(2)}, u32[]{:S(2)}) collective-permute-start(bf16[288,1024]{1,0:T(8,128)(2,1)S(1)} %pad_maximum_fusion.4), channel_id=1, source_target_pairs={{0,64},{1,65},{2,66},{3,67},{4,68},{5,69},{6,70},{7,71},{8,72},{9,... | collective-permute-start | bytes 1769480 | tf_op jit(solution)/shard_map/ppermute | solution.py:34
  242.5 1.6 convolution_convert_fusion.3
  244.1 0.8 copy-done.7
  245.0 1.6 convolution_convert_fusion.4
  246.6 2.2 pad_maximum_fusion
  249.9 2.9 convolution_convert_fusion.5
  253.3 1.2 maximum_maximum_fusion
  254.5 13.7 %all-to-all-start.1 = ((bf16[64,8,8,128]{3,2,1,0:T(8,128)(2,1)}), bf16[64,8,8,128]{3,2,1,0:T(8,128)(2,1)S(1)}, u32[]{:S(2)}, u32[]{:S(2)}) async-start(bf16[64,8,8,128]{3,2,1,0:T(8,128)(2,1)} %maximum_maximum_fusion), calls=%async_computation.1 | async-start | bytes 2097152 | tf_op jit(solution)/shard_map/all_to_all | solution.py:63
  268.2 51.7 %all-to-all-done.1 = bf16[64,8,8,128]{3,2,1,0:T(8,128)(2,1)S(1)} async-done(((bf16[64,8,8,128]{3,2,1,0:T(8,128)(2,1)}), bf16[64,8,8,128]{3,2,1,0:T(8,128)(2,1)S(1)}, u32[]{:S(2)}, u32[]{:S(2)}) %all-to-all-start.1) | async-done | bytes 1048608 | tf_op jit(solution)/shard_map/all_to_all | solution.py:63
  320.7 1.2 broadcast_select_fusion.1
  321.9 3.7 %collective-permute-start.13 = (bf16[112,2048]{1,0:T(8,128)(2,1)S(1)}, bf16[112,2048]{1,0:T(8,128)(2,1)S(1)}, u32[]{:S(2)}, u32[]{:S(2)}) collective-permute-start(bf16[112,2048]{1,0:T(8,128)(2,1)S(1)} %get-tuple-element.26), channel_id=1, source_target_pairs={{0,64},{1,65},{2,0},{3,1},{4,68},{5,69},{6,4},{7,5},{8,72},{9,73},... | collective-permute-start | bytes 1376264 | tf_op jit(solution)/shard_map/ppermute | solution.py:34
  325.7 5.3 %collective-permute-start.12 = (bf16[112,2048]{1,0:T(8,128)(2,1)S(1)}, bf16[112,2048]{1,0:T(8,128)(2,1)S(1)}, u32[]{:S(2)}, u32[]{:S(2)}) collective-permute-start(bf16[112,2048]{1,0:T(8,128)(2,1)S(1)} %get-tuple-element.25), channel_id=1, source_target_pairs={{0,0},{1,1},{2,64},{3,65},{4,4},{5,5},{6,68},{7,69},{8,8},{9,9},{1... | collective-permute-start | bytes 1376264 | tf_op jit(solution)/shard_map/ppermute | solution.py:34
  331.5 1.4 convolution_convert_fusion.2
  332.9 16.8 %collective-permute-done.12 = bf16[112,2048]{1,0:T(8,128)(2,1)S(1)} collective-permute-done((bf16[112,2048]{1,0:T(8,128)(2,1)S(1)}, bf16[112,2048]{1,0:T(8,128)(2,1)S(1)}, u32[]{:S(2)}, u32[]{:S(2)}) %collective-permute-start.12) | collective-permute-done | bytes 458784 | tf_op jit(solution)/shard_map/ppermute | solution.py:34
  349.8 1.0 fusion.73
  (84 shorter events, 5.7 us)
Async XLA Ops:
  7.2 3.4 copy-start
  13.1 120.9 %all-to-all-start = ((bf16[64,16,8,128]{3,2,1,0:T(8,128)(2,1)}), bf16[64,16,8,128]{3,2,1,0:T(8,128)(2,1)S(1)}, u32[]{:S(2)}, u32[]{:S(2)}) async-start(bf16[64,16,8,128]{3,2,1,0:T(8,128)(2,1)} %pad_maximum_fusion.1), calls=%async_computation | async-start | bytes 4194304 | tf_op jit(solution)/shard_map/all_to_all | solution.py:63
  31.8 127.1 %all-gather.3.cloned.1.call-start = ((), (), s32[]{:S(2)}) async-start(), calls=%async_computation.3 | async-start | bytes 2293760 | tf_op jit(solution)/shard_map/all_gather | solution.py:81
  31.8 35.4 %collective-permute-start.1 = (bf16[112,1024]{1,0:T(8,128)(2,1)}, bf16[112,1024]{1,0:T(8,128)(2,1)S(1)}, u32[]{:S(2)}, u32[]{:S(2)}) collective-permute-start(bf16[112,1024]{1,0:T(8,128)(2,1)} %param.11), channel_id=1, source_target_pairs={{0,2},{1,3},{2,66},{3,67},{4,6},{5,7},{6,70},{7,71},{8,10},{9,11},... | collective-permute-start | bytes 688136 | tf_op jit(solution)/shard_map/ppermute | solution.py:34
  34.2 79.2 %collective-permute-start = (bf16[112,1024]{1,0:T(8,128)(2,1)}, bf16[112,1024]{1,0:T(8,128)(2,1)S(1)}, u32[]{:S(2)}, u32[]{:S(2)}) collective-permute-start(bf16[112,1024]{1,0:T(8,128)(2,1)} %param.11), channel_id=1, source_target_pairs={{0,0},{1,1},{2,64},{3,65},{4,4},{5,5},{6,68},{7,69},{8,8},{9,9},{1... | collective-permute-start | bytes 688136 | tf_op jit(solution)/shard_map/ppermute | solution.py:34
  114.3 83.6 %all-gather.5.cloned.1.call-start = ((), (), s32[]{:S(2)}) async-start(), calls=%async_computation.4 | async-start | bytes 2293760 | tf_op jit(solution)/shard_map/all_gather | solution.py:81
  114.4 17.1 %collective-permute-start.5 = (bf16[112,1024]{1,0:T(8,128)(2,1)}, bf16[112,1024]{1,0:T(8,128)(2,1)S(1)}, u32[]{:S(2)}, u32[]{:S(2)}) collective-permute-start(bf16[112,1024]{1,0:T(8,128)(2,1)} %param.10), channel_id=1, source_target_pairs={{0,2},{1,3},{2,66},{3,67},{4,6},{5,7},{6,70},{7,71},{8,10},{9,11},... | collective-permute-start | bytes 688136 | tf_op jit(solution)/shard_map/ppermute | solution.py:34
  118.3 14.6 %collective-permute-start.4 = (bf16[112,1024]{1,0:T(8,128)(2,1)}, bf16[112,1024]{1,0:T(8,128)(2,1)S(1)}, u32[]{:S(2)}, u32[]{:S(2)}) collective-permute-start(bf16[112,1024]{1,0:T(8,128)(2,1)} %param.10), channel_id=1, source_target_pairs={{0,0},{1,1},{2,64},{3,65},{4,4},{5,5},{6,68},{7,69},{8,8},{9,9},{1... | collective-permute-start | bytes 688136 | tf_op jit(solution)/shard_map/ppermute | solution.py:34
  133.8 186.9 %reduce-scatter.2.cloned.1.call-start = ((), (), s32[]{:S(2)}) async-start(), calls=%async_computation.5 | async-start | bytes 4587520 | tf_op jit(solution)/shard_map/reduce_scatter | solution.py:158
  158.9 6.1 %copy-start.1 = (bf16[64,7,8,128]{3,2,1,0:T(8,128)(2,1)S(1)}, bf16[64,7,8,128]{3,2,1,0:T(8,128)(2,1)}, u32[]{:S(2)}) copy-start(bf16[64,7,8,128]{3,2,1,0:T(8,128)(2,1)} %get-tuple-element.9) | copy-start | bytes 2752516
  162.1 41.3 %collective-permute-start.2 = (bf16[288,1024]{1,0:T(8,128)(2,1)}, bf16[288,1024]{1,0:T(8,128)(2,1)}, u32[]{:S(2)}, u32[]{:S(2)}) collective-permute-start(bf16[288,1024]{1,0:T(8,128)(2,1)} %convolution_convert_fusion.7), channel_id=1, source_target_pairs={{0,64},{1,65},{2,66},{3,67},{4,68},{5,69},{6,70},{7,71},{8,72},{9,... | collective-permute-start | bytes 1769480 | tf_op jit(solution)/shard_map/ppermute | solution.py:34
  197.9 5.4 %copy-start.6 = (bf16[896,1024]{1,0:T(8,128)(2,1)S(1)}, bf16[896,1024]{1,0:T(8,128)(2,1)}, u32[]{:S(2)}) copy-start(bf16[896,1024]{1,0:T(8,128)(2,1)} %all-gather.3.cloned.1.call-done) | copy-start | bytes 5505028
  200.6 8.0 %collective-permute-start.6 = (bf16[288,1024]{1,0:T(8,128)(2,1)S(1)}, bf16[288,1024]{1,0:T(8,128)(2,1)S(1)}, u32[]{:S(2)}, u32[]{:S(2)}) collective-permute-start(bf16[288,1024]{1,0:T(8,128)(2,1)S(1)} %convolution_convert_fusion.6), channel_id=1, source_target_pairs={{0,64},{1,65},{2,66},{3,67},{4,68},{5,69},{6,70},{7,71},{8,72},{9,... | collective-permute-start | bytes 1769480 | tf_op jit(solution)/shard_map/ppermute | solution.py:34
  203.4 5.2 %copy-start.5 = (bf16[896,1024]{1,0:T(8,128)(2,1)S(1)}, bf16[896,1024]{1,0:T(8,128)(2,1)}, u32[]{:S(2)}) copy-start(bf16[896,1024]{1,0:T(8,128)(2,1)} %all-gather.5.cloned.1.call-done) | copy-start | bytes 5505028
  205.4 10.5 %collective-permute-start.3 = (bf16[144,1024]{1,0:T(8,128)(2,1)S(1)}, bf16[144,1024]{1,0:T(8,128)(2,1)S(1)}, u32[]{:S(2)}, u32[]{:S(2)}) collective-permute-start(bf16[144,1024]{1,0:T(8,128)(2,1)S(1)} %slice.171), channel_id=1, source_target_pairs={{0,1},{1,0},{2,3},{3,2},{4,5},{5,4},{6,7},{7,6},{8,9},{9,8},{10,11... | collective-permute-start | bytes 884744 | tf_op jit(solution)/shard_map/ppermute | solution.py:34
  209.4 12.7 %collective-permute-start.7 = (bf16[144,1024]{1,0:T(8,128)(2,1)S(1)}, bf16[144,1024]{1,0:T(8,128)(2,1)S(1)}, u32[]{:S(2)}, u32[]{:S(2)}) collective-permute-start(bf16[144,1024]{1,0:T(8,128)(2,1)S(1)} %slice.170), channel_id=1, source_target_pairs={{0,1},{1,0},{2,3},{3,2},{4,5},{5,4},{6,7},{7,6},{8,9},{9,8},{10,11... | collective-permute-start | bytes 884744 | tf_op jit(solution)/shard_map/ppermute | solution.py:34
  222.6 9.6 %collective-permute-start.10 = (bf16[144,1024]{1,0:T(8,128)(2,1)S(1)}, bf16[144,1024]{1,0:T(8,128)(2,1)S(1)}, u32[]{:S(2)}, u32[]{:S(2)}) collective-permute-start(bf16[144,1024]{1,0:T(8,128)(2,1)S(1)} %get-tuple-element.5), channel_id=1, source_target_pairs={{0,1},{1,0},{2,3},{3,2},{4,5},{5,4},{6,7},{7,6},{8,9},{9,8},{10,11... | collective-permute-start | bytes 884744 | tf_op jit(solution)/shard_map/ppermute | solution.py:34
  225.7 12.8 %collective-permute-start.8 = (bf16[144,1024]{1,0:T(8,128)(2,1)S(1)}, bf16[144,1024]{1,0:T(8,128)(2,1)S(1)}, u32[]{:S(2)}, u32[]{:S(2)}) collective-permute-start(bf16[144,1024]{1,0:T(8,128)(2,1)S(1)} %get-tuple-element.6), channel_id=1, source_target_pairs={{0,1},{1,0},{2,3},{3,2},{4,5},{5,4},{6,7},{7,6},{8,9},{9,8},{10,11... | collective-permute-start | bytes 884744 | tf_op jit(solution)/shard_map/ppermute | solution.py:34
  232.2 10.3 %collective-permute-start.11 = (bf16[288,1024]{1,0:T(8,128)(2,1)S(1)}, bf16[288,1024]{1,0:T(8,128)(2,1)S(1)}, u32[]{:S(2)}, u32[]{:S(2)}) collective-permute-start(bf16[288,1024]{1,0:T(8,128)(2,1)S(1)} %pad_maximum_fusion.5), channel_id=1, source_target_pairs={{0,64},{1,65},{2,66},{3,67},{4,68},{5,69},{6,70},{7,71},{8,72},{9,... | collective-permute-start | bytes 1769480 | tf_op jit(solution)/shard_map/ppermute | solution.py:34
  238.5 6.5 %copy-start.2 = (bf16[144,896]{1,0:T(8,128)(2,1)S(1)}, bf16[144,896]{1,0:T(8,128)(2,1)}, u32[]{:S(2)}) copy-start(bf16[144,896]{1,0:T(8,128)(2,1)} %get-tuple-element.17) | copy-start | bytes 774148
  238.5 6.4 %copy-start.3 = (bf16[144,896]{1,0:T(8,128)(2,1)S(1)}, bf16[144,896]{1,0:T(8,128)(2,1)}, u32[]{:S(2)}) copy-start(bf16[144,896]{1,0:T(8,128)(2,1)} %get-tuple-element.18) | copy-start | bytes 774148
  238.5 5.6 %collective-permute-start.9 = (bf16[288,1024]{1,0:T(8,128)(2,1)S(1)}, bf16[288,1024]{1,0:T(8,128)(2,1)S(1)}, u32[]{:S(2)}, u32[]{:S(2)}) collective-permute-start(bf16[288,1024]{1,0:T(8,128)(2,1)S(1)} %pad_maximum_fusion.4), channel_id=1, source_target_pairs={{0,64},{1,65},{2,66},{3,67},{4,68},{5,69},{6,70},{7,71},{8,72},{9,... | collective-permute-start | bytes 1769480 | tf_op jit(solution)/shard_map/ppermute | solution.py:34
  244.1 0.8 copy-start.7
  248.8 1.1 copy-start.8
  253.3 14.9 %copy-start.9 = (s32[128,1]{0,1:T(1,128)S(1)}, s32[128,1]{0,1:T(1,128)}, u32[]{:S(2)}) copy-start(s32[128,1]{0,1:T(1,128)} %param.9) | copy-start | bytes 1540
  254.5 65.4 %all-to-all-start.1 = ((bf16[64,8,8,128]{3,2,1,0:T(8,128)(2,1)}), bf16[64,8,8,128]{3,2,1,0:T(8,128)(2,1)S(1)}, u32[]{:S(2)}, u32[]{:S(2)}) async-start(bf16[64,8,8,128]{3,2,1,0:T(8,128)(2,1)} %maximum_maximum_fusion), calls=%async_computation.1 | async-start | bytes 2097152 | tf_op jit(solution)/shard_map/all_to_all | solution.py:63
  320.0 11.0 %copy-start.4 = (f32[128,1]{0,1:T(1,128)S(1)}, f32[128,1]{0,1:T(1,128)}, u32[]{:S(2)}) copy-start(f32[128,1]{0,1:T(1,128)} %param.8) | copy-start | bytes 1540
  321.9 10.9 %collective-permute-start.13 = (bf16[112,2048]{1,0:T(8,128)(2,1)S(1)}, bf16[112,2048]{1,0:T(8,128)(2,1)S(1)}, u32[]{:S(2)}, u32[]{:S(2)}) collective-permute-start(bf16[112,2048]{1,0:T(8,128)(2,1)S(1)} %get-tuple-element.26), channel_id=1, source_target_pairs={{0,64},{1,65},{2,0},{3,1},{4,68},{5,69},{6,4},{7,5},{8,72},{9,73},... | collective-permute-start | bytes 1376264 | tf_op jit(solution)/shard_map/ppermute | solution.py:34
  325.7 24.0 %collective-permute-start.12 = (bf16[112,2048]{1,0:T(8,128)(2,1)S(1)}, bf16[112,2048]{1,0:T(8,128)(2,1)S(1)}, u32[]{:S(2)}, u32[]{:S(2)}) collective-permute-start(bf16[112,2048]{1,0:T(8,128)(2,1)S(1)} %get-tuple-element.25), channel_id=1, source_target_pairs={{0,0},{1,1},{2,64},{3,65},{4,4},{5,5},{6,68},{7,69},{8,8},{9,9},{1... | collective-permute-start | bytes 1376264 | tf_op jit(solution)/shard_map/ppermute | solution.py:34
Sparse Core Ops, SparseCore 0:
  114.4 44.3 all-gather.2
  161.5 36.3 all-gather.4
  248.9 49.6 reduce-scatter.1

commit v4 on v3

--- a/solution.py
+++ b/solution.py
@@ -24,12 +24,13 @@
     return first, second, third
 
 
-def moved(x, n_rep, n_exp, where):
+def moved(x, n_rep, n_exp, where, shift=0):
     pairs = []
     for rep in range(n_rep):
         for exp in range(n_exp):
             y, core, base, far, near = rep // 2, rep % 2, exp // 4 * 4, exp // 2 % 2, exp % 2
             core, far, near = where(core, far, near)
+            y = (y + shift) % (n_rep // 2)
             pairs.append((rep * n_exp + exp, (y * 2 + core) * n_exp + base + far * 2 + near))
     return lax.ppermute(x, BOTH, pairs)
 
@@ -43,11 +44,9 @@
     slots = 8
     quarter = n_dev // SLICES
     per_quarter = quarter * (slots + 1)
-    hidden = w_up.shape[1]
     bf16, f32 = jnp.bfloat16, jnp.float32
     core, far, near = lax.axis_index("rep") % 2, lax.axis_index("exp") // 2 % 2, lax.axis_index("exp") % 2
     me = core * 2 + near
-    y_groups = [list(range(first, n_rep, 2)) for first in range(2)]
     token_groups = [
         [
             (y * 2 + c) * n_dev + e * SLICES + (k ^ e % Z_BLOCKS // 2) * 2 + b
@@ -59,6 +58,52 @@
         for k in range(2)
     ]
 
+    y_now, y_size = lax.axis_index("rep") // 2, n_rep // 2
+
+    def ring(x, step):
+        return moved(x, n_rep, n_dev, lambda c, h, b: (c, h, b), step)
+
+    def gathered_weights(own_up, own_down):
+        own = jnp.concatenate([own_up, own_down], axis=0)
+        half = own_up.shape[0]
+        left, right = ring(own, 1), ring(own, -1)
+        far_up, far_down = ring(left[:half], 1), ring(right[half:], -1)
+
+        def placed(blocks):
+            twice = jnp.concatenate(blocks + blocks, axis=0)
+            start = (y_size - y_now) * half
+            return lax.dynamic_slice_in_dim(twice, start, y_size * half, axis=0)
+
+        return (
+            placed([own_up, right[:half], far_up, left[:half]]),
+            placed([own_down, right[half:], far_down, left[half:]]),
+        )
+
+    def replica_sum(term, shift):
+        rows_y, cols = term.shape[0] // y_size, term.shape[1] // 2
+
+        def block(step):
+            start = (y_now + shift + step + y_size) % y_size * rows_y
+            return lax.dynamic_slice_in_dim(term, start, rows_y, axis=0)
+
+        def plus(part, got):
+            return (part.astype(f32) + got.astype(f32)).astype(bf16)
+
+        across = block(2)
+        from_left = ring(across[:, :cols], 1)
+        from_right = ring(across[:, cols:], -1)
+        ahead, behind = block(1), block(3)
+        ahead = jnp.concatenate([plus(ahead[:, :cols], from_left), ahead[:, cols:]], axis=1)
+        behind = jnp.concatenate([behind[:, :cols], plus(behind[:, cols:], from_right)], axis=1)
+        from_left, from_right = ring(ahead, 1), ring(behind, -1)
+        total = block(0).astype(f32) + from_left.astype(f32) + from_right.astype(f32)
+        total = total.astype(bf16)
+        low, high = total[: rows_y // 2], total[rows_y // 2 :]
+        first, second = jnp.where(far == 1, high, low), jnp.where(far == 1, low, high)
+        first = moved(first, n_rep, n_dev, lambda c, h, b: (h, c, b), shift)
+        second = moved(second, n_rep, n_dev, lambda c, h, b: (1 - h, c, b), shift)
+        return first.astype(f32) + second.astype(f32)
+
     def routed(x):
         return lax.all_to_all(
             x, BOTH, split_axis=0, concat_axis=0, axis_index_groups=token_groups, tiled=True
@@ -70,18 +115,20 @@
     def other_near(x):
         return moved(x, n_rep, n_dev, lambda c, h, b: (c, h, 1 - b))
 
-    def weights(w):
-        first = moved(w, n_rep, n_dev, lambda c, h, b: (h, c, b))
-        second = moved(w, n_rep, n_dev, lambda c, h, b: (h, 1 - c, b))
-        pair = jnp.where(
-            far == 0,
-            jnp.concatenate([first, second], axis=0),
-            jnp.concatenate([second, first], axis=0),
+    both = jnp.concatenate([w_up, w_down_t], axis=0)
+    first = moved(both, n_rep, n_dev, lambda c, h, b: (h, c, b))
+    second = moved(both, n_rep, n_dev, lambda c, h, b: (h, 1 - c, b))
+    part = w_up.shape[0]
+
+    def paired(rows):
+        ones, twos = first[rows], second[rows]
+        return jnp.where(
+            far == 0, jnp.concatenate([ones, twos], axis=0), jnp.concatenate([twos, ones], axis=0)
         )
-        return lax.all_gather(pair, "rep", axis=0, axis_index_groups=y_groups, tiled=True)
-
-    up = weights(w_up)
-    down = weights(w_down_t)
+
+    own_up = paired(slice(0, part))
+    own_down = paired(slice(part, 2 * part))
+    up, down = gathered_weights(own_up, own_down)
 
     route = routes.reshape(-1)
     order = jnp.arange(tok_dev, dtype=jnp.int32)
@@ -113,11 +160,12 @@
         theirs = other_core(theirs)
         mine = contract(rows_in[: 2 * per_quarter], matrix, ((1,), (0,)))
         mine = mine + theirs.astype(f32)
-        passed = other_near(mine[per_quarter:].astype(bf16))
-        return mine[:per_quarter] + passed.astype(f32)
-
-    def gathered(block):
-        pair = jnp.concatenate([block, other_near(block)], axis=0)
+        ours = mine.astype(bf16)
+        passed = other_near(ours)
+        passed = jnp.concatenate([passed[per_quarter:], passed[:per_quarter]], axis=0)
+        return ours.astype(f32) + passed.astype(f32)
+
+    def gathered(pair):
         return jnp.concatenate([pair, other_core(pair)], axis=0)
 
     out_grad = (gates * cotangent.astype(f32)).astype(bf16)
@@ -130,9 +178,12 @@
     hidden_grad = reduced(d_rows, down)
     gating = jax.nn.sigmoid(activation)
     hidden_act = (activation * gating).astype(bf16)
+    hidden_act, activation = lax.optimization_barrier((hidden_act, activation))
+    gating = jax.nn.sigmoid(activation)
     h_all = gathered(hidden_act)
+    down_term = contract(d_rows, h_all, ((0,), (0,))).astype(bf16)
     act_grad = (hidden_grad * gating * (1.0 + activation * (1.0 - gating))).astype(bf16)
-    dots = jnp.sum(hidden_act.astype(f32) * hidden_grad, axis=1)
+    dots = jnp.sum((hidden_act.astype(f32) * hidden_grad)[:per_quarter], axis=1)
     g_all = gathered(act_grad)
 
     dx = contract(g_all, up, ((1,), (1,))).astype(bf16).reshape(SLICES, per_quarter, piece)
@@ -153,22 +204,9 @@
     sent = jnp.concatenate([main, extra], axis=1)
     back = routed(sent)
 
-    down_term = contract(d_rows, h_all, ((0,), (0,))).astype(bf16)
     up_term = contract(x_rows, g_all, ((0,), (0,))).astype(bf16)
-    terms = lax.psum_scatter(
-        jnp.concatenate([up_term, down_term], axis=1),
-        "rep",
-        scatter_dimension=0,
-        axis_index_groups=y_groups,
-        tiled=True,
-    )
-    part = terms.shape[0] // 2
-    low, high = terms[:part], terms[part:]
-    swap = far == 1
-    first, second = jnp.where(swap, high, low), jnp.where(swap, low, high)
-    first = moved(first, n_rep, n_dev, lambda c, h, b: (h, c, b))
-    second = moved(second, n_rep, n_dev, lambda c, h, b: (1 - h, c, b))
-    sums = first.astype(f32) + second.astype(f32)
+    grad_down_t = replica_sum(down_term, -1)
+    grad_up = replica_sum(up_term, 1)
 
     main = back[:, :tiles].reshape(experts, SLICES, tiles, slots, LANES)
     main = main.transpose(0, 3, 1, 2, 4).reshape(experts * slots, model_width)
@@ -180,7 +218,7 @@
     flat = jnp.concatenate([spare[:, :slots].reshape(-1), spare[:, slots]])
     hit = main_pos[:, None] == jnp.arange(rows, dtype=jnp.int32)[None, :]
     grad_gates = jnp.sum(jnp.where(hit, flat[None, :], 0.0), axis=1, keepdims=True) / gates
-    return grad_tokens, grad_gates, sums[:, :hidden], sums[:, hidden:]
+    return grad_tokens, grad_gates, grad_up, grad_down_t
 
 
 def solution(mesh):

time: 358 us -> 331 us (0.925)
  waiting for transfers between devices: 226 us -> 156 us
  starting transfers between devices: 81.2 us -> 118 us
  local copies, waits for them, and re-layouts: 5.41 us -> 20.3 us
  between operations: 14.4 us -> 1.91 us
    all_gather x2 -> x0, waiting for transfers between devices: 55.6 us -> none  [weights(): lax.all_gather(pair, 'rep', axis=0, axis_index_groups=y_groups, tiled=True)]
    all_to_all x2, waiting for transfers between devices: 51.7 us -> 0.01 us  [routed(): lax.all_to_all(x, BOTH, split_axis=0, concat_axis=0, axis_index_groups=to...]
    ppermute x14 -> x24, starting transfers between devices: 48.7 us -> 92.7 us  [moved(): return lax.ppermute(x, BOTH, pairs)]
    ppermute x14 -> x24, waiting for transfers between devices: 118 us -> 156 us  [moved(): return lax.ppermute(x, BOTH, pairs)]
    unnamed x20 -> x73, local copies, waits for them, and re-layouts: 1.14 us -> 13.1 us
    all_to_all x2, starting transfers between devices: 32.4 us -> 25 us  [routed(): lax.all_to_all(x, BOTH, split_axis=0, concat_axis=0, axis_index_groups=to...]
  transfers between devices with their start and end apart: 19 -> 26, of which waited for: 12 -> 10; matrix products, arithmetic and copies ran while one was open for 6% -> 9% of each run, Pallas kernels for 0% -> 0%
where the time goes in v4:
time: 331 us; the launch traced here: 330 us
  waiting for transfers between devices  156 us (47%)
  starting transfers between devices  118 us (36%)
  local copies, waits for them, and re-layouts  20.3 us (6%)
  matrix products  19.3 us (6%)
  other arithmetic  14.3 us (4%)
    ppermute x24, waiting for transfers between devices, moved(): return lax.ppermute(x, BOTH, pairs)  156 us
    ppermute x24, starting transfers between devices, moved(): return lax.ppermute(x, BOTH, pairs)  92.7 us
    all_to_all x2, starting transfers between devices, routed(): lax.all_to_all(x, BOTH, split_axis=0, concat_axis=0, axis_index_groups=to...  25 us
    dot_general x10, matrix products, contract(): lax.dot_general(left, right, ((dims[0], dims[1]), ((), ())), preferred_el...  19.3 us
    unnamed x73, local copies, waits for them, and re-layouts  13.1 us
  transfers between devices with their start and end apart: 26, of which 10 were waited for; matrix products, arithmetic and copies ran while one was open for 9% of the time, Pallas kernels for 0%

profile of v4, /device:TPU:1, one launch (start us, length us, event | category | flops | bytes accessed | tf_op | source)
XLA Modules:
  0.0 329.5 jit_solution(17560605045497922906)
XLA Ops:
  2.2 1.7 convolution_convert_fusion
  4.9 1.6 pad_maximum_fusion
  6.6 18.8 %all-to-all-start = ((bf16[64,16,8,128]{3,2,1,0:T(8,128)(2,1)}), bf16[64,16,8,128]{3,2,1,0:T(8,128)(2,1)S(1)}, u32[]{:S(2)}, u32[]{:S(2)}) async-start(bf16[64,16,8,128]{3,2,1,0:T(8,128)(2,1)} %pad_maximum_fusion), calls=%async_computation | async-start | bytes 4194304 | tf_op jit(solution)/shard_map/all_to_all | solution.py:108
  26.8 3.9 %collective-permute-start = (bf16[224,1024]{1,0:T(8,128)(2,1)}, bf16[224,1024]{1,0:T(8,128)(2,1)}, u32[]{:S(2)}, u32[]{:S(2)}) collective-permute-start(bf16[224,1024]{1,0:T(8,128)(2,1)} %constant_dynamic-update-slice_fusion), channel_id=1, source_target_pairs={{0,0},{1,1},{2,64},{3,65},{4,4},{5,5},{6,68},{7,69},{8,8},{9,9},{1... | collective-permute-start | bytes 1376264 | tf_op jit(solution)/shard_map/ppermute | solution.py:35
  30.7 3.5 %collective-permute-start.1 = (bf16[224,1024]{1,0:T(8,128)(2,1)}, bf16[224,1024]{1,0:T(8,128)(2,1)S(1)}, u32[]{:S(2)}, u32[]{:S(2)}) collective-permute-start(bf16[224,1024]{1,0:T(8,128)(2,1)} %constant_dynamic-update-slice_fusion), channel_id=1, source_target_pairs={{0,2},{1,3},{2,66},{3,67},{4,6},{5,7},{6,70},{7,71},{8,10},{9,11},... | collective-permute-start | bytes 1376264 | tf_op jit(solution)/shard_map/ppermute | solution.py:35
  34.3 82.1 %collective-permute-done = bf16[224,1024]{1,0:T(8,128)(2,1)} collective-permute-done((bf16[224,1024]{1,0:T(8,128)(2,1)}, bf16[224,1024]{1,0:T(8,128)(2,1)}, u32[]{:S(2)}, u32[]{:S(2)}) %collective-permute-start) | collective-permute-done | bytes 458784 | tf_op jit(solution)/shard_map/ppermute | solution.py:35
  118.7 3.2 collective-permute-start.4
  121.9 3.4 %collective-permute-start.2 = (bf16[448,1024]{1,0:T(8,128)(2,1)S(1)}, bf16[448,1024]{1,0:T(8,128)(2,1)S(1)}, u32[]{:S(2)}, u32[]{:S(2)}) collective-permute-start(bf16[448,1024]{1,0:T(8,128)(2,1)S(1)} %pad_maximum_fusion.3), channel_id=1, source_target_pairs={{0,384},{1,385},{2,386},{3,387},{4,388},{5,389},{6,390},{7,391},{8... | collective-permute-start | bytes 2752520 | tf_op jit(solution)/shard_map/ppermute | solution.py:35
  125.3 18.0 %collective-permute-done.4 = bf16[448,1024]{1,0:T(8,128)(2,1)S(1)} collective-permute-done((bf16[448,1024]{1,0:T(8,128)(2,1)S(1)}, bf16[448,1024]{1,0:T(8,128)(2,1)S(1)}, u32[]{:S(2)}, u32[]{:S(2)}) %collective-permute-start.4) | collective-permute-done | bytes 917536 | tf_op jit(solution)/shard_map/ppermute | solution.py:35
  143.3 1.9 collective-permute-start.7
  145.3 11.8 %collective-permute-done.7 = bf16[224,1024]{1,0:T(8,128)(2,1)S(1)} collective-permute-done((bf16[224,1024]{1,0:T(8,128)(2,1)S(1)}, bf16[224,1024]{1,0:T(8,128)(2,1)S(1)}, u32[]{:S(2)}, u32[]{:S(2)}) %collective-permute-start.7) | collective-permute-done | bytes 458784 | tf_op jit(solution)/shard_map/ppermute | solution.py:35
  159.0 1.8 copy-done.25
  160.8 2.0 collective-permute-start.3
  162.9 1.9 constant_dynamic-update-slice_fusion.9
  164.8 8.1 %collective-permute-done.3 = bf16[224,1024]{1,0:T(8,128)(2,1)} collective-permute-done((bf16[224,1024]{1,0:T(8,128)(2,1)}, bf16[224,1024]{1,0:T(8,128)(2,1)}, u32[]{:S(2)}, u32[]{:S(2)}) %collective-permute-start.3) | collective-permute-done | bytes 458784 | tf_op jit(solution)/shard_map/ppermute | solution.py:35
  172.9 1.8 constant_dynamic-update-slice_fusion.5
  177.4 1.8 constant_dynamic-update-slice_fusion.2
  182.2 1.6 fusion.11
  183.8 5.0 %collective-permute-start.8 = (bf16[288,1024]{1,0:T(8,128)(2,1)}, bf16[288,1024]{1,0:T(8,128)(2,1)}, u32[]{:S(2)}, u32[]{:S(2)}) collective-permute-start(bf16[288,1024]{1,0:T(8,128)(2,1)} %fusion.11), channel_id=1, source_target_pairs={{0,64},{1,65},{2,66},{3,67},{4,68},{5,69},{6,70},{7,71},{8,72},{9,... | collective-permute-start | bytes 1769480 | tf_op jit(solution)/shard_map/ppermute | solution.py:35
  189.9 2.7 fusion.20
  192.6 1.9 collective-permute-start.5
  194.6 2.9 fusion.14
  197.4 1.9 collective-permute-start.9
  200.2 3.4 %collective-permute-start.6 = (bf16[288,1024]{1,0:T(8,128)(2,1)S(1)}, bf16[288,1024]{1,0:T(8,128)(2,1)S(1)}, u32[]{:S(2)}, u32[]{:S(2)}) collective-permute-start(bf16[288,1024]{1,0:T(8,128)(2,1)S(1)} %fusion.17), channel_id=1, source_target_pairs={{0,1},{1,0},{2,3},{3,2},{4,5},{5,4},{6,7},{7,6},{8,9},{9,8},{10,11... | collective-permute-start | bytes 1769480 | tf_op jit(solution)/shard_map/ppermute | solution.py:35
  203.8 10.1 %collective-permute-done.9 = bf16[288,1024]{1,0:T(8,128)(2,1)S(1)} collective-permute-done((bf16[288,1024]{1,0:T(8,128)(2,1)}, bf16[288,1024]{1,0:T(8,128)(2,1)S(1)}, u32[]{:S(2)}, u32[]{:S(2)}) %collective-permute-start.9) | collective-permute-done | bytes 589856 | tf_op jit(solution)/shard_map/ppermute | solution.py:35
  215.4 11.2 %collective-permute-done.6 = bf16[288,1024]{1,0:T(8,128)(2,1)S(1)} collective-permute-done((bf16[288,1024]{1,0:T(8,128)(2,1)S(1)}, bf16[288,1024]{1,0:T(8,128)(2,1)S(1)}, u32[]{:S(2)}, u32[]{:S(2)}) %collective-permute-start.6) | collective-permute-done | bytes 589856 | tf_op jit(solution)/shard_map/ppermute | solution.py:35
  228.2 3.3 collective-permute-start.10
  233.1 3.1 convolution_convert_fusion.5
  236.8 2.0 maximum_maximum_fusion
  238.8 6.2 %all-to-all-start.1 = ((bf16[64,8,8,128]{3,2,1,0:T(8,128)(2,1)}), bf16[64,8,8,128]{3,2,1,0:T(8,128)(2,1)S(1)}, u32[]{:S(2)}, u32[]{:S(2)}) async-start(bf16[64,8,8,128]{3,2,1,0:T(8,128)(2,1)} %maximum_maximum_fusion), calls=%async_computation.1 | async-start | bytes 2097152 | tf_op jit(solution)/shard_map/all_to_all | solution.py:108
  245.1 2.4 collective-permute-start.17
  247.6 3.1 convolution_convert_fusion.4
  250.8 1.9 collective-permute-start.11
  252.7 4.6 %collective-permute-start.13 = (bf16[224,512]{1,0:T(8,128)(2,1)S(1)}, bf16[224,512]{1,0:T(8,128)(2,1)S(1)}, u32[]{:S(2)}, u32[]{:S(2)}) collective-permute-start(bf16[224,512]{1,0:T(8,128)(2,1)S(1)} %get-tuple-element.26), channel_id=1, source_target_pairs={{0,384},{1,385},{2,386},{3,387},{4,388},{5,389},{6,390},{7,391},{8... | collective-permute-start | bytes 688136 | tf_op jit(solution)/shard_map/ppermute | solution.py:35
  257.4 1.6 convolution_convert_fusion.3
  259.1 1.9 collective-permute-start.18
  261.0 4.6 %collective-permute-start.20 = (bf16[224,512]{1,0:T(8,128)(2,1)S(1)}, bf16[224,512]{1,0:T(8,128)(2,1)S(1)}, u32[]{:S(2)}, u32[]{:S(2)}) collective-permute-start(bf16[224,512]{1,0:T(8,128)(2,1)S(1)} %get-tuple-element.20), channel_id=1, source_target_pairs={{0,384},{1,385},{2,386},{3,387},{4,388},{5,389},{6,390},{7,391},{8... | collective-permute-start | bytes 688136 | tf_op jit(solution)/shard_map/ppermute | solution.py:35
  265.9 1.9 collective-permute-start.14
  267.8 3.4 %collective-permute-start.12 = (bf16[224,1024]{1,0:T(8,128)(2,1)S(1)}, bf16[224,1024]{1,0:T(8,128)(2,1)S(1)}, u32[]{:S(2)}, u32[]{:S(2)}) collective-permute-start(bf16[224,1024]{1,0:T(8,128)(2,1)S(1)} %pad_maximum_fusion.6), channel_id=1, source_target_pairs={{0,128},{1,129},{2,130},{3,131},{4,132},{5,133},{6,134},{7,135},{8... | collective-permute-start | bytes 1376264 | tf_op jit(solution)/shard_map/ppermute | solution.py:35
  271.4 3.8 %collective-permute-start.21 = (bf16[224,1024]{1,0:T(8,128)(2,1)S(1)}, bf16[224,1024]{1,0:T(8,128)(2,1)S(1)}, u32[]{:S(2)}, u32[]{:S(2)}) collective-permute-start(bf16[224,1024]{1,0:T(8,128)(2,1)S(1)} %pad_maximum_fusion.9), channel_id=1, source_target_pairs={{0,384},{1,385},{2,386},{3,387},{4,388},{5,389},{6,390},{7,391},{8... | collective-permute-start | bytes 1376264 | tf_op jit(solution)/shard_map/ppermute | solution.py:35
  275.3 1.9 collective-permute-start.19
  277.2 2.3 collective-permute-done.14
  279.5 2.4 collective-permute-done.12
  282.1 13.9 %collective-permute-start.16 = (bf16[112,1024]{1,0:T(8,128)(2,1)S(1)}, bf16[112,1024]{1,0:T(8,128)(2,1)S(1)}, u32[]{:S(2)}, u32[]{:S(2)}) collective-permute-start(bf16[112,1024]{1,0:T(8,128)(2,1)S(1)} %get-tuple-element.56), channel_id=1, source_target_pairs={{0,192},{1,193},{2,128},{3,129},{4,196},{5,197},{6,132},{7,133},{8... | collective-permute-start | bytes 688136 | tf_op jit(solution)/shard_map/ppermute | solution.py:35
  296.1 6.0 %collective-permute-start.15 = (bf16[112,1024]{1,0:T(8,128)(2,1)S(1)}, bf16[112,1024]{1,0:T(8,128)(2,1)S(1)}, u32[]{:S(2)}, u32[]{:S(2)}) collective-permute-start(bf16[112,1024]{1,0:T(8,128)(2,1)S(1)} %get-tuple-element.55), channel_id=1, source_target_pairs={{0,128},{1,129},{2,192},{3,193},{4,132},{5,133},{6,196},{7,197},{8... | collective-permute-start | bytes 688136 | tf_op jit(solution)/shard_map/ppermute | solution.py:35
  302.5 5.2 %collective-permute-start.23 = (bf16[112,1024]{1,0:T(8,128)(2,1)S(1)}, bf16[112,1024]{1,0:T(8,128)(2,1)S(1)}, u32[]{:S(2)}, u32[]{:S(2)}) collective-permute-start(bf16[112,1024]{1,0:T(8,128)(2,1)S(1)} %get-tuple-element.54), channel_id=1, source_target_pairs={{0,448},{1,449},{2,384},{3,385},{4,452},{5,453},{6,388},{7,389},{8... | collective-permute-start | bytes 688136 | tf_op jit(solution)/shard_map/ppermute | solution.py:35
  307.7 7.9 %collective-permute-start.22 = (bf16[112,1024]{1,0:T(8,128)(2,1)S(1)}, bf16[112,1024]{1,0:T(8,128)(2,1)S(1)}, u32[]{:S(2)}, u32[]{:S(2)}) collective-permute-start(bf16[112,1024]{1,0:T(8,128)(2,1)S(1)} %get-tuple-element.53), channel_id=1, source_target_pairs={{0,384},{1,385},{2,448},{3,449},{4,388},{5,389},{6,452},{7,453},{8... | collective-permute-start | bytes 688136 | tf_op jit(solution)/shard_map/ppermute | solution.py:35
  316.5 9.5 %collective-permute-done.22 = bf16[112,1024]{1,0:T(8,128)(2,1)S(1)} collective-permute-done((bf16[112,1024]{1,0:T(8,128)(2,1)S(1)}, bf16[112,1024]{1,0:T(8,128)(2,1)S(1)}, u32[]{:S(2)}, u32[]{:S(2)}) %collective-permute-start.22) | collective-permute-done | bytes 229408 | tf_op jit(solution)/shard_map/ppermute | solution.py:35
  (164 shorter events, 26.5 us)
Async XLA Ops:
  6.6 18.9 %copy-start.22 = (bf16[112,1024]{1,0:T(8,128)(2,1)S(1)}, bf16[112,1024]{1,0:T(8,128)(2,1)}, u32[]{:S(2)}) copy-start(bf16[112,1024]{1,0:T(8,128)(2,1)} %param.10) | copy-start | bytes 688132
  6.6 19.6 %copy-start.23 = (bf16[112,1024]{1,0:T(8,128)(2,1)S(1)}, bf16[112,1024]{1,0:T(8,128)(2,1)}, u32[]{:S(2)}) copy-start(bf16[112,1024]{1,0:T(8,128)(2,1)} %param.11) | copy-start | bytes 688132
  6.6 172.6 %all-to-all-start = ((bf16[64,16,8,128]{3,2,1,0:T(8,128)(2,1)}), bf16[64,16,8,128]{3,2,1,0:T(8,128)(2,1)S(1)}, u32[]{:S(2)}, u32[]{:S(2)}) async-start(bf16[64,16,8,128]{3,2,1,0:T(8,128)(2,1)} %pad_maximum_fusion), calls=%async_computation | async-start | bytes 4194304 | tf_op jit(solution)/shard_map/all_to_all | solution.py:108
  26.8 89.6 %collective-permute-start = (bf16[224,1024]{1,0:T(8,128)(2,1)}, bf16[224,1024]{1,0:T(8,128)(2,1)}, u32[]{:S(2)}, u32[]{:S(2)}) collective-permute-start(bf16[224,1024]{1,0:T(8,128)(2,1)} %constant_dynamic-update-slice_fusion), channel_id=1, source_target_pairs={{0,0},{1,1},{2,64},{3,65},{4,4},{5,5},{6,68},{7,69},{8,8},{9,9},{1... | collective-permute-start | bytes 1376264 | tf_op jit(solution)/shard_map/ppermute | solution.py:35
  30.7 86.8 %collective-permute-start.1 = (bf16[224,1024]{1,0:T(8,128)(2,1)}, bf16[224,1024]{1,0:T(8,128)(2,1)S(1)}, u32[]{:S(2)}, u32[]{:S(2)}) collective-permute-start(bf16[224,1024]{1,0:T(8,128)(2,1)} %constant_dynamic-update-slice_fusion), channel_id=1, source_target_pairs={{0,2},{1,3},{2,66},{3,67},{4,6},{5,7},{6,70},{7,71},{8,10},{9,11},... | collective-permute-start | bytes 1376264 | tf_op jit(solution)/shard_map/ppermute | solution.py:35
  118.7 24.6 %collective-permute-start.4 = (bf16[448,1024]{1,0:T(8,128)(2,1)S(1)}, bf16[448,1024]{1,0:T(8,128)(2,1)S(1)}, u32[]{:S(2)}, u32[]{:S(2)}) collective-permute-start(bf16[448,1024]{1,0:T(8,128)(2,1)S(1)} %pad_maximum_fusion.3), channel_id=1, source_target_pairs={{0,128},{1,129},{2,130},{3,131},{4,132},{5,133},{6,134},{7,135},{8... | collective-permute-start | bytes 2752520 | tf_op jit(solution)/shard_map/ppermute | solution.py:35
  121.9 23.4 %collective-permute-start.2 = (bf16[448,1024]{1,0:T(8,128)(2,1)S(1)}, bf16[448,1024]{1,0:T(8,128)(2,1)S(1)}, u32[]{:S(2)}, u32[]{:S(2)}) collective-permute-start(bf16[448,1024]{1,0:T(8,128)(2,1)S(1)} %pad_maximum_fusion.3), channel_id=1, source_target_pairs={{0,384},{1,385},{2,386},{3,387},{4,388},{5,389},{6,390},{7,391},{8... | collective-permute-start | bytes 2752520 | tf_op jit(solution)/shard_map/ppermute | solution.py:35
  143.3 14.0 %copy-start.1 = (bf16[448,1024]{1,0:T(8,128)(2,1)}, bf16[448,1024]{1,0:T(8,128)(2,1)S(1)}, u32[]{:S(2)}) copy-start(bf16[448,1024]{1,0:T(8,128)(2,1)S(1)} %collective-permute-done.4) | copy-start | bytes 2752516
  143.3 13.8 %collective-permute-start.7 = (bf16[224,1024]{1,0:T(8,128)(2,1)S(1)}, bf16[224,1024]{1,0:T(8,128)(2,1)S(1)}, u32[]{:S(2)}, u32[]{:S(2)}) collective-permute-start(bf16[224,1024]{1,0:T(8,128)(2,1)S(1)} %slice.229), channel_id=1, source_target_pairs={{0,128},{1,129},{2,130},{3,131},{4,132},{5,133},{6,134},{7,135},{8... | collective-permute-start | bytes 1376264 | tf_op jit(solution)/shard_map/ppermute | solution.py:35
  145.3 13.7 %copy-start.5 = (bf16[448,1024]{1,0:T(8,128)(2,1)}, bf16[448,1024]{1,0:T(8,128)(2,1)S(1)}, u32[]{:S(2)}) copy-start(bf16[448,1024]{1,0:T(8,128)(2,1)S(1)} %collective-permute-done.2) | copy-start | bytes 2752516
  160.8 12.1 %collective-permute-start.3 = (bf16[224,1024]{1,0:T(8,128)(2,1)}, bf16[224,1024]{1,0:T(8,128)(2,1)}, u32[]{:S(2)}, u32[]{:S(2)}) collective-permute-start(bf16[224,1024]{1,0:T(8,128)(2,1)} %get-tuple-element.48), channel_id=1, source_target_pairs={{0,384},{1,385},{2,386},{3,387},{4,388},{5,389},{6,390},{7,391},{8... | collective-permute-start | bytes 1376264 | tf_op jit(solution)/shard_map/ppermute | solution.py:35
  162.9 11.9 %copy-start.2 = (bf16[448,1024]{1,0:T(8,128)(2,1)S(1)}, bf16[448,1024]{1,0:T(8,128)(2,1)}, u32[]{:S(2)}) copy-start(bf16[448,1024]{1,0:T(8,128)(2,1)} %copy-done.1) | copy-start | bytes 2752516
  164.8 11.8 %copy-start.6 = (bf16[448,1024]{1,0:T(8,128)(2,1)S(1)}, bf16[448,1024]{1,0:T(8,128)(2,1)}, u32[]{:S(2)}) copy-start(bf16[448,1024]{1,0:T(8,128)(2,1)} %copy-done.5) | copy-start | bytes 2752516
  180.7 13.8 %copy-start.17 = (bf16[144,896]{1,0:T(8,128)(2,1)}, bf16[144,896]{1,0:T(8,128)(2,1)S(1)}, u32[]{:S(2)}) copy-start(bf16[144,896]{1,0:T(8,128)(2,1)S(1)} %get-tuple-element.36) | copy-start | bytes 774148
  180.7 16.7 %copy-start.19 = (bf16[144,896]{1,0:T(8,128)(2,1)}, bf16[144,896]{1,0:T(8,128)(2,1)S(1)}, u32[]{:S(2)}) copy-start(bf16[144,896]{1,0:T(8,128)(2,1)S(1)} %get-tuple-element.37) | copy-start | bytes 774148
  182.2 6.6 %copy-start.3 = (bf16[448,1024]{1,0:T(8,128)(2,1)S(1)}, bf16[448,1024]{1,0:T(8,128)(2,1)}, u32[]{:S(2)}) copy-start(bf16[448,1024]{1,0:T(8,128)(2,1)} %copy-done.1) | copy-start | bytes 2752516
  182.2 7.6 %copy-start.4 = (bf16[64,7,8,128]{3,2,1,0:T(8,128)(2,1)S(1)}, bf16[64,7,8,128]{3,2,1,0:T(8,128)(2,1)}, u32[]{:S(2)}) copy-start(bf16[64,7,8,128]{3,2,1,0:T(8,128)(2,1)} %get-tuple-element.15) | copy-start | bytes 2752516
  183.8 10.7 %collective-permute-start.8 = (bf16[288,1024]{1,0:T(8,128)(2,1)}, bf16[288,1024]{1,0:T(8,128)(2,1)}, u32[]{:S(2)}, u32[]{:S(2)}) collective-permute-start(bf16[288,1024]{1,0:T(8,128)(2,1)} %fusion.11), channel_id=1, source_target_pairs={{0,64},{1,65},{2,66},{3,67},{4,68},{5,69},{6,70},{7,71},{8,72},{9,... | collective-permute-start | bytes 1769480 | tf_op jit(solution)/shard_map/ppermute | solution.py:35
  189.9 9.5 %copy-start.9 = (bf16[144,896]{1,0:T(8,128)(2,1)}, bf16[144,896]{1,0:T(8,128)(2,1)S(1)}, u32[]{:S(2)}) copy-start(bf16[144,896]{1,0:T(8,128)(2,1)S(1)} %get-tuple-element.40) | copy-start | bytes 774148
  189.9 9.5 %copy-start.11 = (bf16[144,896]{1,0:T(8,128)(2,1)}, bf16[144,896]{1,0:T(8,128)(2,1)S(1)}, u32[]{:S(2)}) copy-start(bf16[144,896]{1,0:T(8,128)(2,1)S(1)} %get-tuple-element.41) | copy-start | bytes 774148
  189.9 4.7 %copy-start.27 = (bf16[1792,1024]{1,0:T(8,128)(2,1)S(1)}, bf16[1792,1024]{1,0:T(8,128)(2,1)}, u32[]{:S(2)}) copy-start(bf16[1792,1024]{1,0:T(8,128)(2,1)} %get-tuple-element.44) | copy-start | bytes 11010052
  192.6 6.7 %collective-permute-start.5 = (bf16[288,1024]{1,0:T(8,128)(2,1)S(1)}, bf16[288,1024]{1,0:T(8,128)(2,1)S(1)}, u32[]{:S(2)}, u32[]{:S(2)}) collective-permute-start(bf16[288,1024]{1,0:T(8,128)(2,1)S(1)} %fusion.20), channel_id=1, source_target_pairs={{0,64},{1,65},{2,66},{3,67},{4,68},{5,69},{6,70},{7,71},{8,72},{9,... | collective-permute-start | bytes 1769480 | tf_op jit(solution)/shard_map/ppermute | solution.py:35
  194.6 4.8 %copy-start.24 = (bf16[1792,1024]{1,0:T(8,128)(2,1)S(1)}, bf16[1792,1024]{1,0:T(8,128)(2,1)}, u32[]{:S(2)}) copy-start(bf16[1792,1024]{1,0:T(8,128)(2,1)} %slice_dynamic-update-slice_fusion.3) | copy-start | bytes 11010052
  197.4 16.5 %collective-permute-start.9 = (bf16[288,1024]{1,0:T(8,128)(2,1)}, bf16[288,1024]{1,0:T(8,128)(2,1)S(1)}, u32[]{:S(2)}, u32[]{:S(2)}) collective-permute-start(bf16[288,1024]{1,0:T(8,128)(2,1)} %fusion.14), channel_id=1, source_target_pairs={{0,1},{1,0},{2,3},{3,2},{4,5},{5,4},{6,7},{7,6},{8,9},{9,8},{10,11... | collective-permute-start | bytes 1769480 | tf_op jit(solution)/shard_map/ppermute | solution.py:35
  200.2 15.2 %copy-start.8 = (bf16[288,1024]{1,0:T(8,128)(2,1)}, bf16[288,1024]{1,0:T(8,128)(2,1)S(1)}, u32[]{:S(2)}) copy-start(bf16[288,1024]{1,0:T(8,128)(2,1)S(1)} %fusion.17) | copy-start | bytes 1769476
  200.2 26.3 %collective-permute-start.6 = (bf16[288,1024]{1,0:T(8,128)(2,1)S(1)}, bf16[288,1024]{1,0:T(8,128)(2,1)S(1)}, u32[]{:S(2)}, u32[]{:S(2)}) collective-permute-start(bf16[288,1024]{1,0:T(8,128)(2,1)S(1)} %fusion.17), channel_id=1, source_target_pairs={{0,1},{1,0},{2,3},{3,2},{4,5},{5,4},{6,7},{7,6},{8,9},{9,8},{10,11... | collective-permute-start | bytes 1769480 | tf_op jit(solution)/shard_map/ppermute | solution.py:35
  228.2 4.9 %collective-permute-start.10 = (bf16[288,1024]{1,0:T(8,128)(2,1)S(1)}, bf16[288,1024]{1,0:T(8,128)(2,1)S(1)}, u32[]{:S(2)}, u32[]{:S(2)}) collective-permute-start(bf16[288,1024]{1,0:T(8,128)(2,1)S(1)} %get-tuple-element.28), channel_id=1, source_target_pairs={{0,64},{1,65},{2,66},{3,67},{4,68},{5,69},{6,70},{7,71},{8,72},{9,... | collective-permute-start | bytes 1769480 | tf_op jit(solution)/shard_map/ppermute | solution.py:35
  236.7 10.7 %copy-start.30 = (s32[128,1]{0,1:T(1,128)S(1)}, s32[128,1]{0,1:T(1,128)}, u32[]{:S(2)}) copy-start(s32[128,1]{0,1:T(1,128)} %param.9) | copy-start | bytes 1540
  236.8 10.7 %copy-start.18 = (bf16[144,896]{1,0:T(8,128)(2,1)S(1)}, bf16[144,896]{1,0:T(8,128)(2,1)}, u32[]{:S(2)}) copy-start(bf16[144,896]{1,0:T(8,128)(2,1)} %copy-done.17) | copy-start | bytes 774148
  238.8 88.1 %all-to-all-start.1 = ((bf16[64,8,8,128]{3,2,1,0:T(8,128)(2,1)}), bf16[64,8,8,128]{3,2,1,0:T(8,128)(2,1)S(1)}, u32[]{:S(2)}, u32[]{:S(2)}) async-start(bf16[64,8,8,128]{3,2,1,0:T(8,128)(2,1)} %maximum_maximum_fusion), calls=%async_computation.1 | async-start | bytes 2097152 | tf_op jit(solution)/shard_map/all_to_all | solution.py:108
  245.1 12.2 %collective-permute-start.17 = (bf16[288,1024]{1,0:T(8,128)(2,1)S(1)}, bf16[288,1024]{1,0:T(8,128)(2,1)S(1)}, u32[]{:S(2)}, u32[]{:S(2)}) collective-permute-start(bf16[288,1024]{1,0:T(8,128)(2,1)S(1)} %get-tuple-element.7), channel_id=1, source_target_pairs={{0,64},{1,65},{2,66},{3,67},{4,68},{5,69},{6,70},{7,71},{8,72},{9,... | collective-permute-start | bytes 1769480 | tf_op jit(solution)/shard_map/ppermute | solution.py:35
  247.5 9.8 %copy-start.10 = (bf16[144,896]{1,0:T(8,128)(2,1)S(1)}, bf16[144,896]{1,0:T(8,128)(2,1)}, u32[]{:S(2)}) copy-start(bf16[144,896]{1,0:T(8,128)(2,1)} %copy-done.9) | copy-start | bytes 774148
  247.5 9.8 %copy-start.12 = (bf16[144,896]{1,0:T(8,128)(2,1)S(1)}, bf16[144,896]{1,0:T(8,128)(2,1)}, u32[]{:S(2)}) copy-start(bf16[144,896]{1,0:T(8,128)(2,1)} %copy-done.11) | copy-start | bytes 774148
  247.5 9.8 %copy-start.14 = (bf16[144,896]{1,0:T(8,128)(2,1)S(1)}, bf16[144,896]{1,0:T(8,128)(2,1)}, u32[]{:S(2)}) copy-start(bf16[144,896]{1,0:T(8,128)(2,1)} %copy-done.13) | copy-start | bytes 774148
  247.5 9.8 %copy-start.16 = (bf16[144,896]{1,0:T(8,128)(2,1)S(1)}, bf16[144,896]{1,0:T(8,128)(2,1)}, u32[]{:S(2)}) copy-start(bf16[144,896]{1,0:T(8,128)(2,1)} %copy-done.15) | copy-start | bytes 774148
  250.8 14.8 %collective-permute-start.11 = (bf16[224,512]{1,0:T(8,128)(2,1)S(1)}, bf16[224,512]{1,0:T(8,128)(2,1)S(1)}, u32[]{:S(2)}, u32[]{:S(2)}) collective-permute-start(bf16[224,512]{1,0:T(8,128)(2,1)S(1)} %get-tuple-element.24), channel_id=1, source_target_pairs={{0,128},{1,129},{2,130},{3,131},{4,132},{5,133},{6,134},{7,135},{8... | collective-permute-start | bytes 688136 | tf_op jit(solution)/shard_map/ppermute | solution.py:35
  252.7 12.9 %collective-permute-start.13 = (bf16[224,512]{1,0:T(8,128)(2,1)S(1)}, bf16[224,512]{1,0:T(8,128)(2,1)S(1)}, u32[]{:S(2)}, u32[]{:S(2)}) collective-permute-start(bf16[224,512]{1,0:T(8,128)(2,1)S(1)} %get-tuple-element.26), channel_id=1, source_target_pairs={{0,384},{1,385},{2,386},{3,387},{4,388},{5,389},{6,390},{7,391},{8... | collective-permute-start | bytes 688136 | tf_op jit(solution)/shard_map/ppermute | solution.py:35
  259.1 12.1 %collective-permute-start.18 = (bf16[224,512]{1,0:T(8,128)(2,1)S(1)}, bf16[224,512]{1,0:T(8,128)(2,1)S(1)}, u32[]{:S(2)}, u32[]{:S(2)}) collective-permute-start(bf16[224,512]{1,0:T(8,128)(2,1)S(1)} %get-tuple-element.18), channel_id=1, source_target_pairs={{0,128},{1,129},{2,130},{3,131},{4,132},{5,133},{6,134},{7,135},{8... | collective-permute-start | bytes 688136 | tf_op jit(solution)/shard_map/ppermute | solution.py:35
  261.0 10.2 %collective-permute-start.20 = (bf16[224,512]{1,0:T(8,128)(2,1)S(1)}, bf16[224,512]{1,0:T(8,128)(2,1)S(1)}, u32[]{:S(2)}, u32[]{:S(2)}) collective-permute-start(bf16[224,512]{1,0:T(8,128)(2,1)S(1)} %get-tuple-element.20), channel_id=1, source_target_pairs={{0,384},{1,385},{2,386},{3,387},{4,388},{5,389},{6,390},{7,391},{8... | collective-permute-start | bytes 688136 | tf_op jit(solution)/shard_map/ppermute | solution.py:35
  265.9 13.6 %collective-permute-start.14 = (bf16[224,1024]{1,0:T(8,128)(2,1)S(1)}, bf16[224,1024]{1,0:T(8,128)(2,1)S(1)}, u32[]{:S(2)}, u32[]{:S(2)}) collective-permute-start(bf16[224,1024]{1,0:T(8,128)(2,1)S(1)} %pad_maximum_fusion.7), channel_id=1, source_target_pairs={{0,384},{1,385},{2,386},{3,387},{4,388},{5,389},{6,390},{7,391},{8... | collective-permute-start | bytes 1376264 | tf_op jit(solution)/shard_map/ppermute | solution.py:35
  267.8 14.0 %collective-permute-start.12 = (bf16[224,1024]{1,0:T(8,128)(2,1)S(1)}, bf16[224,1024]{1,0:T(8,128)(2,1)S(1)}, u32[]{:S(2)}, u32[]{:S(2)}) collective-permute-start(bf16[224,1024]{1,0:T(8,128)(2,1)S(1)} %pad_maximum_fusion.6), channel_id=1, source_target_pairs={{0,128},{1,129},{2,130},{3,131},{4,132},{5,133},{6,134},{7,135},{8... | collective-permute-start | bytes 1376264 | tf_op jit(solution)/shard_map/ppermute | solution.py:35
  271.4 30.7 %collective-permute-start.21 = (bf16[224,1024]{1,0:T(8,128)(2,1)S(1)}, bf16[224,1024]{1,0:T(8,128)(2,1)S(1)}, u32[]{:S(2)}, u32[]{:S(2)}) collective-permute-start(bf16[224,1024]{1,0:T(8,128)(2,1)S(1)} %pad_maximum_fusion.9), channel_id=1, source_target_pairs={{0,384},{1,385},{2,386},{3,387},{4,388},{5,389},{6,390},{7,391},{8... | collective-permute-start | bytes 1376264 | tf_op jit(solution)/shard_map/ppermute | solution.py:35
  275.3 26.9 %collective-permute-start.19 = (bf16[224,1024]{1,0:T(8,128)(2,1)S(1)}, bf16[224,1024]{1,0:T(8,128)(2,1)S(1)}, u32[]{:S(2)}, u32[]{:S(2)}) collective-permute-start(bf16[224,1024]{1,0:T(8,128)(2,1)S(1)} %pad_maximum_fusion.8), channel_id=1, source_target_pairs={{0,128},{1,129},{2,130},{3,131},{4,132},{5,133},{6,134},{7,135},{8... | collective-permute-start | bytes 1376264 | tf_op jit(solution)/shard_map/ppermute | solution.py:35
  282.1 33.5 %collective-permute-start.16 = (bf16[112,1024]{1,0:T(8,128)(2,1)S(1)}, bf16[112,1024]{1,0:T(8,128)(2,1)S(1)}, u32[]{:S(2)}, u32[]{:S(2)}) collective-permute-start(bf16[112,1024]{1,0:T(8,128)(2,1)S(1)} %get-tuple-element.56), channel_id=1, source_target_pairs={{0,192},{1,193},{2,128},{3,129},{4,196},{5,197},{6,132},{7,133},{8... | collective-permute-start | bytes 688136 | tf_op jit(solution)/shard_map/ppermute | solution.py:35
  296.1 19.6 %collective-permute-start.15 = (bf16[112,1024]{1,0:T(8,128)(2,1)S(1)}, bf16[112,1024]{1,0:T(8,128)(2,1)S(1)}, u32[]{:S(2)}, u32[]{:S(2)}) collective-permute-start(bf16[112,1024]{1,0:T(8,128)(2,1)S(1)} %get-tuple-element.55), channel_id=1, source_target_pairs={{0,128},{1,129},{2,192},{3,193},{4,132},{5,133},{6,196},{7,197},{8... | collective-permute-start | bytes 688136 | tf_op jit(solution)/shard_map/ppermute | solution.py:35
  302.4 25.1 %copy-start.28 = (f32[128,1]{0,1:T(1,128)S(1)}, f32[128,1]{0,1:T(1,128)}, u32[]{:S(2)}) copy-start(f32[128,1]{0,1:T(1,128)} %param.8) | copy-start | bytes 1540
  302.5 14.0 %collective-permute-start.23 = (bf16[112,1024]{1,0:T(8,128)(2,1)S(1)}, bf16[112,1024]{1,0:T(8,128)(2,1)S(1)}, u32[]{:S(2)}, u32[]{:S(2)}) collective-permute-start(bf16[112,1024]{1,0:T(8,128)(2,1)S(1)} %get-tuple-element.54), channel_id=1, source_target_pairs={{0,448},{1,449},{2,384},{3,385},{4,452},{5,453},{6,388},{7,389},{8... | collective-permute-start | bytes 688136 | tf_op jit(solution)/shard_map/ppermute | solution.py:35
  307.7 18.3 %collective-permute-start.22 = (bf16[112,1024]{1,0:T(8,128)(2,1)S(1)}, bf16[112,1024]{1,0:T(8,128)(2,1)S(1)}, u32[]{:S(2)}, u32[]{:S(2)}) collective-permute-start(bf16[112,1024]{1,0:T(8,128)(2,1)S(1)} %get-tuple-element.53), channel_id=1, source_target_pairs={{0,384},{1,385},{2,448},{3,449},{4,388},{5,389},{6,452},{7,453},{8... | collective-permute-start | bytes 688136 | tf_op jit(solution)/shard_map/ppermute | solution.py:35
  (9 other events, 23.6 us)

commit v5 on v4

--- a/solution.py
+++ b/solution.py
@@ -44,6 +44,7 @@
     slots = 8
     quarter = n_dev // SLICES
     per_quarter = quarter * (slots + 1)
+    hidden = w_up.shape[1]
     bf16, f32 = jnp.bfloat16, jnp.float32
     core, far, near = lax.axis_index("rep") % 2, lax.axis_index("exp") // 2 % 2, lax.axis_index("exp") % 2
     me = core * 2 + near
@@ -79,29 +80,27 @@
             placed([own_down, right[half:], far_down, left[half:]]),
         )
 
-    def replica_sum(term, shift):
-        rows_y, cols = term.shape[0] // y_size, term.shape[1] // 2
-
-        def block(step):
-            start = (y_now + shift + step + y_size) % y_size * rows_y
-            return lax.dynamic_slice_in_dim(term, start, rows_y, axis=0)
-
-        def plus(part, got):
-            return (part.astype(f32) + got.astype(f32)).astype(bf16)
-
-        across = block(2)
-        from_left = ring(across[:, :cols], 1)
-        from_right = ring(across[:, cols:], -1)
-        ahead, behind = block(1), block(3)
-        ahead = jnp.concatenate([plus(ahead[:, :cols], from_left), ahead[:, cols:]], axis=1)
-        behind = jnp.concatenate([behind[:, :cols], plus(behind[:, cols:], from_right)], axis=1)
+    def y_block(term, step):
+        rows_y = term.shape[0] // y_size
+        start = (y_now + 1 + step) % y_size * rows_y
+        return lax.dynamic_slice_in_dim(term, start, rows_y, axis=0)
+
+    def plus(part, got):
+        return (part.astype(f32) + got.astype(f32)).astype(bf16)
+
+    def replica_sum(up_term, down_term, got_up, got_down):
+        ahead = jnp.concatenate([plus(y_block(up_term, 1), got_up), y_block(down_term, 1)], axis=1)
+        behind = jnp.concatenate(
+            [y_block(up_term, 3), plus(y_block(down_term, 3), got_down)], axis=1
+        )
         from_left, from_right = ring(ahead, 1), ring(behind, -1)
-        total = block(0).astype(f32) + from_left.astype(f32) + from_right.astype(f32)
-        total = total.astype(bf16)
-        low, high = total[: rows_y // 2], total[rows_y // 2 :]
+        total = jnp.concatenate([y_block(up_term, 0), y_block(down_term, 0)], axis=1).astype(f32)
+        total = (total + from_left.astype(f32) + from_right.astype(f32)).astype(bf16)
+        half = total.shape[0] // 2
+        low, high = total[:half], total[half:]
         first, second = jnp.where(far == 1, high, low), jnp.where(far == 1, low, high)
-        first = moved(first, n_rep, n_dev, lambda c, h, b: (h, c, b), shift)
-        second = moved(second, n_rep, n_dev, lambda c, h, b: (1 - h, c, b), shift)
+        first = moved(first, n_rep, n_dev, lambda c, h, b: (h, c, b), 1)
+        second = moved(second, n_rep, n_dev, lambda c, h, b: (1 - h, c, b), 1)
         return first.astype(f32) + second.astype(f32)
 
     def routed(x):
@@ -159,8 +158,7 @@
         theirs = contract(rows_in[2 * per_quarter :], matrix, ((1,), (0,))).astype(bf16)
         theirs = other_core(theirs)
         mine = contract(rows_in[: 2 * per_quarter], matrix, ((1,), (0,)))
-        mine = mine + theirs.astype(f32)
-        ours = mine.astype(bf16)
+        ours = (mine + theirs.astype(f32)).astype(bf16)
         passed = other_near(ours)
         passed = jnp.concatenate([passed[per_quarter:], passed[:per_quarter]], axis=0)
         return ours.astype(f32) + passed.astype(f32)
@@ -182,6 +180,7 @@
     gating = jax.nn.sigmoid(activation)
     h_all = gathered(hidden_act)
     down_term = contract(d_rows, h_all, ((0,), (0,))).astype(bf16)
+    got_down = ring(y_block(down_term, 2), -1)
     act_grad = (hidden_grad * gating * (1.0 + activation * (1.0 - gating))).astype(bf16)
     dots = jnp.sum((hidden_act.astype(f32) * hidden_grad)[:per_quarter], axis=1)
     g_all = gathered(act_grad)
@@ -205,8 +204,8 @@
     back = routed(sent)
 
     up_term = contract(x_rows, g_all, ((0,), (0,))).astype(bf16)
-    grad_down_t = replica_sum(down_term, -1)
-    grad_up = replica_sum(up_term, 1)
+    got_up = ring(y_block(up_term, 2), 1)
+    sums = replica_sum(up_term, down_term, got_up, got_down)
 
     main = back[:, :tiles].reshape(experts, SLICES, tiles, slots, LANES)
     main = main.transpose(0, 3, 1, 2, 4).reshape(experts * slots, model_width)
@@ -218,7 +217,7 @@
     flat = jnp.concatenate([spare[:, :slots].reshape(-1), spare[:, slots]])
     hit = main_pos[:, None] == jnp.arange(rows, dtype=jnp.int32)[None, :]
     grad_gates = jnp.sum(jnp.where(hit, flat[None, :], 0.0), axis=1, keepdims=True) / gates
-    return grad_tokens, grad_gates, grad_up, grad_down_t
+    return grad_tokens, grad_gates, sums[:, :hidden], sums[:, hidden:]
 
 
 def solution(mesh):

time: 331 us -> 333 us (level); the launches traced: 330 us -> 327 us
  starting transfers between devices: 118 us -> 92.7 us
  waiting for transfers between devices: 156 us -> 176 us
  local copies, waits for them, and re-layouts: 20.3 us -> 23.8 us
    ppermute x24 -> x18, starting transfers between devices: 92.7 us -> 56.8 us  [moved(): return lax.ppermute(x, BOTH, pairs)]
    ppermute x24 -> x18, waiting for transfers between devices: 156 us -> 176 us  [moved(): return lax.ppermute(x, BOTH, pairs)]
    all_to_all x2, starting transfers between devices: 25 us -> 36 us  [routed(): lax.all_to_all(x, BOTH, split_axis=0, concat_axis=0, axis_index_groups=to...]
    unnamed x73 -> x75, local copies, waits for them, and re-layouts: 13.1 us -> 13.9 us
  transfers between devices with their start and end apart: 26 -> 20, of which waited for: 10 -> 11; matrix products, arithmetic and copies ran while one was open for 9% -> 12% of each run, Pallas kernels for 0% -> 0%
where the time goes in v5:
time: 333 us; the launch traced here: 327 us
  waiting for transfers between devices  176 us (53%)
  starting transfers between devices  92.7 us (28%)
  local copies, waits for them, and re-layouts  23.8 us (7%)
  matrix products  16.9 us (5%)
  other arithmetic  15.4 us (5%)
    ppermute x18, waiting for transfers between devices, moved(): return lax.ppermute(x, BOTH, pairs)  176 us
    ppermute x18, starting transfers between devices, moved(): return lax.ppermute(x, BOTH, pairs)  56.8 us
    all_to_all x2, starting transfers between devices, routed(): lax.all_to_all(x, BOTH, split_axis=0, concat_axis=0, axis_index_groups=to...  36 us
    dot_general x10, matrix products, contract(): lax.dot_general(left, right, ((dims[0], dims[1]), ((), ())), preferred_el...  16.9 us
    unnamed x75, local copies, waits for them, and re-layouts  13.9 us
  transfers between devices with their start and end apart: 20, of which 11 were waited for; matrix products, arithmetic and copies ran while one was open for 12% of the time, Pallas kernels for 0%

profile of v5, /device:TPU:1, one launch (start us, length us, event | category | flops | bytes accessed | tf_op | source)
XLA Modules:
  0.0 326.9 jit_solution(16921528254266917896)
XLA Ops:
  3.8 1.7 pad_maximum_fusion
  5.5 18.8 %all-to-all-start = ((bf16[64,16,8,128]{3,2,1,0:T(8,128)(2,1)}), bf16[64,16,8,128]{3,2,1,0:T(8,128)(2,1)S(1)}, u32[]{:S(2)}, u32[]{:S(2)}) async-start(bf16[64,16,8,128]{3,2,1,0:T(8,128)(2,1)} %pad_maximum_fusion), calls=%async_computation | async-start | bytes 4194304 | tf_op jit(solution)/shard_map/all_to_all | solution.py:107
  25.8 2.4 collective-permute-start.1
  28.1 3.5 %collective-permute-start = (bf16[224,1024]{1,0:T(8,128)(2,1)}, bf16[224,1024]{1,0:T(8,128)(2,1)S(1)}, u32[]{:S(2)}, u32[]{:S(2)}) collective-permute-start(bf16[224,1024]{1,0:T(8,128)(2,1)} %constant_dynamic-update-slice_fusion), channel_id=1, source_target_pairs={{0,0},{1,1},{2,64},{3,65},{4,4},{5,5},{6,68},{7,69},{8,8},{9,9},{1... | collective-permute-start | bytes 1376264 | tf_op jit(solution)/shard_map/ppermute | solution.py:35
  31.6 50.9 %collective-permute-done.1 = bf16[224,1024]{1,0:T(8,128)(2,1)} collective-permute-done((bf16[224,1024]{1,0:T(8,128)(2,1)}, bf16[224,1024]{1,0:T(8,128)(2,1)}, u32[]{:S(2)}, u32[]{:S(2)}) %collective-permute-start.1) | collective-permute-done | bytes 458784 | tf_op jit(solution)/shard_map/ppermute | solution.py:35
  83.7 31.7 %collective-permute-done = bf16[224,1024]{1,0:T(8,128)(2,1)S(1)} collective-permute-done((bf16[224,1024]{1,0:T(8,128)(2,1)}, bf16[224,1024]{1,0:T(8,128)(2,1)S(1)}, u32[]{:S(2)}, u32[]{:S(2)}) %collective-permute-start) | collective-permute-done | bytes 458784 | tf_op jit(solution)/shard_map/ppermute | solution.py:35
  116.5 3.2 collective-permute-start.4
  119.7 3.4 %collective-permute-start.2 = (bf16[448,1024]{1,0:T(8,128)(2,1)S(1)}, bf16[448,1024]{1,0:T(8,128)(2,1)S(1)}, u32[]{:S(2)}, u32[]{:S(2)}) collective-permute-start(bf16[448,1024]{1,0:T(8,128)(2,1)S(1)} %pad_maximum_fusion.3), channel_id=1, source_target_pairs={{0,384},{1,385},{2,386},{3,387},{4,388},{5,389},{6,390},{7,391},{8... | collective-permute-start | bytes 2752520 | tf_op jit(solution)/shard_map/ppermute | solution.py:35
  123.1 15.8 %collective-permute-done.4 = bf16[448,1024]{1,0:T(8,128)(2,1)S(1)} collective-permute-done((bf16[448,1024]{1,0:T(8,128)(2,1)S(1)}, bf16[448,1024]{1,0:T(8,128)(2,1)S(1)}, u32[]{:S(2)}, u32[]{:S(2)}) %collective-permute-start.4) | collective-permute-done | bytes 917536 | tf_op jit(solution)/shard_map/ppermute | solution.py:35
  138.9 1.9 collective-permute-start.7
  140.9 9.7 %collective-permute-done.7 = bf16[224,1024]{1,0:T(8,128)(2,1)S(1)} collective-permute-done((bf16[224,1024]{1,0:T(8,128)(2,1)S(1)}, bf16[224,1024]{1,0:T(8,128)(2,1)S(1)}, u32[]{:S(2)}, u32[]{:S(2)}) %collective-permute-start.7) | collective-permute-done | bytes 458784 | tf_op jit(solution)/shard_map/ppermute | solution.py:35
  152.4 1.8 copy-done.24
  154.2 2.0 collective-permute-start.3
  156.3 1.9 constant_dynamic-update-slice_fusion.9
  158.2 5.9 %collective-permute-done.3 = bf16[224,1024]{1,0:T(8,128)(2,1)} collective-permute-done((bf16[224,1024]{1,0:T(8,128)(2,1)}, bf16[224,1024]{1,0:T(8,128)(2,1)}, u32[]{:S(2)}, u32[]{:S(2)}) %collective-permute-start.3) | collective-permute-done | bytes 458784 | tf_op jit(solution)/shard_map/ppermute | solution.py:35
  164.1 1.8 constant_dynamic-update-slice_fusion.5
  168.5 1.8 constant_dynamic-update-slice_fusion.2
  171.9 1.4 copy-done.25
  173.3 1.6 fusion.11
  175.0 7.2 %collective-permute-start.8 = (bf16[288,1024]{1,0:T(8,128)(2,1)}, bf16[288,1024]{1,0:T(8,128)(2,1)}, u32[]{:S(2)}, u32[]{:S(2)}) collective-permute-start(bf16[288,1024]{1,0:T(8,128)(2,1)} %fusion.11), channel_id=1, source_target_pairs={{0,64},{1,65},{2,66},{3,67},{4,68},{5,69},{6,70},{7,71},{8,72},{9,... | collective-permute-start | bytes 1769480 | tf_op jit(solution)/shard_map/ppermute | solution.py:35
  183.3 2.7 fusion.20
  186.0 1.9 collective-permute-start.5
  188.0 2.0 fusion.14
  190.0 1.9 collective-permute-start.9
  192.8 3.4 %collective-permute-start.6 = (bf16[288,1024]{1,0:T(8,128)(2,1)S(1)}, bf16[288,1024]{1,0:T(8,128)(2,1)S(1)}, u32[]{:S(2)}, u32[]{:S(2)}) collective-permute-start(bf16[288,1024]{1,0:T(8,128)(2,1)S(1)} %fusion.17), channel_id=1, source_target_pairs={{0,1},{1,0},{2,3},{3,2},{4,5},{5,4},{6,7},{7,6},{8,9},{9,8},{10,11... | collective-permute-start | bytes 1769480 | tf_op jit(solution)/shard_map/ppermute | solution.py:35
  196.4 9.9 %collective-permute-done.9 = bf16[288,1024]{1,0:T(8,128)(2,1)S(1)} collective-permute-done((bf16[288,1024]{1,0:T(8,128)(2,1)S(1)}, bf16[288,1024]{1,0:T(8,128)(2,1)S(1)}, u32[]{:S(2)}, u32[]{:S(2)}) %collective-permute-start.9) | collective-permute-done | bytes 589856 | tf_op jit(solution)/shard_map/ppermute | solution.py:35
  206.4 1.4 convert_add_fusion
  207.8 11.2 %collective-permute-done.6 = bf16[288,1024]{1,0:T(8,128)(2,1)S(1)} collective-permute-done((bf16[288,1024]{1,0:T(8,128)(2,1)S(1)}, bf16[288,1024]{1,0:T(8,128)(2,1)S(1)}, u32[]{:S(2)}, u32[]{:S(2)}) %collective-permute-start.6) | collective-permute-done | bytes 589856 | tf_op jit(solution)/shard_map/ppermute | solution.py:35
  219.5 3.3 collective-permute-start.10
  222.8 1.9 collective-permute-start.11
  226.3 2.9 convolution_convert_fusion.4
  230.1 2.1 collective-permute-start.12
  232.2 1.4 convolution_convert_fusion.5
  235.7 1.2 maximum_maximum_fusion
  236.9 17.1 %all-to-all-start.1 = ((bf16[64,8,8,128]{3,2,1,0:T(8,128)(2,1)}), bf16[64,8,8,128]{3,2,1,0:T(8,128)(2,1)S(1)}, u32[]{:S(2)}, u32[]{:S(2)}) async-start(bf16[64,8,8,128]{3,2,1,0:T(8,128)(2,1)} %maximum_maximum_fusion), calls=%async_computation.1 | async-start | bytes 2097152 | tf_op jit(solution)/shard_map/all_to_all | solution.py:107
  254.0 3.1 convolution_convert_fusion.3
  257.3 4.9 %collective-permute-start.14 = (bf16[224,1024]{1,0:T(8,128)(2,1)S(1)}, bf16[224,1024]{1,0:T(8,128)(2,1)S(1)}, u32[]{:S(2)}, u32[]{:S(2)}) collective-permute-start(bf16[224,1024]{1,0:T(8,128)(2,1)S(1)} %get-tuple-element.20), channel_id=1, source_target_pairs={{0,384},{1,385},{2,386},{3,387},{4,388},{5,389},{6,390},{7,391},{8... | collective-permute-start | bytes 1376264 | tf_op jit(solution)/shard_map/ppermute | solution.py:35
  262.2 1.3 add_convert_fusion.2
  264.5 1.9 collective-permute-start.13
  266.4 5.1 %collective-permute-done.14 = bf16[224,1024]{1,0:T(8,128)(2,1)S(1)} collective-permute-done((bf16[224,1024]{1,0:T(8,128)(2,1)S(1)}, bf16[224,1024]{1,0:T(8,128)(2,1)S(1)}, u32[]{:S(2)}, u32[]{:S(2)}) %collective-permute-start.14) | collective-permute-done | bytes 458784 | tf_op jit(solution)/shard_map/ppermute | solution.py:35
  272.7 5.3 %collective-permute-start.15 = (bf16[224,2048]{1,0:T(8,128)(2,1)}, bf16[224,2048]{1,0:T(8,128)(2,1)}, u32[]{:S(2)}, u32[]{:S(2)}) collective-permute-start(bf16[224,2048]{1,0:T(8,128)(2,1)} %pad_maximum_fusion.5), channel_id=1, source_target_pairs={{0,384},{1,385},{2,386},{3,387},{4,388},{5,389},{6,390},{7,391},{8... | collective-permute-start | bytes 2752520 | tf_op jit(solution)/shard_map/ppermute | solution.py:35
  278.0 11.0 %collective-permute-done.13 = bf16[224,2048]{1,0:T(8,128)(2,1)} collective-permute-done((bf16[224,2048]{1,0:T(8,128)(2,1)}, bf16[224,2048]{1,0:T(8,128)(2,1)}, u32[]{:S(2)}, u32[]{:S(2)}) %collective-permute-start.13) | collective-permute-done | bytes 917536 | tf_op jit(solution)/shard_map/ppermute | solution.py:35
  289.1 7.6 %collective-permute-done.15 = bf16[224,2048]{1,0:T(8,128)(2,1)} collective-permute-done((bf16[224,2048]{1,0:T(8,128)(2,1)}, bf16[224,2048]{1,0:T(8,128)(2,1)}, u32[]{:S(2)}, u32[]{:S(2)}) %collective-permute-start.15) | collective-permute-done | bytes 917536 | tf_op jit(solution)/shard_map/ppermute | solution.py:35
  296.7 1.9 add_convert_fusion
  298.7 4.4 %collective-permute-start.16 = (bf16[112,2048]{1,0:T(8,128)(2,1)S(1)}, bf16[112,2048]{1,0:T(8,128)(2,1)S(1)}, u32[]{:S(2)}, u32[]{:S(2)}) collective-permute-start(bf16[112,2048]{1,0:T(8,128)(2,1)S(1)} %get-tuple-element.40), channel_id=1, source_target_pairs={{0,128},{1,129},{2,192},{3,193},{4,132},{5,133},{6,196},{7,197},{8... | collective-permute-start | bytes 1376264 | tf_op jit(solution)/shard_map/ppermute | solution.py:35
  303.2 2.3 collective-permute-start.17
  305.5 17.6 %collective-permute-done.16 = bf16[112,2048]{1,0:T(8,128)(2,1)S(1)} collective-permute-done((bf16[112,2048]{1,0:T(8,128)(2,1)S(1)}, bf16[112,2048]{1,0:T(8,128)(2,1)S(1)}, u32[]{:S(2)}, u32[]{:S(2)}) %collective-permute-start.16) | collective-permute-done | bytes 458784 | tf_op jit(solution)/shard_map/ppermute | solution.py:35
  325.6 1.4 convolution_convert_fusion.2
  (150 shorter events, 24.6 us)
Async XLA Ops:
  0.6 2.2 copy-start.28
  0.7 2.2 copy-start.9
  5.5 18.9 %copy-start.21 = (bf16[112,1024]{1,0:T(8,128)(2,1)S(1)}, bf16[112,1024]{1,0:T(8,128)(2,1)}, u32[]{:S(2)}) copy-start(bf16[112,1024]{1,0:T(8,128)(2,1)} %param.10) | copy-start | bytes 688132
  5.5 19.6 %copy-start.22 = (bf16[112,1024]{1,0:T(8,128)(2,1)S(1)}, bf16[112,1024]{1,0:T(8,128)(2,1)}, u32[]{:S(2)}) copy-start(bf16[112,1024]{1,0:T(8,128)(2,1)} %param.11) | copy-start | bytes 688132
  5.5 164.9 %all-to-all-start = ((bf16[64,16,8,128]{3,2,1,0:T(8,128)(2,1)}), bf16[64,16,8,128]{3,2,1,0:T(8,128)(2,1)S(1)}, u32[]{:S(2)}, u32[]{:S(2)}) async-start(bf16[64,16,8,128]{3,2,1,0:T(8,128)(2,1)} %pad_maximum_fusion), calls=%async_computation | async-start | bytes 4194304 | tf_op jit(solution)/shard_map/all_to_all | solution.py:107
  25.8 56.8 %collective-permute-start.1 = (bf16[224,1024]{1,0:T(8,128)(2,1)}, bf16[224,1024]{1,0:T(8,128)(2,1)}, u32[]{:S(2)}, u32[]{:S(2)}) collective-permute-start(bf16[224,1024]{1,0:T(8,128)(2,1)} %constant_dynamic-update-slice_fusion), channel_id=1, source_target_pairs={{0,2},{1,3},{2,66},{3,67},{4,6},{5,7},{6,70},{7,71},{8,10},{9,11},... | collective-permute-start | bytes 1376264 | tf_op jit(solution)/shard_map/ppermute | solution.py:35
  28.1 87.2 %collective-permute-start = (bf16[224,1024]{1,0:T(8,128)(2,1)}, bf16[224,1024]{1,0:T(8,128)(2,1)S(1)}, u32[]{:S(2)}, u32[]{:S(2)}) collective-permute-start(bf16[224,1024]{1,0:T(8,128)(2,1)} %constant_dynamic-update-slice_fusion), channel_id=1, source_target_pairs={{0,0},{1,1},{2,64},{3,65},{4,4},{5,5},{6,68},{7,69},{8,8},{9,9},{1... | collective-permute-start | bytes 1376264 | tf_op jit(solution)/shard_map/ppermute | solution.py:35
  116.5 22.4 %collective-permute-start.4 = (bf16[448,1024]{1,0:T(8,128)(2,1)S(1)}, bf16[448,1024]{1,0:T(8,128)(2,1)S(1)}, u32[]{:S(2)}, u32[]{:S(2)}) collective-permute-start(bf16[448,1024]{1,0:T(8,128)(2,1)S(1)} %pad_maximum_fusion.3), channel_id=1, source_target_pairs={{0,128},{1,129},{2,130},{3,131},{4,132},{5,133},{6,134},{7,135},{8... | collective-permute-start | bytes 2752520 | tf_op jit(solution)/shard_map/ppermute | solution.py:35
  119.7 21.2 %collective-permute-start.2 = (bf16[448,1024]{1,0:T(8,128)(2,1)S(1)}, bf16[448,1024]{1,0:T(8,128)(2,1)S(1)}, u32[]{:S(2)}, u32[]{:S(2)}) collective-permute-start(bf16[448,1024]{1,0:T(8,128)(2,1)S(1)} %pad_maximum_fusion.3), channel_id=1, source_target_pairs={{0,384},{1,385},{2,386},{3,387},{4,388},{5,389},{6,390},{7,391},{8... | collective-permute-start | bytes 2752520 | tf_op jit(solution)/shard_map/ppermute | solution.py:35
  138.9 11.8 %copy-start.1 = (bf16[448,1024]{1,0:T(8,128)(2,1)}, bf16[448,1024]{1,0:T(8,128)(2,1)S(1)}, u32[]{:S(2)}) copy-start(bf16[448,1024]{1,0:T(8,128)(2,1)S(1)} %collective-permute-done.4) | copy-start | bytes 2752516
  138.9 11.6 %collective-permute-start.7 = (bf16[224,1024]{1,0:T(8,128)(2,1)S(1)}, bf16[224,1024]{1,0:T(8,128)(2,1)S(1)}, u32[]{:S(2)}, u32[]{:S(2)}) collective-permute-start(bf16[224,1024]{1,0:T(8,128)(2,1)S(1)} %slice.181), channel_id=1, source_target_pairs={{0,128},{1,129},{2,130},{3,131},{4,132},{5,133},{6,134},{7,135},{8... | collective-permute-start | bytes 1376264 | tf_op jit(solution)/shard_map/ppermute | solution.py:35
  140.9 11.5 %copy-start.5 = (bf16[448,1024]{1,0:T(8,128)(2,1)}, bf16[448,1024]{1,0:T(8,128)(2,1)S(1)}, u32[]{:S(2)}) copy-start(bf16[448,1024]{1,0:T(8,128)(2,1)S(1)} %collective-permute-done.2) | copy-start | bytes 2752516
  154.2 9.9 %collective-permute-start.3 = (bf16[224,1024]{1,0:T(8,128)(2,1)}, bf16[224,1024]{1,0:T(8,128)(2,1)}, u32[]{:S(2)}, u32[]{:S(2)}) collective-permute-start(bf16[224,1024]{1,0:T(8,128)(2,1)} %get-tuple-element.46), channel_id=1, source_target_pairs={{0,384},{1,385},{2,386},{3,387},{4,388},{5,389},{6,390},{7,391},{8... | collective-permute-start | bytes 1376264 | tf_op jit(solution)/shard_map/ppermute | solution.py:35
  156.3 9.7 %copy-start.2 = (bf16[448,1024]{1,0:T(8,128)(2,1)S(1)}, bf16[448,1024]{1,0:T(8,128)(2,1)}, u32[]{:S(2)}) copy-start(bf16[448,1024]{1,0:T(8,128)(2,1)} %copy-done.1) | copy-start | bytes 2752516
  158.2 9.6 %copy-start.6 = (bf16[448,1024]{1,0:T(8,128)(2,1)S(1)}, bf16[448,1024]{1,0:T(8,128)(2,1)}, u32[]{:S(2)}) copy-start(bf16[448,1024]{1,0:T(8,128)(2,1)} %copy-done.5) | copy-start | bytes 2752516
  170.6 2.7 copy-start.25
  171.9 3.1 copy-start.19
  171.9 3.1 copy-start.20
  171.9 16.1 %copy-start.15 = (bf16[144,896]{1,0:T(8,128)(2,1)}, bf16[144,896]{1,0:T(8,128)(2,1)S(1)}, u32[]{:S(2)}) copy-start(bf16[144,896]{1,0:T(8,128)(2,1)S(1)} %get-tuple-element.30) | copy-start | bytes 774148
  171.9 16.1 %copy-start.17 = (bf16[144,896]{1,0:T(8,128)(2,1)}, bf16[144,896]{1,0:T(8,128)(2,1)S(1)}, u32[]{:S(2)}) copy-start(bf16[144,896]{1,0:T(8,128)(2,1)S(1)} %get-tuple-element.31) | copy-start | bytes 774148
  173.3 8.8 %copy-start.3 = (bf16[448,1024]{1,0:T(8,128)(2,1)S(1)}, bf16[448,1024]{1,0:T(8,128)(2,1)}, u32[]{:S(2)}) copy-start(bf16[448,1024]{1,0:T(8,128)(2,1)} %copy-done.1) | copy-start | bytes 2752516
  173.3 9.8 %copy-start.4 = (bf16[64,7,8,128]{3,2,1,0:T(8,128)(2,1)S(1)}, bf16[64,7,8,128]{3,2,1,0:T(8,128)(2,1)}, u32[]{:S(2)}) copy-start(bf16[64,7,8,128]{3,2,1,0:T(8,128)(2,1)} %get-tuple-element.15) | copy-start | bytes 2752516
  175.0 12.9 %collective-permute-start.8 = (bf16[288,1024]{1,0:T(8,128)(2,1)}, bf16[288,1024]{1,0:T(8,128)(2,1)}, u32[]{:S(2)}, u32[]{:S(2)}) collective-permute-start(bf16[288,1024]{1,0:T(8,128)(2,1)} %fusion.11), channel_id=1, source_target_pairs={{0,64},{1,65},{2,66},{3,67},{4,68},{5,69},{6,70},{7,71},{8,72},{9,... | collective-permute-start | bytes 1769480 | tf_op jit(solution)/shard_map/ppermute | solution.py:35
  183.2 2.7 copy-start.13
  183.3 2.7 copy-start.14
  183.3 8.7 %copy-start.11 = (bf16[144,896]{1,0:T(8,128)(2,1)}, bf16[144,896]{1,0:T(8,128)(2,1)S(1)}, u32[]{:S(2)}) copy-start(bf16[144,896]{1,0:T(8,128)(2,1)S(1)} %get-tuple-element.34) | copy-start | bytes 774148
  183.3 8.7 %copy-start.12 = (bf16[144,896]{1,0:T(8,128)(2,1)}, bf16[144,896]{1,0:T(8,128)(2,1)S(1)}, u32[]{:S(2)}) copy-start(bf16[144,896]{1,0:T(8,128)(2,1)S(1)} %get-tuple-element.35) | copy-start | bytes 774148
  183.3 4.7 %copy-start.26 = (bf16[1792,1024]{1,0:T(8,128)(2,1)S(1)}, bf16[1792,1024]{1,0:T(8,128)(2,1)}, u32[]{:S(2)}) copy-start(bf16[1792,1024]{1,0:T(8,128)(2,1)} %get-tuple-element.42) | copy-start | bytes 11010052
  186.0 6.0 %collective-permute-start.5 = (bf16[288,1024]{1,0:T(8,128)(2,1)S(1)}, bf16[288,1024]{1,0:T(8,128)(2,1)S(1)}, u32[]{:S(2)}, u32[]{:S(2)}) collective-permute-start(bf16[288,1024]{1,0:T(8,128)(2,1)S(1)} %fusion.20), channel_id=1, source_target_pairs={{0,64},{1,65},{2,66},{3,67},{4,68},{5,69},{6,70},{7,71},{8,72},{9,... | collective-permute-start | bytes 1769480 | tf_op jit(solution)/shard_map/ppermute | solution.py:35
  188.0 4.0 %copy-start.23 = (bf16[1792,1024]{1,0:T(8,128)(2,1)S(1)}, bf16[1792,1024]{1,0:T(8,128)(2,1)}, u32[]{:S(2)}) copy-start(bf16[1792,1024]{1,0:T(8,128)(2,1)} %slice_dynamic-update-slice_fusion.3) | copy-start | bytes 11010052
  190.0 16.3 %copy-start.10 = (bf16[288,1024]{1,0:T(8,128)(2,1)}, bf16[288,1024]{1,0:T(8,128)(2,1)S(1)}, u32[]{:S(2)}) copy-start(bf16[288,1024]{1,0:T(8,128)(2,1)S(1)} %fusion.14) | copy-start | bytes 1769476
  190.0 16.3 %collective-permute-start.9 = (bf16[288,1024]{1,0:T(8,128)(2,1)S(1)}, bf16[288,1024]{1,0:T(8,128)(2,1)S(1)}, u32[]{:S(2)}, u32[]{:S(2)}) collective-permute-start(bf16[288,1024]{1,0:T(8,128)(2,1)S(1)} %fusion.14), channel_id=1, source_target_pairs={{0,1},{1,0},{2,3},{3,2},{4,5},{5,4},{6,7},{7,6},{8,9},{9,8},{10,11... | collective-permute-start | bytes 1769480 | tf_op jit(solution)/shard_map/ppermute | solution.py:35
  192.8 26.1 %collective-permute-start.6 = (bf16[288,1024]{1,0:T(8,128)(2,1)S(1)}, bf16[288,1024]{1,0:T(8,128)(2,1)S(1)}, u32[]{:S(2)}, u32[]{:S(2)}) collective-permute-start(bf16[288,1024]{1,0:T(8,128)(2,1)S(1)} %fusion.17), channel_id=1, source_target_pairs={{0,1},{1,0},{2,3},{3,2},{4,5},{5,4},{6,7},{7,6},{8,9},{9,8},{10,11... | collective-permute-start | bytes 1769480 | tf_op jit(solution)/shard_map/ppermute | solution.py:35
  219.0 7.3 %copy-start.16 = (bf16[144,896]{1,0:T(8,128)(2,1)S(1)}, bf16[144,896]{1,0:T(8,128)(2,1)}, u32[]{:S(2)}) copy-start(bf16[144,896]{1,0:T(8,128)(2,1)} %copy-done.15) | copy-start | bytes 774148
  219.0 7.3 %copy-start.18 = (bf16[144,896]{1,0:T(8,128)(2,1)S(1)}, bf16[144,896]{1,0:T(8,128)(2,1)}, u32[]{:S(2)}) copy-start(bf16[144,896]{1,0:T(8,128)(2,1)} %copy-done.17) | copy-start | bytes 774148
  219.5 5.9 %collective-permute-start.10 = (bf16[288,1024]{1,0:T(8,128)(2,1)S(1)}, bf16[288,1024]{1,0:T(8,128)(2,1)S(1)}, u32[]{:S(2)}, u32[]{:S(2)}) collective-permute-start(bf16[288,1024]{1,0:T(8,128)(2,1)S(1)} %get-tuple-element.22), channel_id=1, source_target_pairs={{0,64},{1,65},{2,66},{3,67},{4,68},{5,69},{6,70},{7,71},{8,72},{9,... | collective-permute-start | bytes 1769480 | tf_op jit(solution)/shard_map/ppermute | solution.py:35
  222.8 31.2 %collective-permute-start.11 = (bf16[288,1024]{1,0:T(8,128)(2,1)S(1)}, bf16[288,1024]{1,0:T(8,128)(2,1)}, u32[]{:S(2)}, u32[]{:S(2)}) collective-permute-start(bf16[288,1024]{1,0:T(8,128)(2,1)S(1)} %get-tuple-element.7), channel_id=1, source_target_pairs={{0,64},{1,65},{2,66},{3,67},{4,68},{5,69},{6,70},{7,71},{8,72},{9,... | collective-permute-start | bytes 1769480 | tf_op jit(solution)/shard_map/ppermute | solution.py:35
  226.3 5.9 %copy-start.27 = (bf16[1792,1024]{1,0:T(8,128)(2,1)S(1)}, bf16[1792,1024]{1,0:T(8,128)(2,1)}, u32[]{:S(2)}) copy-start(bf16[1792,1024]{1,0:T(8,128)(2,1)} %get-tuple-element.42) | copy-start | bytes 11010052
  229.2 4.5 %copy-start.8 = (bf16[896,1024]{1,0:T(8,128)(2,1)}, bf16[896,1024]{1,0:T(8,128)(2,1)S(1)}, u32[]{:S(2)}) copy-start(bf16[896,1024]{1,0:T(8,128)(2,1)S(1)} %convolution_convert_fusion.4) | copy-start | bytes 5505028
  229.2 3.0 copy-start.30
  230.1 32.1 %collective-permute-start.12 = (bf16[224,1024]{1,0:T(8,128)(2,1)}, bf16[224,1024]{1,0:T(8,128)(2,1)}, u32[]{:S(2)}, u32[]{:S(2)}) collective-permute-start(bf16[224,1024]{1,0:T(8,128)(2,1)} %get-tuple-element.18), channel_id=1, source_target_pairs={{0,128},{1,129},{2,130},{3,131},{4,132},{5,133},{6,134},{7,135},{8... | collective-permute-start | bytes 1376264 | tf_op jit(solution)/shard_map/ppermute | solution.py:35
  236.9 87.4 %all-to-all-start.1 = ((bf16[64,8,8,128]{3,2,1,0:T(8,128)(2,1)}), bf16[64,8,8,128]{3,2,1,0:T(8,128)(2,1)S(1)}, u32[]{:S(2)}, u32[]{:S(2)}) async-start(bf16[64,8,8,128]{3,2,1,0:T(8,128)(2,1)} %maximum_maximum_fusion), calls=%async_computation.1 | async-start | bytes 2097152 | tf_op jit(solution)/shard_map/all_to_all | solution.py:107
  257.3 14.3 %collective-permute-start.14 = (bf16[224,1024]{1,0:T(8,128)(2,1)S(1)}, bf16[224,1024]{1,0:T(8,128)(2,1)S(1)}, u32[]{:S(2)}, u32[]{:S(2)}) collective-permute-start(bf16[224,1024]{1,0:T(8,128)(2,1)S(1)} %get-tuple-element.20), channel_id=1, source_target_pairs={{0,384},{1,385},{2,386},{3,387},{4,388},{5,389},{6,390},{7,391},{8... | collective-permute-start | bytes 1376264 | tf_op jit(solution)/shard_map/ppermute | solution.py:35
  264.5 24.6 %collective-permute-start.13 = (bf16[224,2048]{1,0:T(8,128)(2,1)}, bf16[224,2048]{1,0:T(8,128)(2,1)}, u32[]{:S(2)}, u32[]{:S(2)}) collective-permute-start(bf16[224,2048]{1,0:T(8,128)(2,1)} %pad_maximum_fusion.4), channel_id=1, source_target_pairs={{0,128},{1,129},{2,130},{3,131},{4,132},{5,133},{6,134},{7,135},{8... | collective-permute-start | bytes 2752520 | tf_op jit(solution)/shard_map/ppermute | solution.py:35
  272.7 24.0 %collective-permute-start.15 = (bf16[224,2048]{1,0:T(8,128)(2,1)}, bf16[224,2048]{1,0:T(8,128)(2,1)}, u32[]{:S(2)}, u32[]{:S(2)}) collective-permute-start(bf16[224,2048]{1,0:T(8,128)(2,1)} %pad_maximum_fusion.5), channel_id=1, source_target_pairs={{0,384},{1,385},{2,386},{3,387},{4,388},{5,389},{6,390},{7,391},{8... | collective-permute-start | bytes 2752520 | tf_op jit(solution)/shard_map/ppermute | solution.py:35
  296.7 8.8 %copy-start.31 = (s32[128,1]{0,1:T(1,128)S(1)}, s32[128,1]{0,1:T(1,128)}, u32[]{:S(2)}) copy-start(s32[128,1]{0,1:T(1,128)} %param.9) | copy-start | bytes 1540
  298.7 24.4 %collective-permute-start.16 = (bf16[112,2048]{1,0:T(8,128)(2,1)S(1)}, bf16[112,2048]{1,0:T(8,128)(2,1)S(1)}, u32[]{:S(2)}, u32[]{:S(2)}) collective-permute-start(bf16[112,2048]{1,0:T(8,128)(2,1)S(1)} %get-tuple-element.40), channel_id=1, source_target_pairs={{0,128},{1,129},{2,192},{3,193},{4,132},{5,133},{6,196},{7,197},{8... | collective-permute-start | bytes 1376264 | tf_op jit(solution)/shard_map/ppermute | solution.py:35
  303.2 20.0 %collective-permute-start.17 = (bf16[112,2048]{1,0:T(8,128)(2,1)S(1)}, bf16[112,2048]{1,0:T(8,128)(2,1)S(1)}, u32[]{:S(2)}, u32[]{:S(2)}) collective-permute-start(bf16[112,2048]{1,0:T(8,128)(2,1)S(1)} %get-tuple-element.41), channel_id=1, source_target_pairs={{0,192},{1,193},{2,128},{3,129},{4,196},{5,197},{6,132},{7,133},{8... | collective-permute-start | bytes 1376264 | tf_op jit(solution)/shard_map/ppermute | solution.py:35
  (4 other events, 5.1 us)

commit v6 on v5

--- a/solution.py
+++ b/solution.py
@@ -82,7 +82,7 @@
 
     def y_block(term, step):
         rows_y = term.shape[0] // y_size
-        start = (y_now + 1 + step) % y_size * rows_y
+        start = (y_now + step) % y_size * rows_y
         return lax.dynamic_slice_in_dim(term, start, rows_y, axis=0)
 
     def plus(part, got):
@@ -99,8 +99,8 @@
         half = total.shape[0] // 2
         low, high = total[:half], total[half:]
         first, second = jnp.where(far == 1, high, low), jnp.where(far == 1, low, high)
-        first = moved(first, n_rep, n_dev, lambda c, h, b: (h, c, b), 1)
-        second = moved(second, n_rep, n_dev, lambda c, h, b: (1 - h, c, b), 1)
+        first = moved(first, n_rep, n_dev, lambda c, h, b: (h, c, b))
+        second = moved(second, n_rep, n_dev, lambda c, h, b: (1 - h, c, b))
         return first.astype(f32) + second.astype(f32)
 
     def routed(x):

time: 333 us -> 330 us (level)
    ppermute x18, waiting for transfers between devices: 176 us -> 173 us  [moved(): return lax.ppermute(x, BOTH, pairs)]
where the time goes in v6:
time: 330 us; the launch traced here: 324 us
  waiting for transfers between devices  173 us (52%)
  starting transfers between devices  93.2 us (28%)
  local copies, waits for them, and re-layouts  23.8 us (7%)
  matrix products  16.9 us (5%)
  other arithmetic  15.4 us (5%)
    ppermute x18, waiting for transfers between devices, moved(): return lax.ppermute(x, BOTH, pairs)  173 us
    ppermute x18, starting transfers between devices, moved(): return lax.ppermute(x, BOTH, pairs)  57.2 us
    all_to_all x2, starting transfers between devices, routed(): lax.all_to_all(x, BOTH, split_axis=0, concat_axis=0, axis_index_groups=to...  36 us
    dot_general x10, matrix products, contract(): lax.dot_general(left, right, ((dims[0], dims[1]), ((), ())), preferred_el...  16.9 us
    unnamed x75, local copies, waits for them, and re-layouts  13.9 us
  transfers between devices with their start and end apart: 20, of which 11 were waited for; matrix products, arithmetic and copies ran while one was open for 12% of the time, Pallas kernels for 0%

profile of v6, /device:TPU:1, one launch (start us, length us, event | category | flops | bytes accessed | tf_op | source)
XLA Modules:
  0.0 323.8 jit_solution(17926622440293895905)
XLA Ops:
  3.8 1.7 pad_maximum_fusion
  5.5 18.8 %all-to-all-start = ((bf16[64,16,8,128]{3,2,1,0:T(8,128)(2,1)}), bf16[64,16,8,128]{3,2,1,0:T(8,128)(2,1)S(1)}, u32[]{:S(2)}, u32[]{:S(2)}) async-start(bf16[64,16,8,128]{3,2,1,0:T(8,128)(2,1)} %pad_maximum_fusion), calls=%async_computation | async-start | bytes 4194304 | tf_op jit(solution)/shard_map/all_to_all | solution.py:107
  25.8 2.4 collective-permute-start.1
  28.1 3.5 %collective-permute-start = (bf16[224,1024]{1,0:T(8,128)(2,1)}, bf16[224,1024]{1,0:T(8,128)(2,1)S(1)}, u32[]{:S(2)}, u32[]{:S(2)}) collective-permute-start(bf16[224,1024]{1,0:T(8,128)(2,1)} %constant_dynamic-update-slice_fusion), channel_id=1, source_target_pairs={{0,0},{1,1},{2,64},{3,65},{4,4},{5,5},{6,68},{7,69},{8,8},{9,9},{1... | collective-permute-start | bytes 1376264 | tf_op jit(solution)/shard_map/ppermute | solution.py:35
  31.6 50.9 %collective-permute-done.1 = bf16[224,1024]{1,0:T(8,128)(2,1)} collective-permute-done((bf16[224,1024]{1,0:T(8,128)(2,1)}, bf16[224,1024]{1,0:T(8,128)(2,1)}, u32[]{:S(2)}, u32[]{:S(2)}) %collective-permute-start.1) | collective-permute-done | bytes 458784 | tf_op jit(solution)/shard_map/ppermute | solution.py:35
  83.7 31.7 %collective-permute-done = bf16[224,1024]{1,0:T(8,128)(2,1)S(1)} collective-permute-done((bf16[224,1024]{1,0:T(8,128)(2,1)}, bf16[224,1024]{1,0:T(8,128)(2,1)S(1)}, u32[]{:S(2)}, u32[]{:S(2)}) %collective-permute-start) | collective-permute-done | bytes 458784 | tf_op jit(solution)/shard_map/ppermute | solution.py:35
  116.5 3.2 collective-permute-start.4
  119.7 3.4 %collective-permute-start.2 = (bf16[448,1024]{1,0:T(8,128)(2,1)S(1)}, bf16[448,1024]{1,0:T(8,128)(2,1)S(1)}, u32[]{:S(2)}, u32[]{:S(2)}) collective-permute-start(bf16[448,1024]{1,0:T(8,128)(2,1)S(1)} %pad_maximum_fusion.3), channel_id=1, source_target_pairs={{0,384},{1,385},{2,386},{3,387},{4,388},{5,389},{6,390},{7,391},{8... | collective-permute-start | bytes 2752520 | tf_op jit(solution)/shard_map/ppermute | solution.py:35
  123.1 15.8 %collective-permute-done.4 = bf16[448,1024]{1,0:T(8,128)(2,1)S(1)} collective-permute-done((bf16[448,1024]{1,0:T(8,128)(2,1)S(1)}, bf16[448,1024]{1,0:T(8,128)(2,1)S(1)}, u32[]{:S(2)}, u32[]{:S(2)}) %collective-permute-start.4) | collective-permute-done | bytes 917536 | tf_op jit(solution)/shard_map/ppermute | solution.py:35
  138.9 1.9 collective-permute-start.7
  140.9 9.7 %collective-permute-done.7 = bf16[224,1024]{1,0:T(8,128)(2,1)S(1)} collective-permute-done((bf16[224,1024]{1,0:T(8,128)(2,1)S(1)}, bf16[224,1024]{1,0:T(8,128)(2,1)S(1)}, u32[]{:S(2)}, u32[]{:S(2)}) %collective-permute-start.7) | collective-permute-done | bytes 458784 | tf_op jit(solution)/shard_map/ppermute | solution.py:35
  152.4 1.8 copy-done.24
  154.2 2.0 collective-permute-start.3
  156.3 1.9 constant_dynamic-update-slice_fusion.9
  158.2 5.9 %collective-permute-done.3 = bf16[224,1024]{1,0:T(8,128)(2,1)} collective-permute-done((bf16[224,1024]{1,0:T(8,128)(2,1)}, bf16[224,1024]{1,0:T(8,128)(2,1)}, u32[]{:S(2)}, u32[]{:S(2)}) %collective-permute-start.3) | collective-permute-done | bytes 458784 | tf_op jit(solution)/shard_map/ppermute | solution.py:35
  164.1 1.8 constant_dynamic-update-slice_fusion.5
  168.5 1.8 constant_dynamic-update-slice_fusion.2
  171.9 1.4 copy-done.25
  173.3 1.6 fusion.11
  175.0 7.2 %collective-permute-start.8 = (bf16[288,1024]{1,0:T(8,128)(2,1)}, bf16[288,1024]{1,0:T(8,128)(2,1)}, u32[]{:S(2)}, u32[]{:S(2)}) collective-permute-start(bf16[288,1024]{1,0:T(8,128)(2,1)} %fusion.11), channel_id=1, source_target_pairs={{0,64},{1,65},{2,66},{3,67},{4,68},{5,69},{6,70},{7,71},{8,72},{9,... | collective-permute-start | bytes 1769480 | tf_op jit(solution)/shard_map/ppermute | solution.py:35
  183.3 2.7 fusion.20
  186.0 1.9 collective-permute-start.5
  188.0 2.0 fusion.14
  190.0 1.9 collective-permute-start.9
  192.8 3.4 %collective-permute-start.6 = (bf16[288,1024]{1,0:T(8,128)(2,1)S(1)}, bf16[288,1024]{1,0:T(8,128)(2,1)S(1)}, u32[]{:S(2)}, u32[]{:S(2)}) collective-permute-start(bf16[288,1024]{1,0:T(8,128)(2,1)S(1)} %fusion.17), channel_id=1, source_target_pairs={{0,1},{1,0},{2,3},{3,2},{4,5},{5,4},{6,7},{7,6},{8,9},{9,8},{10,11... | collective-permute-start | bytes 1769480 | tf_op jit(solution)/shard_map/ppermute | solution.py:35
  196.4 9.9 %collective-permute-done.9 = bf16[288,1024]{1,0:T(8,128)(2,1)S(1)} collective-permute-done((bf16[288,1024]{1,0:T(8,128)(2,1)S(1)}, bf16[288,1024]{1,0:T(8,128)(2,1)S(1)}, u32[]{:S(2)}, u32[]{:S(2)}) %collective-permute-start.9) | collective-permute-done | bytes 589856 | tf_op jit(solution)/shard_map/ppermute | solution.py:35
  206.4 1.4 convert_add_fusion
  207.8 11.2 %collective-permute-done.6 = bf16[288,1024]{1,0:T(8,128)(2,1)S(1)} collective-permute-done((bf16[288,1024]{1,0:T(8,128)(2,1)S(1)}, bf16[288,1024]{1,0:T(8,128)(2,1)S(1)}, u32[]{:S(2)}, u32[]{:S(2)}) %collective-permute-start.6) | collective-permute-done | bytes 589856 | tf_op jit(solution)/shard_map/ppermute | solution.py:35
  219.5 3.3 %collective-permute-start.10 = (bf16[288,1024]{1,0:T(8,128)(2,1)S(1)}, bf16[288,1024]{1,0:T(8,128)(2,1)S(1)}, u32[]{:S(2)}, u32[]{:S(2)}) collective-permute-start(bf16[288,1024]{1,0:T(8,128)(2,1)S(1)} %get-tuple-element.22), channel_id=1, source_target_pairs={{0,64},{1,65},{2,66},{3,67},{4,68},{5,69},{6,70},{7,71},{8,72},{9,... | collective-permute-start | bytes 1769480 | tf_op jit(solution)/shard_map/ppermute | solution.py:35
  222.8 1.9 collective-permute-start.11
  226.3 2.9 convolution_convert_fusion.4
  230.1 2.1 collective-permute-start.12
  232.2 1.4 convolution_convert_fusion.5
  235.7 1.2 maximum_maximum_fusion
  236.9 17.1 %all-to-all-start.1 = ((bf16[64,8,8,128]{3,2,1,0:T(8,128)(2,1)}), bf16[64,8,8,128]{3,2,1,0:T(8,128)(2,1)S(1)}, u32[]{:S(2)}, u32[]{:S(2)}) async-start(bf16[64,8,8,128]{3,2,1,0:T(8,128)(2,1)} %maximum_maximum_fusion), calls=%async_computation.1 | async-start | bytes 2097152 | tf_op jit(solution)/shard_map/all_to_all | solution.py:107
  254.0 3.1 convolution_convert_fusion.3
  257.3 4.9 %collective-permute-start.14 = (bf16[224,1024]{1,0:T(8,128)(2,1)S(1)}, bf16[224,1024]{1,0:T(8,128)(2,1)S(1)}, u32[]{:S(2)}, u32[]{:S(2)}) collective-permute-start(bf16[224,1024]{1,0:T(8,128)(2,1)S(1)} %get-tuple-element.20), channel_id=1, source_target_pairs={{0,384},{1,385},{2,386},{3,387},{4,388},{5,389},{6,390},{7,391},{8... | collective-permute-start | bytes 1376264 | tf_op jit(solution)/shard_map/ppermute | solution.py:35
  262.2 1.3 add_convert_fusion.2
  264.5 1.9 collective-permute-start.13
  266.4 5.1 %collective-permute-done.14 = bf16[224,1024]{1,0:T(8,128)(2,1)S(1)} collective-permute-done((bf16[224,1024]{1,0:T(8,128)(2,1)S(1)}, bf16[224,1024]{1,0:T(8,128)(2,1)S(1)}, u32[]{:S(2)}, u32[]{:S(2)}) %collective-permute-start.14) | collective-permute-done | bytes 458784 | tf_op jit(solution)/shard_map/ppermute | solution.py:35
  272.7 5.3 %collective-permute-start.15 = (bf16[224,2048]{1,0:T(8,128)(2,1)}, bf16[224,2048]{1,0:T(8,128)(2,1)}, u32[]{:S(2)}, u32[]{:S(2)}) collective-permute-start(bf16[224,2048]{1,0:T(8,128)(2,1)} %pad_maximum_fusion.5), channel_id=1, source_target_pairs={{0,384},{1,385},{2,386},{3,387},{4,388},{5,389},{6,390},{7,391},{8... | collective-permute-start | bytes 2752520 | tf_op jit(solution)/shard_map/ppermute | solution.py:35
  278.0 11.0 %collective-permute-done.13 = bf16[224,2048]{1,0:T(8,128)(2,1)} collective-permute-done((bf16[224,2048]{1,0:T(8,128)(2,1)}, bf16[224,2048]{1,0:T(8,128)(2,1)}, u32[]{:S(2)}, u32[]{:S(2)}) %collective-permute-start.13) | collective-permute-done | bytes 917536 | tf_op jit(solution)/shard_map/ppermute | solution.py:35
  289.1 7.6 %collective-permute-done.15 = bf16[224,2048]{1,0:T(8,128)(2,1)} collective-permute-done((bf16[224,2048]{1,0:T(8,128)(2,1)}, bf16[224,2048]{1,0:T(8,128)(2,1)}, u32[]{:S(2)}, u32[]{:S(2)}) %collective-permute-start.15) | collective-permute-done | bytes 917536 | tf_op jit(solution)/shard_map/ppermute | solution.py:35
  296.7 1.9 add_convert_fusion
  298.7 5.3 %collective-permute-start.16 = (bf16[112,2048]{1,0:T(8,128)(2,1)S(1)}, bf16[112,2048]{1,0:T(8,128)(2,1)S(1)}, u32[]{:S(2)}, u32[]{:S(2)}) collective-permute-start(bf16[112,2048]{1,0:T(8,128)(2,1)S(1)} %get-tuple-element.40), channel_id=1, source_target_pairs={{0,0},{1,1},{2,64},{3,65},{4,4},{5,5},{6,68},{7,69},{8,8},{9,9},{1... | collective-permute-start | bytes 1376264 | tf_op jit(solution)/shard_map/ppermute | solution.py:35
  304.0 1.9 collective-permute-start.17
  306.0 14.0 %collective-permute-done.16 = bf16[112,2048]{1,0:T(8,128)(2,1)S(1)} collective-permute-done((bf16[112,2048]{1,0:T(8,128)(2,1)S(1)}, bf16[112,2048]{1,0:T(8,128)(2,1)S(1)}, u32[]{:S(2)}, u32[]{:S(2)}) %collective-permute-start.16) | collective-permute-done | bytes 458784 | tf_op jit(solution)/shard_map/ppermute | solution.py:35
  322.4 1.4 convolution_convert_fusion.2
  (150 shorter events, 24.6 us)
Async XLA Ops:
  0.6 2.2 copy-start.28
  0.7 2.2 copy-start.9
  5.5 18.9 %copy-start.21 = (bf16[112,1024]{1,0:T(8,128)(2,1)S(1)}, bf16[112,1024]{1,0:T(8,128)(2,1)}, u32[]{:S(2)}) copy-start(bf16[112,1024]{1,0:T(8,128)(2,1)} %param.10) | copy-start | bytes 688132
  5.5 19.6 %copy-start.22 = (bf16[112,1024]{1,0:T(8,128)(2,1)S(1)}, bf16[112,1024]{1,0:T(8,128)(2,1)}, u32[]{:S(2)}) copy-start(bf16[112,1024]{1,0:T(8,128)(2,1)} %param.11) | copy-start | bytes 688132
  5.5 164.9 %all-to-all-start = ((bf16[64,16,8,128]{3,2,1,0:T(8,128)(2,1)}), bf16[64,16,8,128]{3,2,1,0:T(8,128)(2,1)S(1)}, u32[]{:S(2)}, u32[]{:S(2)}) async-start(bf16[64,16,8,128]{3,2,1,0:T(8,128)(2,1)} %pad_maximum_fusion), calls=%async_computation | async-start | bytes 4194304 | tf_op jit(solution)/shard_map/all_to_all | solution.py:107
  25.8 56.8 %collective-permute-start.1 = (bf16[224,1024]{1,0:T(8,128)(2,1)}, bf16[224,1024]{1,0:T(8,128)(2,1)}, u32[]{:S(2)}, u32[]{:S(2)}) collective-permute-start(bf16[224,1024]{1,0:T(8,128)(2,1)} %constant_dynamic-update-slice_fusion), channel_id=1, source_target_pairs={{0,2},{1,3},{2,66},{3,67},{4,6},{5,7},{6,70},{7,71},{8,10},{9,11},... | collective-permute-start | bytes 1376264 | tf_op jit(solution)/shard_map/ppermute | solution.py:35
  28.1 87.2 %collective-permute-start = (bf16[224,1024]{1,0:T(8,128)(2,1)}, bf16[224,1024]{1,0:T(8,128)(2,1)S(1)}, u32[]{:S(2)}, u32[]{:S(2)}) collective-permute-start(bf16[224,1024]{1,0:T(8,128)(2,1)} %constant_dynamic-update-slice_fusion), channel_id=1, source_target_pairs={{0,0},{1,1},{2,64},{3,65},{4,4},{5,5},{6,68},{7,69},{8,8},{9,9},{1... | collective-permute-start | bytes 1376264 | tf_op jit(solution)/shard_map/ppermute | solution.py:35
  116.5 22.4 %collective-permute-start.4 = (bf16[448,1024]{1,0:T(8,128)(2,1)S(1)}, bf16[448,1024]{1,0:T(8,128)(2,1)S(1)}, u32[]{:S(2)}, u32[]{:S(2)}) collective-permute-start(bf16[448,1024]{1,0:T(8,128)(2,1)S(1)} %pad_maximum_fusion.3), channel_id=1, source_target_pairs={{0,128},{1,129},{2,130},{3,131},{4,132},{5,133},{6,134},{7,135},{8... | collective-permute-start | bytes 2752520 | tf_op jit(solution)/shard_map/ppermute | solution.py:35
  119.7 21.2 %collective-permute-start.2 = (bf16[448,1024]{1,0:T(8,128)(2,1)S(1)}, bf16[448,1024]{1,0:T(8,128)(2,1)S(1)}, u32[]{:S(2)}, u32[]{:S(2)}) collective-permute-start(bf16[448,1024]{1,0:T(8,128)(2,1)S(1)} %pad_maximum_fusion.3), channel_id=1, source_target_pairs={{0,384},{1,385},{2,386},{3,387},{4,388},{5,389},{6,390},{7,391},{8... | collective-permute-start | bytes 2752520 | tf_op jit(solution)/shard_map/ppermute | solution.py:35
  138.9 11.8 %copy-start.1 = (bf16[448,1024]{1,0:T(8,128)(2,1)}, bf16[448,1024]{1,0:T(8,128)(2,1)S(1)}, u32[]{:S(2)}) copy-start(bf16[448,1024]{1,0:T(8,128)(2,1)S(1)} %collective-permute-done.4) | copy-start | bytes 2752516
  138.9 11.6 %collective-permute-start.7 = (bf16[224,1024]{1,0:T(8,128)(2,1)S(1)}, bf16[224,1024]{1,0:T(8,128)(2,1)S(1)}, u32[]{:S(2)}, u32[]{:S(2)}) collective-permute-start(bf16[224,1024]{1,0:T(8,128)(2,1)S(1)} %slice.181), channel_id=1, source_target_pairs={{0,128},{1,129},{2,130},{3,131},{4,132},{5,133},{6,134},{7,135},{8... | collective-permute-start | bytes 1376264 | tf_op jit(solution)/shard_map/ppermute | solution.py:35
  140.9 11.5 %copy-start.5 = (bf16[448,1024]{1,0:T(8,128)(2,1)}, bf16[448,1024]{1,0:T(8,128)(2,1)S(1)}, u32[]{:S(2)}) copy-start(bf16[448,1024]{1,0:T(8,128)(2,1)S(1)} %collective-permute-done.2) | copy-start | bytes 2752516
  154.2 9.9 %collective-permute-start.3 = (bf16[224,1024]{1,0:T(8,128)(2,1)}, bf16[224,1024]{1,0:T(8,128)(2,1)}, u32[]{:S(2)}, u32[]{:S(2)}) collective-permute-start(bf16[224,1024]{1,0:T(8,128)(2,1)} %get-tuple-element.46), channel_id=1, source_target_pairs={{0,384},{1,385},{2,386},{3,387},{4,388},{5,389},{6,390},{7,391},{8... | collective-permute-start | bytes 1376264 | tf_op jit(solution)/shard_map/ppermute | solution.py:35
  156.3 9.7 %copy-start.2 = (bf16[448,1024]{1,0:T(8,128)(2,1)S(1)}, bf16[448,1024]{1,0:T(8,128)(2,1)}, u32[]{:S(2)}) copy-start(bf16[448,1024]{1,0:T(8,128)(2,1)} %copy-done.1) | copy-start | bytes 2752516
  158.2 9.6 %copy-start.6 = (bf16[448,1024]{1,0:T(8,128)(2,1)S(1)}, bf16[448,1024]{1,0:T(8,128)(2,1)}, u32[]{:S(2)}) copy-start(bf16[448,1024]{1,0:T(8,128)(2,1)} %copy-done.5) | copy-start | bytes 2752516
  170.6 2.7 copy-start.25
  171.9 3.1 copy-start.19
  171.9 3.1 copy-start.20
  171.9 16.1 %copy-start.15 = (bf16[144,896]{1,0:T(8,128)(2,1)}, bf16[144,896]{1,0:T(8,128)(2,1)S(1)}, u32[]{:S(2)}) copy-start(bf16[144,896]{1,0:T(8,128)(2,1)S(1)} %get-tuple-element.30) | copy-start | bytes 774148
  171.9 16.1 %copy-start.17 = (bf16[144,896]{1,0:T(8,128)(2,1)}, bf16[144,896]{1,0:T(8,128)(2,1)S(1)}, u32[]{:S(2)}) copy-start(bf16[144,896]{1,0:T(8,128)(2,1)S(1)} %get-tuple-element.31) | copy-start | bytes 774148
  173.3 8.8 %copy-start.3 = (bf16[448,1024]{1,0:T(8,128)(2,1)S(1)}, bf16[448,1024]{1,0:T(8,128)(2,1)}, u32[]{:S(2)}) copy-start(bf16[448,1024]{1,0:T(8,128)(2,1)} %copy-done.1) | copy-start | bytes 2752516
  173.3 9.8 %copy-start.4 = (bf16[64,7,8,128]{3,2,1,0:T(8,128)(2,1)S(1)}, bf16[64,7,8,128]{3,2,1,0:T(8,128)(2,1)}, u32[]{:S(2)}) copy-start(bf16[64,7,8,128]{3,2,1,0:T(8,128)(2,1)} %get-tuple-element.15) | copy-start | bytes 2752516
  175.0 12.9 %collective-permute-start.8 = (bf16[288,1024]{1,0:T(8,128)(2,1)}, bf16[288,1024]{1,0:T(8,128)(2,1)}, u32[]{:S(2)}, u32[]{:S(2)}) collective-permute-start(bf16[288,1024]{1,0:T(8,128)(2,1)} %fusion.11), channel_id=1, source_target_pairs={{0,64},{1,65},{2,66},{3,67},{4,68},{5,69},{6,70},{7,71},{8,72},{9,... | collective-permute-start | bytes 1769480 | tf_op jit(solution)/shard_map/ppermute | solution.py:35
  183.2 2.7 copy-start.13
  183.3 2.7 copy-start.14
  183.3 8.7 %copy-start.11 = (bf16[144,896]{1,0:T(8,128)(2,1)}, bf16[144,896]{1,0:T(8,128)(2,1)S(1)}, u32[]{:S(2)}) copy-start(bf16[144,896]{1,0:T(8,128)(2,1)S(1)} %get-tuple-element.34) | copy-start | bytes 774148
  183.3 8.7 %copy-start.12 = (bf16[144,896]{1,0:T(8,128)(2,1)}, bf16[144,896]{1,0:T(8,128)(2,1)S(1)}, u32[]{:S(2)}) copy-start(bf16[144,896]{1,0:T(8,128)(2,1)S(1)} %get-tuple-element.35) | copy-start | bytes 774148
  183.3 4.7 %copy-start.26 = (bf16[1792,1024]{1,0:T(8,128)(2,1)S(1)}, bf16[1792,1024]{1,0:T(8,128)(2,1)}, u32[]{:S(2)}) copy-start(bf16[1792,1024]{1,0:T(8,128)(2,1)} %get-tuple-element.42) | copy-start | bytes 11010052
  186.0 6.0 %collective-permute-start.5 = (bf16[288,1024]{1,0:T(8,128)(2,1)S(1)}, bf16[288,1024]{1,0:T(8,128)(2,1)S(1)}, u32[]{:S(2)}, u32[]{:S(2)}) collective-permute-start(bf16[288,1024]{1,0:T(8,128)(2,1)S(1)} %fusion.20), channel_id=1, source_target_pairs={{0,64},{1,65},{2,66},{3,67},{4,68},{5,69},{6,70},{7,71},{8,72},{9,... | collective-permute-start | bytes 1769480 | tf_op jit(solution)/shard_map/ppermute | solution.py:35
  188.0 4.0 %copy-start.23 = (bf16[1792,1024]{1,0:T(8,128)(2,1)S(1)}, bf16[1792,1024]{1,0:T(8,128)(2,1)}, u32[]{:S(2)}) copy-start(bf16[1792,1024]{1,0:T(8,128)(2,1)} %slice_dynamic-update-slice_fusion.3) | copy-start | bytes 11010052
  190.0 16.3 %copy-start.10 = (bf16[288,1024]{1,0:T(8,128)(2,1)}, bf16[288,1024]{1,0:T(8,128)(2,1)S(1)}, u32[]{:S(2)}) copy-start(bf16[288,1024]{1,0:T(8,128)(2,1)S(1)} %fusion.14) | copy-start | bytes 1769476
  190.0 16.3 %collective-permute-start.9 = (bf16[288,1024]{1,0:T(8,128)(2,1)S(1)}, bf16[288,1024]{1,0:T(8,128)(2,1)S(1)}, u32[]{:S(2)}, u32[]{:S(2)}) collective-permute-start(bf16[288,1024]{1,0:T(8,128)(2,1)S(1)} %fusion.14), channel_id=1, source_target_pairs={{0,1},{1,0},{2,3},{3,2},{4,5},{5,4},{6,7},{7,6},{8,9},{9,8},{10,11... | collective-permute-start | bytes 1769480 | tf_op jit(solution)/shard_map/ppermute | solution.py:35
  192.8 26.1 %collective-permute-start.6 = (bf16[288,1024]{1,0:T(8,128)(2,1)S(1)}, bf16[288,1024]{1,0:T(8,128)(2,1)S(1)}, u32[]{:S(2)}, u32[]{:S(2)}) collective-permute-start(bf16[288,1024]{1,0:T(8,128)(2,1)S(1)} %fusion.17), channel_id=1, source_target_pairs={{0,1},{1,0},{2,3},{3,2},{4,5},{5,4},{6,7},{7,6},{8,9},{9,8},{10,11... | collective-permute-start | bytes 1769480 | tf_op jit(solution)/shard_map/ppermute | solution.py:35
  219.0 7.3 %copy-start.16 = (bf16[144,896]{1,0:T(8,128)(2,1)S(1)}, bf16[144,896]{1,0:T(8,128)(2,1)}, u32[]{:S(2)}) copy-start(bf16[144,896]{1,0:T(8,128)(2,1)} %copy-done.15) | copy-start | bytes 774148
  219.0 7.3 %copy-start.18 = (bf16[144,896]{1,0:T(8,128)(2,1)S(1)}, bf16[144,896]{1,0:T(8,128)(2,1)}, u32[]{:S(2)}) copy-start(bf16[144,896]{1,0:T(8,128)(2,1)} %copy-done.17) | copy-start | bytes 774148
  219.5 5.9 %collective-permute-start.10 = (bf16[288,1024]{1,0:T(8,128)(2,1)S(1)}, bf16[288,1024]{1,0:T(8,128)(2,1)S(1)}, u32[]{:S(2)}, u32[]{:S(2)}) collective-permute-start(bf16[288,1024]{1,0:T(8,128)(2,1)S(1)} %get-tuple-element.22), channel_id=1, source_target_pairs={{0,64},{1,65},{2,66},{3,67},{4,68},{5,69},{6,70},{7,71},{8,72},{9,... | collective-permute-start | bytes 1769480 | tf_op jit(solution)/shard_map/ppermute | solution.py:35
  222.8 31.2 %collective-permute-start.11 = (bf16[288,1024]{1,0:T(8,128)(2,1)S(1)}, bf16[288,1024]{1,0:T(8,128)(2,1)}, u32[]{:S(2)}, u32[]{:S(2)}) collective-permute-start(bf16[288,1024]{1,0:T(8,128)(2,1)S(1)} %get-tuple-element.7), channel_id=1, source_target_pairs={{0,64},{1,65},{2,66},{3,67},{4,68},{5,69},{6,70},{7,71},{8,72},{9,... | collective-permute-start | bytes 1769480 | tf_op jit(solution)/shard_map/ppermute | solution.py:35
  226.3 5.9 %copy-start.27 = (bf16[1792,1024]{1,0:T(8,128)(2,1)S(1)}, bf16[1792,1024]{1,0:T(8,128)(2,1)}, u32[]{:S(2)}) copy-start(bf16[1792,1024]{1,0:T(8,128)(2,1)} %get-tuple-element.42) | copy-start | bytes 11010052
  229.2 4.5 %copy-start.8 = (bf16[896,1024]{1,0:T(8,128)(2,1)}, bf16[896,1024]{1,0:T(8,128)(2,1)S(1)}, u32[]{:S(2)}) copy-start(bf16[896,1024]{1,0:T(8,128)(2,1)S(1)} %convolution_convert_fusion.4) | copy-start | bytes 5505028
  229.2 3.0 copy-start.30
  230.1 32.1 %collective-permute-start.12 = (bf16[224,1024]{1,0:T(8,128)(2,1)}, bf16[224,1024]{1,0:T(8,128)(2,1)}, u32[]{:S(2)}, u32[]{:S(2)}) collective-permute-start(bf16[224,1024]{1,0:T(8,128)(2,1)} %get-tuple-element.18), channel_id=1, source_target_pairs={{0,128},{1,129},{2,130},{3,131},{4,132},{5,133},{6,134},{7,135},{8... | collective-permute-start | bytes 1376264 | tf_op jit(solution)/shard_map/ppermute | solution.py:35
  236.9 84.3 %all-to-all-start.1 = ((bf16[64,8,8,128]{3,2,1,0:T(8,128)(2,1)}), bf16[64,8,8,128]{3,2,1,0:T(8,128)(2,1)S(1)}, u32[]{:S(2)}, u32[]{:S(2)}) async-start(bf16[64,8,8,128]{3,2,1,0:T(8,128)(2,1)} %maximum_maximum_fusion), calls=%async_computation.1 | async-start | bytes 2097152 | tf_op jit(solution)/shard_map/all_to_all | solution.py:107
  257.3 14.3 %collective-permute-start.14 = (bf16[224,1024]{1,0:T(8,128)(2,1)S(1)}, bf16[224,1024]{1,0:T(8,128)(2,1)S(1)}, u32[]{:S(2)}, u32[]{:S(2)}) collective-permute-start(bf16[224,1024]{1,0:T(8,128)(2,1)S(1)} %get-tuple-element.20), channel_id=1, source_target_pairs={{0,384},{1,385},{2,386},{3,387},{4,388},{5,389},{6,390},{7,391},{8... | collective-permute-start | bytes 1376264 | tf_op jit(solution)/shard_map/ppermute | solution.py:35
  264.5 24.6 %collective-permute-start.13 = (bf16[224,2048]{1,0:T(8,128)(2,1)}, bf16[224,2048]{1,0:T(8,128)(2,1)}, u32[]{:S(2)}, u32[]{:S(2)}) collective-permute-start(bf16[224,2048]{1,0:T(8,128)(2,1)} %pad_maximum_fusion.4), channel_id=1, source_target_pairs={{0,128},{1,129},{2,130},{3,131},{4,132},{5,133},{6,134},{7,135},{8... | collective-permute-start | bytes 2752520 | tf_op jit(solution)/shard_map/ppermute | solution.py:35
  272.7 24.0 %collective-permute-start.15 = (bf16[224,2048]{1,0:T(8,128)(2,1)}, bf16[224,2048]{1,0:T(8,128)(2,1)}, u32[]{:S(2)}, u32[]{:S(2)}) collective-permute-start(bf16[224,2048]{1,0:T(8,128)(2,1)} %pad_maximum_fusion.5), channel_id=1, source_target_pairs={{0,384},{1,385},{2,386},{3,387},{4,388},{5,389},{6,390},{7,391},{8... | collective-permute-start | bytes 2752520 | tf_op jit(solution)/shard_map/ppermute | solution.py:35
  296.7 9.2 %copy-start.31 = (s32[128,1]{0,1:T(1,128)S(1)}, s32[128,1]{0,1:T(1,128)}, u32[]{:S(2)}) copy-start(s32[128,1]{0,1:T(1,128)} %param.9) | copy-start | bytes 1540
  298.7 21.3 %collective-permute-start.16 = (bf16[112,2048]{1,0:T(8,128)(2,1)S(1)}, bf16[112,2048]{1,0:T(8,128)(2,1)S(1)}, u32[]{:S(2)}, u32[]{:S(2)}) collective-permute-start(bf16[112,2048]{1,0:T(8,128)(2,1)S(1)} %get-tuple-element.40), channel_id=1, source_target_pairs={{0,0},{1,1},{2,64},{3,65},{4,4},{5,5},{6,68},{7,69},{8,8},{9,9},{1... | collective-permute-start | bytes 1376264 | tf_op jit(solution)/shard_map/ppermute | solution.py:35
  304.0 16.0 %collective-permute-start.17 = (bf16[112,2048]{1,0:T(8,128)(2,1)S(1)}, bf16[112,2048]{1,0:T(8,128)(2,1)S(1)}, u32[]{:S(2)}, u32[]{:S(2)}) collective-permute-start(bf16[112,2048]{1,0:T(8,128)(2,1)S(1)} %get-tuple-element.41), channel_id=1, source_target_pairs={{0,64},{1,65},{2,0},{3,1},{4,68},{5,69},{6,4},{7,5},{8,72},{9,73},... | collective-permute-start | bytes 1376264 | tf_op jit(solution)/shard_map/ppermute | solution.py:35
  (4 other events, 5.1 us)
